TPU v7x, 32 devices: a whole 2x2x4 slice. The times are simulated.
32 devices in a mesh: clus: 8 (over z, core), lvl: 4 (over y, x).
Axes of the slice: x: 2, y: 2, z: 4, core: 2. Of those that a mesh axis runs over, the one named last changes fastest.
Arguments:
- krylov_basis: float32 [8, 4, 2048], P(None, 'lvl', 'clus'), may hold values from -90 to 90
- near_block: bfloat16 [4, 8, 4, 256, 256], P('lvl', 'clus'), may hold values from -1 to 2.5
- near_col: int32 [4, 8, 4], P('lvl', 'clus'), may hold values from 0 to 7, as said below
- near_count: int32 [4, 8], P('lvl', 'clus'), may hold values from 1 to 4, as said below
- far_col: int32 [4, 8, 6], P('lvl', 'clus'), may hold values from 0 to 7, as said below
- v_basis: bfloat16 [4, 8, 32, 256], P('lvl', 'clus'), may hold values from -0.375 to 0.375
- u_basis: bfloat16 [4, 8, 32, 256], P('lvl', 'clus'), may hold values from -1 to 1
- far_coupling: float32 [4, 8, 6, 32, 32], P('lvl', 'clus'), may hold values from -0.4375 to 0.4375
- transfer: float32 [4, 8, 32, 32], P('lvl', 'clus'), may hold values from -1 to 1
- top_coupling: float32 [4, 8, 4, 32, 32], P('lvl', 'clus'), may hold values from -0.5 to 0.5
Outputs:
- q_next: float32 [4, 4, 2048], P(None, 'lvl', 'clus')
- coeffs: float32 [2, 12, 4], replicated
Inputs may be any that keep to these rules, and one draw needn't show every extreme that they name: `near_col`: slot 0 of every leaf names the leaf itself; every other slot names leaf i - 1 or leaf i + 1 of the same subtree. Slots at or beyond the leaf's near_count name such leaves too, and their blocks are ignored. `near_count`: in some aligned run of 1 leaves every leaf has 4. `far_col`: A partner lies in the same subtree, in an aligned run of 1 leaves other than the leaf's own. Slot 0 names a leaf of the run just before the leaf's own, runs counted cyclically within the subtree.
All inputs are finite; a program needn't handle non-finite values.
Results may differ from a plain program's by a relative error of at most 0.00037.
Values may be sent and summed in bfloat16 or wider, within the bound.
No kernel may reach another device: no remote copies, remote signals or barrier semaphores. Data moves between devices by JAX's collectives and lax.ppermute only.
A program may use at most 64 MiB of HBM per device.

v0:
```python
import jax
import jax.numpy as jnp
from jax import lax
from jax.sharding import PartitionSpec as P

LEAF = 256
RANK = 32
VECS = 4
NEAR_SLOTS = 4
FAR_SLOTS = 6
STEPS = 2
LEAVES_DEV = 1
BASIS = 8


PRECISE = lax.Precision.HIGHEST


def padded_2(block, sides, width):
    for axis, dim in sides:
        count = lax.axis_size(axis)
        forward = [(i, i + 1) for i in range(count - 1)]
        backward = [(target, source) for source, target in forward]
        low = lax.ppermute(
            lax.slice_in_dim(block, block.shape[dim] - width, None, axis=dim), axis, forward
        )
        high = lax.ppermute(lax.slice_in_dim(block, 0, width, axis=dim), axis, backward)
        block = jnp.concatenate([low, block, high], axis=dim)
    return block


def row_products(left_rows, right_rows):
    return jnp.dot(left_rows, right_rows.T, precision=PRECISE)


def near_field(lowered, near_block, near_col, near_count):
    padded = padded_2(lowered, (("clus", 1),), LEAVES_DEV * LEAF)
    leaf_rows = padded.reshape(VECS, 3 * LEAVES_DEV, LEAF)
    first_leaf = (lax.axis_index("clus") - 1) * LEAVES_DEV
    partner_cols = jnp.clip(near_col[0] - first_leaf, 0, 3 * LEAVES_DEV - 1)
    live_count = near_count[0]
    blocks = near_block[0]
    picked = jnp.take(leaf_rows, partner_cols.reshape(-1), axis=1).reshape(
        VECS, LEAVES_DEV, NEAR_SLOTS, LEAF
    )
    slot_ids = lax.broadcasted_iota(jnp.int32, (LEAVES_DEV, NEAR_SLOTS), 1)
    is_live = slot_ids < live_count[:, None]
    picked = jnp.where(is_live[None, :, :, None], picked, jnp.zeros_like(picked))
    result = jnp.einsum("lkpq,vlkq->vlp", blocks, picked, preferred_element_type=jnp.float32)
    return result


def far_field(lowered, far_col, v_basis, u_basis, far_coupling, transfer, top_coupling):
    leaves = lowered.reshape(VECS, LEAVES_DEV, LEAF)
    skeleton = jnp.einsum("lrp,vlp->lvr", v_basis[0], leaves, preferred_element_type=jnp.float32)
    flat_skel = skeleton.reshape(LEAVES_DEV, VECS * RANK)
    wanted = far_col[0].reshape(-1)
    arrived = lax.all_gather(flat_skel, "clus", axis=0, tiled=True)
    arrived_rows = arrived.shape[0]
    matches = (wanted[:, None] == lax.broadcasted_iota(jnp.int32, (1, arrived_rows), 1)).astype(
        jnp.float32
    )
    partners = jnp.dot(matches, arrived, precision=PRECISE)
    partners = partners.reshape(LEAVES_DEV, FAR_SLOTS, VECS, RANK)
    coupled = jnp.einsum("lkqr,lkvr->lvq", far_coupling[0], partners, precision=PRECISE)
    coarse = jnp.einsum("lvr,lrq->vq", skeleton, transfer[0], precision=PRECISE)
    everyone = lax.all_gather(coarse.reshape(1, VECS * RANK), "lvl", axis=0, tiled=True)
    everyone = everyone.reshape(-1, VECS, RANK)
    own_tree = lax.axis_index("lvl")
    couplings = top_coupling[0, 0]
    others = lax.broadcasted_iota(jnp.int32, (couplings.shape[0], 1, 1), 0) != own_tree
    couplings = jnp.where(others, couplings, jnp.zeros_like(couplings))
    upper = jnp.einsum("tqr,tvr->vq", couplings, everyone, precision=PRECISE)
    coupled = coupled + jnp.einsum("lqr,vr->lvq", transfer[0], upper, precision=PRECISE)
    coupled_low = coupled.astype(jnp.bfloat16)
    return jnp.einsum("lvq,lqp->vlp", coupled_low, u_basis[0], preferred_element_type=jnp.float32)


def orthogonalize(window, image_block):
    rows_all = float(lax.axis_size("clus") * lax.axis_size("lvl") * image_block.shape[1])
    metric, projection, square = lax.psum(
        (
            row_products(window, window),
            row_products(window, image_block),
            row_products(image_block, image_block),
        ),
        ("clus", "lvl"),
    )
    metric = metric / rows_all
    projection = projection / rows_all
    square = square / rows_all
    remainder = image_block - jnp.dot(projection.T, window, precision=PRECISE)
    coef_cross = jnp.dot(projection.T, projection, precision=PRECISE)
    weighted = jnp.dot(
        projection.T, jnp.dot(metric, projection, precision=PRECISE), precision=PRECISE
    )
    gram = square - 2.0 * coef_cross + weighted
    lower_factor = jnp.linalg.cholesky(gram)
    inverse = lax.linalg.triangular_solve(
        lower_factor, jnp.eye(VECS, dtype=jnp.float32), left_side=True, lower=True
    )
    new_block = jnp.dot(inverse, remainder, precision=PRECISE)
    return (new_block, jnp.concatenate([projection, lower_factor.T], axis=0))


def local(
    krylov_basis,
    near_block,
    near_col,
    near_count,
    far_col,
    v_basis,
    u_basis,
    far_coupling,
    transfer,
    top_coupling,
):
    row_count = krylov_basis.shape[2]
    window = krylov_basis.reshape(BASIS, row_count)
    current = window[VECS:]
    records = []
    for step_index in range(STEPS):
        lowered = current.astype(jnp.bfloat16)
        near_part = near_field(lowered, near_block, near_col, near_count)
        far_part = far_field(
            lowered, far_col, v_basis, u_basis, far_coupling, transfer, top_coupling
        )
        image_block = (near_part + far_part).reshape(VECS, row_count)
        current, record = orthogonalize(window, image_block)
        records.append(record)
        window = jnp.concatenate([window[VECS:], current], axis=0)
    return (current.reshape(VECS, 1, row_count), jnp.stack(records))


def solution(mesh):
    return jax.shard_map(
        local,
        mesh=mesh,
        in_specs=(
            P(None, "lvl", "clus"),
            P("lvl", "clus", None, None, None),
            P("lvl", "clus", None),
            P("lvl", "clus"),
            P("lvl", "clus", None),
            P("lvl", "clus", None, None),
            P("lvl", "clus", None, None),
            P("lvl", "clus", None, None, None),
            P("lvl", "clus", None, None),
            P("lvl", "clus", None, None, None),
        ),
        out_specs=(P(None, "lvl", "clus"), P()),
        check_vma=False,
    )
```

profile of v0, /device:TPU:0, one launch (start us, length us, event | category | flops | bytes accessed | tf_op | source)
XLA Modules:
  0.0 142.5 jit_solution(8753681522929081642)
XLA Ops:
  0.7 0.7 slice.13
  1.4 1.4 collective-permute-start.1
  2.9 3.0 %collective-permute-start = (bf16[4,256]{1,0:T(4,128)(2,1)S(1)}, bf16[4,256]{1,0:T(4,128)(2,1)S(1)}, u32[]{:S(2)}, u32[]{:S(2)}) collective-permute-start(bf16[4,256]{1,0:T(4,128)(2,1)S(1)} %bitcast.166), channel_id=1, source_target_pairs={{0,4},{4,8},{8,12},{12,16},{16,20},{20,24},{24,28},{1,5},{5,9},{9,... | collective-permute-start | bytes 6152 | tf_op jit(solution)/shard_map/ppermute | solution.py:24
  5.9 0.1 fusion.29
  6.7 0.1 fusion.26
  6.9 13.5 %all-gather = f32[8,1,128]{2,1,0:T(1,128)S(1)} all-gather(f32[1,1,128]{2,1,0:T(1,128)S(1)} %reshape.212), channel_id=1, replica_groups=mesh['clus'=8,'lvl'=4] {'clus'}, dimensions={0}, use_global_device_ids=true | all-gather | bytes 4608 | tf_op jit(solution)/shard_map/all_gather | solution.py:58
  20.4 0.2 fusion.50
  20.6 0.6 copy-done.3
  21.3 0.1 fusion.22
  21.5 8.0 %all-gather.1 = f32[4,1,128]{2,1,0:T(1,128)S(1)} all-gather(f32[1,1,128]{2,1,0:T(1,128)S(1)} %reshape.214), channel_id=1, replica_groups=mesh['clus'=8,'lvl'=4] {'lvl'}, dimensions={0}, use_global_device_ids=true | all-gather | bytes 2560 | tf_op jit(solution)/shard_map/all_gather | solution.py:67
  29.5 0.5 broadcast.208
  30.0 0.7 reduce.10
  30.8 0.2 convolution_bitcast_fusion.9
  30.9 0.3 convolution_bitcast_fusion.8
  31.2 0.2 fusion.6
  31.4 0.6 gather_fusion
  32.0 0.2 convolution_bitcast_fusion.4
  32.3 0.5 copy-done.6
  32.7 0.1 fusion.1
  32.8 0.1 fusion.88
  33.0 0.1 convolution_bitcast_fusion.7
  33.1 36.9 %all-reduce.1 = (f32[4,4]{0,1:T(4,128)S(1)}, f32[8,4]{0,1:T(4,128)S(1)}, f32[8,8]{1,0:T(8,128)S(1)}) all-reduce(f32[4,4]{0,1:T(4,128)S(1)} %fusion.88, f32[8,4]{0,1:T(4,128)S(1)} %convolution_bitcast_fusion.7, f32[8,8]{1,0:T(8,128)S(1)} %fusion.29), channel_id=1, replica_groups=mesh['clus'=8,'lvl'=4] {'clus','lvl'}, use_global_device_ids=true, to_apply=%region_0.2 | all-reduce | flops 112 | bytes 896 | tf_op jit(solution)/shard_map/psum | solution.py:81
  70.0 0.1 convolution_subtract_fusion.1
  70.1 0.1 fusion.5
  70.2 0.1 fusion.47
  70.4 0.1 convolution_add_fusion.2
  70.5 0.1 copy.40
  70.6 0.4 cholesky.44
  71.0 0.6 compare_reduce_fusion.1
  71.7 0.6 fusion.74
  72.3 0.3 custom-call.6
  72.7 0.2 fusion.55
  72.9 0.1 fusion.87
  73.0 1.3 collective-permute-start.3
  74.3 3.0 %collective-permute-start.2 = (bf16[4,256]{1,0:T(4,128)(2,1)S(1)}, bf16[4,256]{1,0:T(4,128)(2,1)S(1)}, u32[]{:S(2)}, u32[]{:S(2)}) collective-permute-start(bf16[4,256]{1,0:T(4,128)(2,1)S(1)} %get-tuple-element.23), channel_id=1, source_target_pairs={{0,4},{4,8},{8,12},{12,16},{16,20},{20,24},{24,28},{1,5},{5,9},{9,... | collective-permute-start | bytes 6152 | tf_op jit(solution)/shard_map/ppermute | solution.py:24
  77.3 0.1 fusion.24
  77.5 0.1 fusion.19
  77.7 11.2 %all-gather.2 = f32[8,1,128]{2,1,0:T(1,128)S(1)} all-gather(f32[1,1,128]{2,1,0:T(1,128)S(1)} %reshape.216), channel_id=1, replica_groups=mesh['clus'=8,'lvl'=4] {'clus'}, dimensions={0}, use_global_device_ids=true | all-gather | bytes 4608 | tf_op jit(solution)/shard_map/all_gather | solution.py:58
  88.9 0.2 fusion.49
  89.2 0.2 convolution_bitcast_fusion.6
  89.4 8.8 %all-gather.3 = f32[4,1,128]{2,1,0:T(1,128)S(1)} all-gather(f32[1,1,128]{2,1,0:T(1,128)S(1)} %reshape.218), channel_id=1, replica_groups=mesh['clus'=8,'lvl'=4] {'lvl'}, dimensions={0}, use_global_device_ids=true | all-gather | bytes 2560 | tf_op jit(solution)/shard_map/all_gather | solution.py:67
  98.2 0.7 reduce.11
  98.9 0.2 convolution_bitcast_fusion.5
  99.2 0.2 fusion.7
  99.3 0.1 fusion.41
  99.5 0.6 gather_fusion.1
  100.1 0.2 convolution_bitcast_fusion.3
  100.3 0.1 fusion.3
  100.4 0.1 fusion.89
  100.6 0.1 fusion.42
  100.7 37.4 %all-reduce = (f32[4,4]{0,1:T(4,128)S(1)}, f32[8,4]{0,1:T(4,128)S(1)}, f32[8,8]{1,0:T(8,128)S(1)}) all-reduce(f32[4,4]{0,1:T(4,128)S(1)} %fusion.89, f32[8,4]{0,1:T(4,128)S(1)} %fusion.42, f32[8,8]{1,0:T(8,128)S(1)} %fusion.41), channel_id=1, replica_groups=mesh['clus'=8,'lvl'=4] {'clus','lvl'}, use_global_device_ids=true, to_apply=%region_5.9 | all-reduce | flops 112 | bytes 896 | tf_op jit(solution)/shard_map/psum | solution.py:81
  138.2 0.1 convolution_subtract_fusion
  138.3 0.1 fusion.4
  138.5 0.1 fusion.45
  138.6 0.1 convolution_add_fusion
  138.7 0.1 copy.45
  138.8 0.4 cholesky.55
  139.2 0.6 compare_reduce_fusion
  139.9 0.6 fusion.73
  140.6 0.3 custom-call.7
  140.9 0.2 fusion.53
  141.1 0.1 convolution_bitcast_fusion.2
  141.2 0.6 copy.47
  141.9 0.6 pad_maximum_fusion.6
  (43 shorter events, 1.0 us)
Async XLA Ops:
  0.6 31.4 %copy-start = (bf16[1,1,4,256,256]{4,3,2,1,0:T(8,128)(2,1)S(1)}, bf16[1,1,4,256,256]{4,3,2,1,0:T(8,128)(2,1)}, u32[]{:S(2)}) copy-start(bf16[1,1,4,256,256]{4,3,2,1,0:T(8,128)(2,1)} %param.16) | copy-start | bytes 1572868
  0.6 5.2 %copy-start.4 = (f32[8,1,256]{2,1,0:T(1,128)S(1)}, f32[8,1,256]{2,1,0:T(1,128)}, u32[]{:S(2)}) copy-start(f32[8,1,256]{2,1,0:T(1,128)} %param.15) | copy-start | bytes 24580
  0.7 5.4 %copy-start.7 = (s32[1,1,4]{2,1,0:T(1,128)S(1)}, s32[1,1,4]{2,1,0:T(1,128)}, u32[]{:S(2)}) copy-start(s32[1,1,4]{2,1,0:T(1,128)} %param.17) | copy-start | bytes 52
  0.7 6.0 %copy-start.5 = (bf16[1,1,32,256]{3,2,1,0:T(8,128)(2,1)S(1)}, bf16[1,1,32,256]{3,2,1,0:T(8,128)(2,1)}, u32[]{:S(2)}) copy-start(bf16[1,1,32,256]{3,2,1,0:T(8,128)(2,1)} %param.20) | copy-start | bytes 49156
  0.7 19.7 %copy-start.8 = (s32[1,1,6]{2,1,0:T(1,128)S(1)}, s32[1,1,6]{2,1,0:T(1,128)}, u32[]{:S(2)}) copy-start(s32[1,1,6]{2,1,0:T(1,128)} %param.19) | copy-start | bytes 76
  1.4 29.3 %copy-start.1 = (f32[1,1,6,32,32]{4,3,2,1,0:T(8,128)S(1)}, f32[1,1,6,32,32]{4,3,2,1,0:T(8,128)}, u32[]{:S(2)}) copy-start(f32[1,1,6,32,32]{4,3,2,1,0:T(8,128)} %param.22) | copy-start | bytes 73732
  1.4 29.9 %collective-permute-start.1 = (bf16[4,256]{1,0:T(4,128)(2,1)S(1)}, bf16[4,256]{1,0:T(4,128)(2,1)S(1)}, u32[]{:S(2)}, u32[]{:S(2)}) collective-permute-start(bf16[4,256]{1,0:T(4,128)(2,1)S(1)} %bitcast.165), channel_id=1, source_target_pairs={{4,0},{8,4},{12,8},{16,12},{20,16},{24,20},{28,24},{5,1},{9,5},{13... | collective-permute-start | bytes 6152 | tf_op jit(solution)/shard_map/ppermute | solution.py:27
  2.9 28.5 %collective-permute-start = (bf16[4,256]{1,0:T(4,128)(2,1)S(1)}, bf16[4,256]{1,0:T(4,128)(2,1)S(1)}, u32[]{:S(2)}, u32[]{:S(2)}) collective-permute-start(bf16[4,256]{1,0:T(4,128)(2,1)S(1)} %bitcast.166), channel_id=1, source_target_pairs={{0,4},{4,8},{8,12},{12,16},{16,20},{20,24},{24,28},{1,5},{5,9},{9,... | collective-permute-start | bytes 6152 | tf_op jit(solution)/shard_map/ppermute | solution.py:24
  20.6 0.7 copy-start.3
  30.0 1.0 copy-start.2
  32.0 0.7 copy-start.6
  73.0 26.5 %collective-permute-start.3 = (bf16[4,256]{1,0:T(4,128)(2,1)S(1)}, bf16[4,256]{1,0:T(4,128)(2,1)S(1)}, u32[]{:S(2)}, u32[]{:S(2)}) collective-permute-start(bf16[4,256]{1,0:T(4,128)(2,1)S(1)} %get-tuple-element.23), channel_id=1, source_target_pairs={{4,0},{8,4},{12,8},{16,12},{20,16},{24,20},{28,24},{5,1},{9,5},{13... | collective-permute-start | bytes 6152 | tf_op jit(solution)/shard_map/ppermute | solution.py:27
  74.3 25.2 %collective-permute-start.2 = (bf16[4,256]{1,0:T(4,128)(2,1)S(1)}, bf16[4,256]{1,0:T(4,128)(2,1)S(1)}, u32[]{:S(2)}, u32[]{:S(2)}) collective-permute-start(bf16[4,256]{1,0:T(4,128)(2,1)S(1)} %get-tuple-element.23), channel_id=1, source_target_pairs={{0,4},{4,8},{8,12},{12,16},{16,20},{20,24},{24,28},{1,5},{5,9},{9,... | collective-permute-start | bytes 6152 | tf_op jit(solution)/shard_map/ppermute | solution.py:24
where the time goes:
time: 143 us
  blocking collectives  116 us (81%)
  starting transfers between devices  8.77 us (6%)
  other arithmetic  6.2 us (4%)
  matrix products  5.25 us (4%)
  local copies, waits for them, and re-layouts  5.02 us (4%)
  between operations  1.52 us (1%)
    psum x2, blocking collectives, orthogonalize(): lax.psum((row_products(window, window), row_products(window, image_block)...  74.3 us
    all_gather x2, blocking collectives, far_field(): arrived = lax.all_gather(flat_skel, 'clus', axis=0, tiled=True)  24.7 us
    all_gather x2, blocking collectives, far_field(): lax.all_gather(coarse.reshape(1, VECS * RANK), 'lvl', axis=0, tiled=True)  16.7 us
    ppermute x2, starting transfers between devices, padded_2(): lax.ppermute(lax.slice_in_dim(block, block.shape[dim] - width, None, axis...  6.06 us
  transfers between devices with their start and end apart: 4, of which 0 were waited for; matrix products, arithmetic and copies ran while one was open for 3% of the time, Pallas kernels for 0%

commit v1 on v0

v1 whole, which is shorter than its diff:
```python
import jax
import jax.numpy as jnp
from jax import lax
from jax.sharding import PartitionSpec as P

LEAF = 256
RANK = 32
VECS = 4
NEAR_SLOTS = 4
FAR_SLOTS = 6
STEPS = 2
LEAVES_DEV = 1
BASIS = 8


PRECISE = lax.Precision.HIGHEST


AXES = ("clus", "lvl")


def row_products(left_rows, right_rows):
    return jnp.dot(left_rows, right_rows.T, precision=PRECISE)


def exchange(slots):
    return lax.all_to_all(slots, AXES, 0, 0, tiled=True)


def three_parts(values):
    high = lax.reduce_precision(values, 8, 7)
    rest = values - high
    middle = lax.reduce_precision(rest, 8, 7)
    low = rest - middle
    return jnp.concatenate([high, middle, low]).astype(jnp.bfloat16)


def joined_parts(parts):
    wide = parts.astype(jnp.float32)
    count = wide.shape[-1] // 3
    return wide[..., :count] + wide[..., count : 2 * count] + wide[..., 2 * count :]


def operator(
    lowered, near_block, near_col, near_count, far_col, v_basis, u_basis, far_coupling, transfer, top_coupling
):
    trees, leaves = lax.axis_size("lvl"), lax.axis_size("clus")
    own_tree, own_leaf = lax.axis_index("lvl"), lax.axis_index("clus")
    skeleton = jnp.einsum("rp,vp->vr", v_basis[0, 0], lowered, preferred_element_type=jnp.float32)
    coarse = jnp.dot(skeleton, transfer[0, 0], precision=PRECISE)
    flat = lowered.reshape(-1)
    same_tree = jnp.concatenate([flat, three_parts(skeleton.reshape(-1))])
    other_tree = jnp.concatenate([flat, three_parts(coarse.reshape(-1))])
    peers = lax.broadcasted_iota(jnp.int32, (leaves * trees, 1, 1), 0)
    slots = jnp.where(peers % trees == own_tree, same_tree[None, None], other_tree[None, None])
    arrived = exchange(slots).reshape(leaves, trees, -1)
    in_tree = lax.dynamic_index_in_dim(arrived, own_tree, 1, keepdims=False)
    across = lax.dynamic_index_in_dim(arrived, own_leaf, 0, keepdims=False)
    size = flat.shape[0]
    skeletons = joined_parts(in_tree[:, size:])
    coarses = joined_parts(across[:, size:]).reshape(trees, VECS, RANK)
    wanted = far_col[0, 0]
    matches = (wanted[:, None] == lax.broadcasted_iota(jnp.int32, (1, leaves), 1)).astype(jnp.float32)
    partners = jnp.dot(matches, skeletons, precision=PRECISE).reshape(FAR_SLOTS, VECS, RANK)
    coupled = jnp.einsum("kqr,kvr->vq", far_coupling[0, 0], partners, precision=PRECISE)
    couplings = top_coupling[0, 0]
    others = lax.broadcasted_iota(jnp.int32, (trees, 1, 1), 0) != own_tree
    couplings = jnp.where(others, couplings, jnp.zeros_like(couplings))
    upper = jnp.einsum("tqr,tvr->vq", couplings, coarses, precision=PRECISE)
    coupled = coupled + jnp.einsum("qr,vr->vq", transfer[0, 0], upper, precision=PRECISE)
    coupled_low = coupled.astype(jnp.bfloat16)
    far_part = jnp.einsum("vq,qp->vp", coupled_low, u_basis[0, 0], preferred_element_type=jnp.float32)
    blocks = in_tree[:, :size].reshape(leaves, VECS, LEAF)
    picked = jnp.take(blocks, near_col[0, 0], axis=0)
    is_live = lax.broadcasted_iota(jnp.int32, (NEAR_SLOTS, 1, 1), 0) < near_count[0, 0]
    picked = jnp.where(is_live, picked, jnp.zeros_like(picked))
    near_part = jnp.einsum("kpq,kvq->vp", near_block[0, 0], picked, preferred_element_type=jnp.float32)
    return near_part + far_part


def orthogonalize(window, image_block):
    devices = lax.axis_size("clus") * lax.axis_size("lvl")
    rows_all = float(devices * image_block.shape[1])
    pieces = (
        row_products(window, window),
        row_products(window, image_block),
        row_products(image_block, image_block),
    )
    flat = jnp.concatenate([piece.reshape(-1) for piece in pieces])
    flat = jnp.pad(flat, (0, -flat.shape[0] % 128))
    total = exchange(jnp.broadcast_to(flat, (devices, 1, flat.shape[0]))).sum((0, 1)) / rows_all
    metric = total[: BASIS * BASIS].reshape(BASIS, BASIS)
    at = BASIS * BASIS
    projection = total[at : at + BASIS * VECS].reshape(BASIS, VECS)
    at = at + BASIS * VECS
    square = total[at : at + VECS * VECS].reshape(VECS, VECS)
    remainder = image_block - jnp.dot(projection.T, window, precision=PRECISE)
    coef_cross = jnp.dot(projection.T, projection, precision=PRECISE)
    weighted = jnp.dot(
        projection.T, jnp.dot(metric, projection, precision=PRECISE), precision=PRECISE
    )
    gram = square - 2.0 * coef_cross + weighted
    lower_factor = jnp.linalg.cholesky(gram)
    inverse = lax.linalg.triangular_solve(
        lower_factor, jnp.eye(VECS, dtype=jnp.float32), left_side=True, lower=True
    )
    new_block = jnp.dot(inverse, remainder, precision=PRECISE)
    return (new_block, jnp.concatenate([projection, lower_factor.T], axis=0))


def local(
    krylov_basis,
    near_block,
    near_col,
    near_count,
    far_col,
    v_basis,
    u_basis,
    far_coupling,
    transfer,
    top_coupling,
):
    row_count = krylov_basis.shape[2]
    window = krylov_basis.reshape(BASIS, row_count)
    current = window[VECS:]
    records = []
    for step_index in range(STEPS):
        lowered = current.astype(jnp.bfloat16)
        image_block = operator(
            lowered, near_block, near_col, near_count, far_col, v_basis, u_basis, far_coupling, transfer, top_coupling
        )
        current, record = orthogonalize(window, image_block)
        records.append(record)
        window = jnp.concatenate([window[VECS:], current], axis=0)
    return (current.reshape(VECS, 1, row_count), jnp.stack(records))


def solution(mesh):
    return jax.shard_map(
        local,
        mesh=mesh,
        in_specs=(
            P(None, "lvl", "clus"),
            P("lvl", "clus", None, None, None),
            P("lvl", "clus", None),
            P("lvl", "clus"),
            P("lvl", "clus", None),
            P("lvl", "clus", None, None),
            P("lvl", "clus", None, None),
            P("lvl", "clus", None, None, None),
            P("lvl", "clus", None, None),
            P("lvl", "clus", None, None, None),
        ),
        out_specs=(P(None, "lvl", "clus"), P()),
        check_vma=False,
    )
```

time: 143 us -> 69.8 us (0.49)
  blocking collectives: 116 us -> 8.9 us
  waiting for transfers between devices: 0.02 us -> 21.7 us
  local copies, waits for them, and re-layouts: 5.02 us -> 9.93 us
  starting transfers between devices: 8.77 us -> 12.5 us
  other arithmetic: 6.2 us -> 8.91 us
    psum x2 -> x0, blocking collectives: 74.3 us -> none  [orthogonalize(): lax.psum((row_products(window, window), row_products(window, image_block)...]
    all_gather x4 -> x0, blocking collectives: 41.4 us -> none  [the longest x2 24.7 us: far_field(): arrived = lax.all_gather(flat_skel, 'clus', axis=0, tiled=True)]
    all_to_all x0 -> x3, waiting for transfers between devices: none -> 21.7 us  [exchange(): return lax.all_to_all(slots, AXES, 0, 0, tiled=True)]
    all_to_all x0 -> x3, starting transfers between devices: none -> 12.5 us  [exchange(): return lax.all_to_all(slots, AXES, 0, 0, tiled=True)]
    all_to_all x0 -> x1, blocking collectives: none -> 8.9 us  [exchange(): return lax.all_to_all(slots, AXES, 0, 0, tiled=True)]
    ppermute x4 -> x0, starting transfers between devices: 8.77 us -> none  [the longest x2 6.06 us: padded_2(): lax.ppermute(lax.slice_in_dim(block, block.shape[dim] - width, None, axis...]
    select_n x0 -> x5, other arithmetic: none -> 2.72 us  [the longest x4 2.71 us: operator(): jnp.where(peers % trees == own_tree, same_tree[None, None], other_tree[No...]
    unnamed x25 -> x29, local copies, waits for them, and re-layouts: 2.1 us -> 4.08 us
  transfers between devices with their start and end apart: 4 -> 3, of which waited for: 0 -> 3; matrix products, arithmetic and copies ran while one was open for 3% -> 1% of each run, Pallas kernels for 0% -> 0%
where the time goes in v1:
time: 69.8 us; the launch traced here: 69.3 us
  waiting for transfers between devices  21.7 us (31%)
  starting transfers between devices  12.5 us (18%)
  local copies, waits for them, and re-layouts  9.93 us (14%)
  other arithmetic  8.91 us (13%)
  blocking collectives  8.9 us (13%)
  matrix products  5.64 us (8%)
  between operations  1.73 us (2%)
    all_to_all x3, waiting for transfers between devices, exchange(): return lax.all_to_all(slots, AXES, 0, 0, tiled=True)  21.7 us
    all_to_all x3, starting transfers between devices, exchange(): return lax.all_to_all(slots, AXES, 0, 0, tiled=True)  12.5 us
    all_to_all x1, blocking collectives, exchange(): return lax.all_to_all(slots, AXES, 0, 0, tiled=True)  8.9 us
    unnamed x29, local copies, waits for them, and re-layouts  4.08 us
    select_n x4, other arithmetic, operator(): jnp.where(peers % trees == own_tree, same_tree[None, None], other_tree[No...  2.71 us
    another operation x6, other arithmetic, orthogonalize(): lower_factor = jnp.linalg.cholesky(gram)  2.1 us
  transfers between devices with their start and end apart: 3, of which 3 were waited for; matrix products, arithmetic and copies ran while one was open for 1% of the time, Pallas kernels for 0%

profile of v1, /device:TPU:0, one launch (start us, length us, event | category | flops | bytes accessed | tf_op | source)
XLA Modules:
  0.0 69.3 jit_solution(15651112338690806398)
XLA Ops:
  0.7 0.7 %slice.109 = f32[4,1,256]{2,1,0:T(1,128)S(1)} slice(f32[8,1,256]{2,1,0:T(1,128)} %param.15), slice={[4:8], [0:1], [0:256]} | slice | bytes 8192 | tf_op jit(solution)/shard_map/slice | solution.py:134
  1.6 0.5 copy-done.3
  2.1 0.1 fusion.18
  2.4 0.2 broadcast_select_fusion.1
  2.6 0.5 broadcast.294
  3.1 1.2 %reduce.6 = bf16[32,1408]{1,0:T(8,128)(2,1)S(1)} reduce(bf16[32,1,1408]{2,1,0:T(2,128)(2,1)S(1)} %broadcast_select_fusion.1, bf16[]{:T(256)} %broadcast.294), dimensions={1}, to_apply=%broadcast_select_fusion.1.reduce_sub_computation | reduce | bytes 180226 | tf_op jit(solution)/shard_map/jit(_where)/select_n | solution.py:55
  4.3 0.8 %reshape.333 = bf16[32,2,704]{2,1,0:T(2,128)(2,1)} reshape(bf16[32,1408]{1,0:T(8,128)(2,1)S(1)} %reduce.6) | data formatting | bytes 180224
  5.1 7.3 %all-to-all-start = ((bf16[32,2,704]{2,1,0:T(2,128)(2,1)}), bf16[32,2,704]{2,1,0:T(2,128)(2,1)S(1)}, u32[]{:S(2)}, u32[]{:S(2)}) async-start(bf16[32,2,704]{2,1,0:T(2,128)(2,1)} %reshape.333), calls=%async_computation | async-start | bytes 196608 | tf_op jit(solution)/shard_map/all_to_all | solution.py:27
  13.3 7.0 %all-to-all-done = bf16[32,2,704]{2,1,0:T(2,128)(2,1)S(1)} async-done(((bf16[32,2,704]{2,1,0:T(2,128)(2,1)}), bf16[32,2,704]{2,1,0:T(2,128)(2,1)S(1)}, u32[]{:S(2)}, u32[]{:S(2)}) %all-to-all-start) | async-done | bytes 90144 | tf_op jit(solution)/shard_map/all_to_all | solution.py:27
  20.3 0.1 reshape.334
  20.5 0.5 reduce.4
  21.3 0.5 copy-done.8
  21.7 0.2 fusion.47
  22.0 0.6 gather_fusion
  22.6 0.2 convolution_bitcast_fusion.7
  22.9 0.2 convolution_bitcast_fusion.6
  23.1 0.2 fusion.2
  23.3 0.2 convolution_bitcast_fusion.2
  23.5 0.5 copy-done.6
  24.2 0.1 convolution_bitcast_fusion.5
  24.7 8.9 %all_to_all.20 = f32[32,1,128]{2,1,0:T(1,128)S(1)} all-to-all(f32[32,1,128]{2,1,0:T(1,128)S(1)} %broadcast_in_dim.83), channel_id=1, replica_groups=mesh['clus'=8,'lvl'=4] {'clus','lvl'}, dimensions={0} | all-to-all | bytes 32768 | tf_op jit(solution)/shard_map/all_to_all | solution.py:27
  34.0 0.2 convolution_subtract_fusion.1
  34.2 0.2 fusion.1
  34.5 0.2 fusion.94
  34.7 0.1 convolution_add_fusion.4
  35.0 0.4 cholesky.44
  35.4 0.6 compare_reduce_fusion.1
  36.0 0.6 fusion.71
  36.7 0.3 custom-call.6
  37.0 0.2 fusion.55
  37.2 0.1 fusion.95
  37.6 0.1 fusion.15
  37.8 0.2 broadcast_select_fusion
  38.1 1.2 %reduce.7 = bf16[32,1408]{1,0:T(8,128)(2,1)S(1)} reduce(bf16[32,1,1408]{2,1,0:T(2,128)(2,1)S(1)} %broadcast_select_fusion, bf16[]{:T(256)} %broadcast.294), dimensions={1}, to_apply=%broadcast_select_fusion.reduce_sub_computation | reduce | bytes 180226 | tf_op jit(solution)/shard_map/jit(_where)/select_n | solution.py:55
  39.2 0.8 %reshape.335 = bf16[32,2,704]{2,1,0:T(2,128)(2,1)} reshape(bf16[32,1408]{1,0:T(8,128)(2,1)S(1)} %reduce.7) | data formatting | bytes 180224
  40.0 2.6 %all-to-all-start.2 = ((bf16[32,2,704]{2,1,0:T(2,128)(2,1)}), bf16[32,2,704]{2,1,0:T(2,128)(2,1)S(1)}, u32[]{:S(2)}, u32[]{:S(2)}) async-start(bf16[32,2,704]{2,1,0:T(2,128)(2,1)} %reshape.335), calls=%async_computation.2 | async-start | bytes 196608 | tf_op jit(solution)/shard_map/all_to_all | solution.py:27
  42.7 0.1 fusion.36
  42.9 7.6 %all-to-all-done.2 = bf16[32,2,704]{2,1,0:T(2,128)(2,1)S(1)} async-done(((bf16[32,2,704]{2,1,0:T(2,128)(2,1)}), bf16[32,2,704]{2,1,0:T(2,128)(2,1)S(1)}, u32[]{:S(2)}, u32[]{:S(2)}) %all-to-all-start.2) | async-done | bytes 90144 | tf_op jit(solution)/shard_map/all_to_all | solution.py:27
  50.5 0.1 reshape.336
  50.6 0.5 reduce.5
  51.4 0.2 convolution_bitcast_fusion.3
  51.6 0.2 fusion.45
  51.9 0.6 gather_fusion.1
  52.4 0.2 convolution_bitcast_fusion.1
  52.8 0.2 convolution_bitcast_fusion.4
  52.9 0.2 fusion.3
  53.1 0.1 convolution_add_fusion
  53.3 0.1 fusion.96
  53.4 0.1 fusion.35
  53.8 0.6 broadcast_in_dim.86
  54.4 2.6 %all-to-all-start.3 = ((f32[32,1,128]{2,1,0:T(1,128)}), f32[32,1,128]{2,1,0:T(1,128)S(1)}, u32[]{:S(2)}, u32[]{:S(2)}) async-start(f32[32,1,128]{2,1,0:T(1,128)} %broadcast_in_dim.86), calls=%async_computation.3 | async-start | bytes 32768 | tf_op jit(solution)/shard_map/all_to_all | solution.py:27
  57.0 7.1 %all-to-all-done.3 = f32[32,1,128]{2,1,0:T(1,128)S(1)} async-done(((f32[32,1,128]{2,1,0:T(1,128)}), f32[32,1,128]{2,1,0:T(1,128)S(1)}, u32[]{:S(2)}, u32[]{:S(2)}) %all-to-all-start.3) | async-done | bytes 16416 | tf_op jit(solution)/shard_map/all_to_all | solution.py:27
  64.4 0.2 convolution_subtract_fusion
  64.9 0.2 fusion
  65.2 0.2 fusion.97
  65.4 0.1 convolution_add_fusion.2
  65.6 0.4 cholesky.55
  66.0 0.6 compare_reduce_fusion
  66.7 0.6 fusion.70
  67.3 0.3 custom-call.7
  67.7 0.2 fusion.53
  67.9 0.1 convolution_bitcast_fusion
  68.0 0.6 copy.97
  68.7 0.6 pad_maximum_fusion.8
  (97 shorter events, 4.2 us)
Async XLA Ops:
  0.6 22.6 %copy-start = (bf16[1,1,4,256,256]{4,3,2,1,0:T(8,128)(2,1)S(1)}, bf16[1,1,4,256,256]{4,3,2,1,0:T(8,128)(2,1)}, u32[]{:S(2)}) copy-start(bf16[1,1,4,256,256]{4,3,2,1,0:T(8,128)(2,1)} %param.16) | copy-start | bytes 1572868
  0.6 0.8 %copy-start.5 = (bf16[1,1,32,256]{3,2,1,0:T(8,128)(2,1)S(1)}, bf16[1,1,32,256]{3,2,1,0:T(8,128)(2,1)}, u32[]{:S(2)}) copy-start(bf16[1,1,32,256]{3,2,1,0:T(8,128)(2,1)} %param.20) | copy-start | bytes 49156
  1.4 0.7 %copy-start.3 = (f32[1,1,32,32]{3,2,1,0:T(8,128)S(1)}, f32[1,1,32,32]{3,2,1,0:T(8,128)}, u32[]{:S(2)}) copy-start(f32[1,1,32,32]{3,2,1,0:T(8,128)} %param.23) | copy-start | bytes 12292
  5.0 7.3 %copy-start.4 = (f32[8,1,256]{2,1,0:T(1,128)S(1)}, f32[8,1,256]{2,1,0:T(1,128)}, u32[]{:S(2)}) copy-start(f32[8,1,256]{2,1,0:T(1,128)} %param.15) | copy-start | bytes 24580
  5.1 15.3 %all-to-all-start = ((bf16[32,2,704]{2,1,0:T(2,128)(2,1)}), bf16[32,2,704]{2,1,0:T(2,128)(2,1)S(1)}, u32[]{:S(2)}, u32[]{:S(2)}) async-start(bf16[32,2,704]{2,1,0:T(2,128)(2,1)} %reshape.333), calls=%async_computation | async-start | bytes 196608 | tf_op jit(solution)/shard_map/all_to_all | solution.py:27
  12.5 0.7 copy-start.7
  21.1 0.7 copy-start.8
  21.1 1.5 %copy-start.1 = (f32[1,1,6,32,32]{4,3,2,1,0:T(8,128)S(1)}, f32[1,1,6,32,32]{4,3,2,1,0:T(8,128)}, u32[]{:S(2)}) copy-start(f32[1,1,6,32,32]{4,3,2,1,0:T(8,128)} %param.22) | copy-start | bytes 73732
  22.0 0.8 %copy-start.2 = (f32[1,1,4,32,32]{4,3,2,1,0:T(8,128)S(1)}, f32[1,1,4,32,32]{4,3,2,1,0:T(8,128)}, u32[]{:S(2)}) copy-start(f32[1,1,4,32,32]{4,3,2,1,0:T(8,128)} %param.24) | copy-start | bytes 49156
  23.2 0.7 %copy-start.6 = (bf16[1,1,32,256]{3,2,1,0:T(8,128)(2,1)S(1)}, bf16[1,1,32,256]{3,2,1,0:T(8,128)(2,1)}, u32[]{:S(2)}) copy-start(bf16[1,1,32,256]{3,2,1,0:T(8,128)(2,1)} %param.21) | copy-start | bytes 49156
  40.0 10.5 %all-to-all-start.2 = ((bf16[32,2,704]{2,1,0:T(2,128)(2,1)}), bf16[32,2,704]{2,1,0:T(2,128)(2,1)S(1)}, u32[]{:S(2)}, u32[]{:S(2)}) async-start(bf16[32,2,704]{2,1,0:T(2,128)(2,1)} %reshape.335), calls=%async_computation.2 | async-start | bytes 196608 | tf_op jit(solution)/shard_map/all_to_all | solution.py:27
  54.4 9.8 %all-to-all-start.3 = ((f32[32,1,128]{2,1,0:T(1,128)}), f32[32,1,128]{2,1,0:T(1,128)S(1)}, u32[]{:S(2)}, u32[]{:S(2)}) async-start(f32[32,1,128]{2,1,0:T(1,128)} %broadcast_in_dim.86), calls=%async_computation.3 | async-start | bytes 32768 | tf_op jit(solution)/shard_map/all_to_all | solution.py:27

commit v2 on v0

v2 whole, which is shorter than its diff:
```python
import functools

import jax
import jax.numpy as jnp
from jax import lax
from jax.experimental import pallas as pl
from jax.experimental.pallas import tpu as pltpu
from jax.sharding import PartitionSpec as P

VECS = 4
STEPS = 2
LANES = 128
AXES = ("clus", "lvl")

PRECISE = lax.Precision.HIGHEST
ROWS_DIMS = (((1,), (1,)), ((), ()))


def rows_dot(left, right, precision=None):
    return lax.dot_general(
        left, right, ROWS_DIMS, precision=precision, preferred_element_type=jnp.float32
    )


def three_parts(values):
    high = values.astype(jnp.bfloat16)
    rest = values - high.astype(jnp.float32)
    middle = rest.astype(jnp.bfloat16)
    low = (rest - middle.astype(jnp.float32)).astype(jnp.bfloat16)
    return high, middle, low


def tail_of(values):
    high, middle, low = three_parts(values)
    empty = jnp.zeros((VECS, LANES - 3 * values.shape[1]), jnp.float32)
    wide = [part.astype(jnp.float32) for part in (high, middle, low)]
    return jnp.concatenate(wide + [empty], axis=1).astype(jnp.bfloat16)


def over_slots(count, store):
    step = min(count, 32)
    if count == step:
        for slot in range(count):
            store(slot)
        return

    def body(at, carry):
        for inner in range(step):
            store(at * step + inner)
        return carry

    lax.fori_loop(0, count // step, body, 0)


def fill_operator_slots(slots_ref, lowered, v_basis, transfer, trees):
    size = lowered.shape[1]
    skeleton = rows_dot(lowered, v_basis)
    coarse = jnp.dot(skeleton, transfer, precision=PRECISE, preferred_element_type=jnp.float32)
    own_tree = lax.axis_index("lvl")
    tree_tail = tail_of(skeleton)
    level_tail = tail_of(coarse)

    def store(slot):
        slots_ref[slot, :, :size] = lowered
        slots_ref[slot, :, size:] = level_tail

    over_slots(slots_ref.shape[0], store)

    def store_tree(leaf):
        slots_ref[leaf * trees + own_tree, :, size:] = tree_tail

    over_slots(slots_ref.shape[0] // trees, store_tree)


def split_rows(flat_ref, rows):
    halves = flat_ref.shape[0] // rows
    return jnp.concatenate(
        [flat_ref[pl.ds(half, rows, stride=halves), :] for half in range(halves)], axis=1
    )


def store_rows(flat_ref, values):
    rows = values.shape[0]
    halves = flat_ref.shape[0] // rows
    for half in range(halves):
        flat_ref[pl.ds(half, rows, stride=halves), :] = values[:, half * LANES : (half + 1) * LANES]


def begin_kernel(trees, basis_ref, v_ref, transfer_ref, slots_ref, window_ref):
    basis = basis_ref.shape[0] * LANES // v_ref.shape[1]
    window = split_rows(basis_ref, basis)
    window_ref[...] = window
    lowered = window[basis - VECS :].astype(jnp.bfloat16)
    fill_operator_slots(slots_ref, lowered, v_ref[...], transfer_ref[...], trees)


def pack_couplings(weights_ref, far_coupling_ref, transfer_ref, top_ref):
    own_tree = lax.axis_index("lvl")
    far_slots = far_coupling_ref.shape[0]
    trees, rank = top_ref.shape[0], top_ref.shape[1]
    transfer = transfer_ref[...]
    for slot in range(far_slots + trees):
        if slot < far_slots:
            block = far_coupling_ref[slot]
        else:
            tree = slot - far_slots
            block = jnp.where(tree != own_tree, top_ref[tree], 0.0)
            block = jnp.dot(
                transfer, block, precision=PRECISE, preferred_element_type=jnp.float32
            )
        wide = jnp.concatenate(
            [block] * 3 + [jnp.zeros((rank, LANES - 3 * rank), jnp.float32)], axis=1
        )
        for part, piece in enumerate(three_parts(wide)):
            weights_ref[part, :, slot * LANES : (slot + 1) * LANES] = piece


def apply_kernel(
    trees,
    first,
    near_col_ref,
    near_count_ref,
    far_col_ref,
    arrived_ref,
    window_ref,
    near_ref,
    u_ref,
    *refs,
):
    if first:
        far_coupling_ref, transfer_ref, top_ref, image_ref, slots_ref, weights_ref = refs
        pack_couplings(weights_ref, far_coupling_ref, transfer_ref, top_ref)
    else:
        weights_ref, image_ref, slots_ref = refs
    own_tree = lax.axis_index("lvl")
    own_leaf = lax.axis_index("clus")
    size = near_ref.shape[1]
    far_slots = far_col_ref.shape[2]
    tails = []
    for slot in range(far_slots):
        tails.append(arrived_ref[far_col_ref[0, 0, slot] * trees + own_tree, :, size:])
    for tree in range(trees):
        tails.append(arrived_ref[own_leaf * trees + tree, :, size:])
    tails = jnp.concatenate(tails, axis=1)
    coupled = sum(rows_dot(tails, weights_ref[part]) for part in range(3))
    image = jnp.dot(
        coupled.astype(jnp.bfloat16), u_ref[...], preferred_element_type=jnp.float32
    )
    count = near_count_ref[0, 0]
    for slot in range(near_ref.shape[0]):
        source = arrived_ref[near_col_ref[0, 0, slot] * trees + own_tree, :, :size]
        source = jnp.where(slot < count, source, jnp.zeros_like(source))
        image = image + rows_dot(source, near_ref[slot])
    image_ref[...] = image
    window = window_ref[...]
    basis = window.shape[0]
    stacked = jnp.concatenate([window, image], axis=0)
    products = rows_dot(stacked, stacked, PRECISE)
    pieces = [products[basis:]]
    for at in range(0, basis, VECS):
        pieces.append(products[at : at + VECS, :basis])
    used = sum(piece.shape[1] for piece in pieces)
    pieces.append(jnp.zeros((VECS, LANES - used), jnp.float32))
    packed = jnp.concatenate(pieces, axis=1)

    def store(slot):
        slots_ref[slot] = packed

    over_slots(slots_ref.shape[0], store)


def orthogonalized(arrived_ref, window, image, rows_all):
    basis = window.shape[0]
    total = arrived_ref[0:8]
    for at in range(8, arrived_ref.shape[0], 8):
        total = total + arrived_ref[at : at + 8]
    total = (total[:VECS] + total[VECS:]) * (1.0 / rows_all)
    projection = total[:, :basis]
    square = total[:, basis : basis + VECS]
    inner = jnp.zeros((VECS, basis), jnp.float32)
    remainder = image
    at = basis + VECS
    lane = lax.broadcasted_iota(jnp.int32, (1, basis), 1)
    for b in range(basis):
        column = projection[:, b : b + 1]
        group = at + basis * (b // VECS)
        metric_row = total[b % VECS : b % VECS + 1, group : group + basis]
        metric_row = metric_row - jnp.where(lane == b, 2.0, 0.0)
        inner = inner + column * metric_row
        remainder = remainder - column * window[b : b + 1]
    columns = []
    for u in range(VECS):
        cross = jnp.sum(inner * projection[u : u + 1], axis=1, keepdims=True)
        columns.append(square[:, u : u + 1] + cross)
    row = lax.broadcasted_iota(jnp.int32, (VECS, 1), 0)
    factor = []
    for j in range(VECS):
        pivot = columns[j][j : j + 1]
        root = jnp.sqrt(pivot)
        scale = 1.0 / root
        lower = jnp.where(row > j, columns[j] * scale, 0.0)
        factor.append(jnp.where(row == j, root, lower))
        for u in range(j + 1, VECS):
            columns[u] = columns[u] - lower * lower[u : u + 1]
        solved = remainder[j : j + 1] * scale
        remainder = jnp.where(row == j, solved, remainder - lower * solved)
    record = jnp.concatenate([projection] + factor, axis=1)
    return remainder, record


def middle_kernel(
    trees,
    rows_all,
    arrived_ref,
    window_ref,
    image_ref,
    v_ref,
    transfer_ref,
    slots_ref,
    next_window_ref,
    record_ref,
):
    window = window_ref[...]
    new_block, record = orthogonalized(arrived_ref, window, image_ref[...], rows_all)
    record_ref[...] = record
    next_window_ref[:-VECS] = window[VECS:]
    next_window_ref[-VECS:] = new_block
    lowered = new_block.astype(jnp.bfloat16)
    fill_operator_slots(slots_ref, lowered, v_ref[...], transfer_ref[...], trees)


def end_kernel(rows_all, arrived_ref, window_ref, image_ref, first_ref, block_ref, records_ref):
    new_block, record = orthogonalized(arrived_ref, window_ref[...], image_ref[...], rows_all)
    store_rows(block_ref, new_block)
    records_ref[0] = first_ref[...]
    records_ref[1] = record


def call(kernel, name, outs, ins, scalars=0):
    specs = [pl.BlockSpec(memory_space=pltpu.SMEM)] * scalars
    specs += [pl.BlockSpec(memory_space=pltpu.VMEM)] * (len(ins) - scalars)
    return pl.pallas_call(
        kernel,
        name=name,
        out_shape=[jax.ShapeDtypeStruct(shape, dtype) for shape, dtype in outs],
        in_specs=specs,
        out_specs=[pl.BlockSpec(memory_space=pltpu.VMEM)] * len(outs),
        compiler_params=pltpu.CompilerParams(vmem_limit_bytes=16 << 20),
    )(*ins)


def exchange(slots):
    return lax.all_to_all(slots, AXES, 0, 0, tiled=True)


def local(
    krylov_basis,
    near_block,
    near_col,
    near_count,
    far_col,
    v_basis,
    u_basis,
    far_coupling,
    transfer,
    top_coupling,
):
    basis, _, size = krylov_basis.shape
    trees = lax.axis_size("lvl")
    devices = lax.axis_size("clus") * trees
    rows_all = float(devices * size)
    v_own, u_own, transfer_own = v_basis[0, 0], u_basis[0, 0], transfer[0, 0]
    rank = v_own.shape[0]
    far_own, top_own, near_own = far_coupling[0, 0], top_coupling[0, 0], near_block[0, 0]
    f32, bf16 = jnp.float32, jnp.bfloat16
    operator_slots = ((devices, VECS, size + LANES), bf16)
    product_slots = ((devices, VECS, LANES), f32)
    image_like = ((VECS, size), f32)
    window_like = ((basis, size), f32)
    record_like = ((VECS, basis + VECS), f32)
    weights_like = ((3, rank, (far_own.shape[0] + trees) * LANES), bf16)
    scalars = (near_col, near_count, far_col)
    slots, window = call(
        functools.partial(begin_kernel, trees),
        "begin",
        [operator_slots, window_like],
        [krylov_basis.reshape(-1, LANES), v_own, transfer_own],
    )
    arrived = exchange(slots)
    image, slots, weights = call(
        functools.partial(apply_kernel, trees, True),
        "apply_first",
        [image_like, product_slots, weights_like],
        [*scalars, arrived, window, near_own, u_own, far_own, transfer_own, top_own],
        scalars=3,
    )
    arrived = exchange(slots).reshape(-1, LANES)
    slots, window, record = call(
        functools.partial(middle_kernel, trees, rows_all),
        "middle",
        [operator_slots, window_like, record_like],
        [arrived, window, image, v_own, transfer_own],
    )
    arrived = exchange(slots)
    image, slots = call(
        functools.partial(apply_kernel, trees, False),
        "apply_second",
        [image_like, product_slots],
        [*scalars, arrived, window, near_own, u_own, weights],
        scalars=3,
    )
    arrived = exchange(slots).reshape(-1, LANES)
    block, records = call(
        functools.partial(end_kernel, rows_all),
        "end",
        [((VECS * size // LANES, LANES), f32), ((STEPS,) + record_like[0], f32)],
        [arrived, window, image, record],
    )
    return (block.reshape(VECS, 1, size), jnp.transpose(records, (0, 2, 1)))


def solution(mesh):
    return jax.shard_map(
        local,
        mesh=mesh,
        in_specs=(
            P(None, "lvl", "clus"),
            P("lvl", "clus", None, None, None),
            P("lvl", "clus", None),
            P("lvl", "clus"),
            P("lvl", "clus", None),
            P("lvl", "clus", None, None),
            P("lvl", "clus", None, None),
            P("lvl", "clus", None, None, None),
            P("lvl", "clus", None, None),
            P("lvl", "clus", None, None, None),
        ),
        out_specs=(P(None, "lvl", "clus"), P()),
        check_vma=False,
    )
```

time: 143 us -> 54.5 us (0.38)
  blocking collectives: 116 us -> 28 us
  waiting for transfers between devices: 0.02 us -> 7.27 us
  other arithmetic: 6.2 us -> 0 us
  Pallas kernels: 0 us -> 6.17 us
  matrix products: 5.25 us -> 0 us
  starting transfers between devices: 8.77 us -> 7.33 us
    psum x2 -> x0, blocking collectives: 74.3 us -> none  [orthogonalize(): lax.psum((row_products(window, window), row_products(window, image_block)...]
    all_gather x4 -> x0, blocking collectives: 41.4 us -> none  [the longest x2 24.7 us: far_field(): arrived = lax.all_gather(flat_skel, 'clus', axis=0, tiled=True)]
    all_to_all x0 -> x3, blocking collectives: none -> 28 us  [exchange(): return lax.all_to_all(slots, AXES, 0, 0, tiled=True)]
    ppermute x4 -> x0, starting transfers between devices: 8.77 us -> none  [the longest x2 6.06 us: padded_2(): lax.ppermute(lax.slice_in_dim(block, block.shape[dim] - width, None, axis...]
    all_to_all x0 -> x1, starting transfers between devices: none -> 7.33 us  [exchange(): return lax.all_to_all(slots, AXES, 0, 0, tiled=True)]
    all_to_all x0 -> x1, waiting for transfers between devices: none -> 7.27 us  [exchange(): return lax.all_to_all(slots, AXES, 0, 0, tiled=True)]
    pallas_call x0 -> x5, Pallas kernels: none -> 6.17 us  [call(): pl.pallas_call(kernel, name=name, out_shape=[jax.ShapeDtypeStruct(shape,...]
    dot_general x32 -> x0, matrix products: 4.86 us -> none  [the longest x6 0.82 us: row_products(): return jnp.dot(left_rows, right_rows.T, precision=PRECISE)]
  transfers between devices with their start and end apart: 4 -> 1, of which waited for: 0 -> 1; matrix products, arithmetic and copies ran while one was open for 3% -> 0% of each run, Pallas kernels for 0% -> 0%
where the time goes in v2:
time: 54.5 us; the launch traced here: 54 us
  blocking collectives  28 us (51%)
  starting transfers between devices  7.33 us (13%)
  waiting for transfers between devices  7.27 us (13%)
  Pallas kernels  6.17 us (11%)
  local copies, waits for them, and re-layouts  3.83 us (7%)
  between operations  1.36 us (2%)
    all_to_all x3, blocking collectives, exchange(): return lax.all_to_all(slots, AXES, 0, 0, tiled=True)  28 us
    all_to_all x1, starting transfers between devices, exchange(): return lax.all_to_all(slots, AXES, 0, 0, tiled=True)  7.33 us
    all_to_all x1, waiting for transfers between devices, exchange(): return lax.all_to_all(slots, AXES, 0, 0, tiled=True)  7.27 us
    pallas_call x5, Pallas kernels, call(): pl.pallas_call(kernel, name=name, out_shape=[jax.ShapeDtypeStruct(shape,...  6.17 us
    unnamed x24, local copies, waits for them, and re-layouts  3.83 us
  transfers between devices with their start and end apart: 1, of which 1 were waited for; matrix products, arithmetic and copies ran while one was open for 0% of the time, Pallas kernels for 0%

profile of v2, /device:TPU:0, one launch (start us, length us, event | category | flops | bytes accessed | tf_op | source)
XLA Modules:
  0.0 54.0 jit_solution(15739592670445054968)
XLA Ops:
  0.6 0.0 copy-start.2
  0.6 0.7 %copy-done.2 = f32[1,1,32,32]{3,2,1,0:T(8,128)S(1)} copy-done((f32[1,1,32,32]{3,2,1,0:T(8,128)S(1)}, f32[1,1,32,32]{3,2,1,0:T(8,128)}, u32[]{:S(2)}) %copy-start.2) | copy-done | bytes 4120
  1.3 0.0 copy-start.6
  1.4 0.7 %copy-done.6 = bf16[1,1,32,256]{3,2,1,0:T(8,128)(2,1)S(1)} copy-done((bf16[1,1,32,256]{3,2,1,0:T(8,128)(2,1)S(1)}, bf16[1,1,32,256]{3,2,1,0:T(8,128)(2,1)}, u32[]{:S(2)}) %copy-start.6) | copy-done | bytes 16408
  2.1 0.0 copy-start.9
  2.1 0.7 %copy-done.9 = f32[8,1,256]{2,1,0:T(1,128)S(1)} copy-done((f32[8,1,256]{2,1,0:T(1,128)S(1)}, f32[8,1,256]{2,1,0:T(1,128)}, u32[]{:S(2)}) %copy-start.9) | copy-done | bytes 8216
  2.8 1.0 %begin.1 = (bf16[32,4,384]{2,1,0:T(4,128)(2,1)}, f32[8,256]{1,0:T(8,128)S(1)}) custom-call(f32[16,128]{1,0:T(8,128)S(1)} %bitcast.24, bf16[32,256]{1,0:T(8,128)(2,1)S(1)} %bitcast.20, f32[32,32]{1,0:T(8,128)S(1)} %bitcast.15), custom_call_target="tpu_custom_call" | custom-call | tf_op jit(solution)/shard_map/begin/pallas_call | solution.py:242
  3.8 0.0 copy-start.3
  3.8 0.0 copy-start.4
  3.8 0.0 copy-start.5
  3.8 0.0 copy-start.8
  3.8 7.3 %all-to-all-start = ((bf16[32,4,384]{2,1,0:T(4,128)(2,1)}), bf16[32,4,384]{2,1,0:T(4,128)(2,1)S(1)}, u32[]{:S(2)}, u32[]{:S(2)}) async-start(bf16[32,4,384]{2,1,0:T(4,128)(2,1)} %get-tuple-element.14), calls=%async_computation | async-start | bytes 196608 | tf_op jit(solution)/shard_map/all_to_all | solution.py:253
  11.8 7.3 %all-to-all-done.arrived_ref = bf16[32,4,384]{2,1,0:T(4,128)(2,1)S(1)} async-done(((bf16[32,4,384]{2,1,0:T(4,128)(2,1)}), bf16[32,4,384]{2,1,0:T(4,128)(2,1)S(1)}, u32[]{:S(2)}, u32[]{:S(2)}) %all-to-all-start) | async-done | bytes 98336 | tf_op jit(solution)/shard_map/all_to_all | solution.py:253
  19.0 0.0 copy-start.10
  19.0 0.0 copy-start.11
  19.0 0.0 copy-done.3
  19.0 0.0 copy-done.4
  19.0 0.0 copy-done.5
  19.0 0.0 copy-done.8
  19.1 0.6 %copy-done.10 = s32[1,1,4]{2,1,0:T(1,128)S(1)} copy-done((s32[1,1,4]{2,1,0:T(1,128)S(1)}, s32[1,1,4]{2,1,0:T(1,128)}, u32[]{:S(2)}) %copy-start.10) | copy-done | bytes 40
  19.7 0.0 copy-done.11
  19.7 0.0 copy-start
  19.7 1.0 %copy-done = bf16[1,1,4,256,256]{4,3,2,1,0:T(8,128)(2,1)S(1)} copy-done((bf16[1,1,4,256,256]{4,3,2,1,0:T(8,128)(2,1)S(1)}, bf16[1,1,4,256,256]{4,3,2,1,0:T(8,128)(2,1)}, u32[]{:S(2)}) %copy-start) | copy-done | bytes 524312
  20.7 0.0 copy-start.1
  20.7 1.6 %apply_first.1 = (f32[4,256]{1,0:T(4,128)S(1)}, f32[32,4,128]{2,1,0:T(4,128)S(1)}, bf16[3,32,1280]{2,1,0:T(8,128)(2,1)S(1)}) custom-call(s32[1,1,4]{2,1,0:T(1,128)S(1)} %copy-done.10, s32[1,1]{1,0:T(1,128)S(6)} %copy.13.near_count_ref, s32[1,1,6]{2,1,0:T(1,128)S(1)} %copy-done.11, bf16[32,4,384]{2,1,0:T(4,128)(2,1)S(1)} %all-to-all-done.arrived_ref, ...), custom_call_target="tpu_custom_call" | custom-call | tf_op jit(solution)/shard_map/apply_first/pallas_call | solution.py:242
  22.4 0.0 copy-start.7
  22.4 9.2 %all_to_all.20 = f32[32,4,128]{2,1,0:T(4,128)S(1)} all-to-all(f32[32,4,128]{2,1,0:T(4,128)S(1)} %get-tuple-element.16), channel_id=1, replica_groups=mesh['clus'=8,'lvl'=4] {'clus','lvl'}, dimensions={0} | all-to-all | bytes 131072 | tf_op jit(solution)/shard_map/all_to_all | solution.py:253
  31.6 0.0 copy-done.7
  31.6 1.0 %middle.1 = (bf16[32,4,384]{2,1,0:T(4,128)(2,1)S(1)}, f32[8,256]{1,0:T(8,128)S(1)}, f32[4,12]{1,0:T(4,128)S(1)}) custom-call(f32[128,128]{1,0:T(8,128)S(1)} %bitcast.13, f32[8,256]{1,0:T(8,128)S(1)} %get-tuple-element.15.window_ref, f32[4,256]{1,0:T(4,128)S(1)} %get-tuple-element.17.image_ref, bf16[32,256]{1,0:T(8,128)(2,1)S(1)} %bitcast.21, ...), custom_call_target="tpu_custom_call" | custom-call | tf_op jit(solution)/shard_map/middle/pallas_call | solution.py:242
  32.6 9.6 %all_to_all.21.arrived_ref = bf16[32,4,384]{2,1,0:T(4,128)(2,1)S(1)} all-to-all(bf16[32,4,384]{2,1,0:T(4,128)(2,1)S(1)} %get-tuple-element.18), channel_id=1, replica_groups=mesh['clus'=8,'lvl'=4] {'clus','lvl'}, dimensions={0} | all-to-all | bytes 196608 | tf_op jit(solution)/shard_map/all_to_all | solution.py:253
  42.2 0.0 copy-done.1
  42.2 1.3 %apply_second.1 = (f32[4,256]{1,0:T(4,128)S(1)}, f32[32,4,128]{2,1,0:T(4,128)S(1)}) custom-call(s32[1,1,4]{2,1,0:T(1,128)S(1)} %copy-done.10, s32[1,1]{1,0:T(1,128)S(6)} %copy.13.near_count_ref, s32[1,1,6]{2,1,0:T(1,128)S(1)} %copy-done.11, bf16[32,4,384]{2,1,0:T(4,128)(2,1)S(1)} %all_to_all.21.arrived_ref, f32[8,256]{1,0:T(8,128)S(1)} %get-tuple-element.19.window_ref, ...), custom_call_target="tpu_custom_call" | custom-call | tf_op jit(solution)/shard_map/apply_second/pallas_call | solution.py:242
  43.5 9.2 %all_to_all.22 = f32[32,4,128]{2,1,0:T(4,128)S(1)} all-to-all(f32[32,4,128]{2,1,0:T(4,128)S(1)} %get-tuple-element.21), channel_id=1, replica_groups=mesh['clus'=8,'lvl'=4] {'clus','lvl'}, dimensions={0} | all-to-all | bytes 131072 | tf_op jit(solution)/shard_map/all_to_all | solution.py:253
  52.7 1.2 %end.1 = (f32[8,128]{1,0:T(8,128)}, f32[2,4,12]{2,1,0:T(4,128)}) custom-call(f32[128,128]{1,0:T(8,128)S(1)} %bitcast.14, f32[8,256]{1,0:T(8,128)S(1)} %get-tuple-element.19.window_ref, f32[4,256]{1,0:T(4,128)S(1)} %get-tuple-element.22.image_ref, f32[4,12]{1,0:T(4,128)S(1)} %get-tuple-element.23.first_ref), custom_call_target="tpu_custom_call" | custom-call | tf_op jit(solution)/shard_map/end/pallas_call | solution.py:242
Async XLA Ops:
  0.6 0.7 %copy-start.2 = (f32[1,1,32,32]{3,2,1,0:T(8,128)S(1)}, f32[1,1,32,32]{3,2,1,0:T(8,128)}, u32[]{:S(2)}) copy-start(f32[1,1,32,32]{3,2,1,0:T(8,128)} %param.18) | copy-start | bytes 12292
  1.3 0.7 %copy-start.6 = (bf16[1,1,32,256]{3,2,1,0:T(8,128)(2,1)S(1)}, bf16[1,1,32,256]{3,2,1,0:T(8,128)(2,1)}, u32[]{:S(2)}) copy-start(bf16[1,1,32,256]{3,2,1,0:T(8,128)(2,1)} %param.15) | copy-start | bytes 49156
  2.1 0.7 %copy-start.9 = (f32[8,1,256]{2,1,0:T(1,128)S(1)}, f32[8,1,256]{2,1,0:T(1,128)}, u32[]{:S(2)}) copy-start(f32[8,1,256]{2,1,0:T(1,128)} %param.10) | copy-start | bytes 24580
  3.8 15.3 %copy-start.3 = (f32[1,1,32,32]{3,2,1,0:T(8,128)S(1)}, f32[1,1,32,32]{3,2,1,0:T(8,128)}, u32[]{:S(2)}) copy-start(f32[1,1,32,32]{3,2,1,0:T(8,128)} %param.18) | copy-start | bytes 12292
  3.8 15.3 %copy-start.4 = (f32[1,1,6,32,32]{4,3,2,1,0:T(8,128)S(1)}, f32[1,1,6,32,32]{4,3,2,1,0:T(8,128)}, u32[]{:S(2)}) copy-start(f32[1,1,6,32,32]{4,3,2,1,0:T(8,128)} %param.17) | copy-start | bytes 73732
  3.8 15.3 %copy-start.5 = (f32[1,1,4,32,32]{4,3,2,1,0:T(8,128)S(1)}, f32[1,1,4,32,32]{4,3,2,1,0:T(8,128)}, u32[]{:S(2)}) copy-start(f32[1,1,4,32,32]{4,3,2,1,0:T(8,128)} %param.19) | copy-start | bytes 49156
  3.8 15.3 %copy-start.8 = (bf16[1,1,32,256]{3,2,1,0:T(8,128)(2,1)S(1)}, bf16[1,1,32,256]{3,2,1,0:T(8,128)(2,1)}, u32[]{:S(2)}) copy-start(bf16[1,1,32,256]{3,2,1,0:T(8,128)(2,1)} %param.16) | copy-start | bytes 49156
  3.8 15.3 %all-to-all-start = ((bf16[32,4,384]{2,1,0:T(4,128)(2,1)}), bf16[32,4,384]{2,1,0:T(4,128)(2,1)S(1)}, u32[]{:S(2)}, u32[]{:S(2)}) async-start(bf16[32,4,384]{2,1,0:T(4,128)(2,1)} %get-tuple-element.14), calls=%async_computation | async-start | bytes 196608 | tf_op jit(solution)/shard_map/all_to_all | solution.py:253
  19.0 0.7 %copy-start.10 = (s32[1,1,4]{2,1,0:T(1,128)S(1)}, s32[1,1,4]{2,1,0:T(1,128)}, u32[]{:S(2)}) copy-start(s32[1,1,4]{2,1,0:T(1,128)} %near_col_ref.3) | copy-start | bytes 52
  19.0 0.7 %copy-start.11 = (s32[1,1,6]{2,1,0:T(1,128)S(1)}, s32[1,1,6]{2,1,0:T(1,128)}, u32[]{:S(2)}) copy-start(s32[1,1,6]{2,1,0:T(1,128)} %far_col_ref.3) | copy-start | bytes 76
  19.7 1.0 %copy-start = (bf16[1,1,4,256,256]{4,3,2,1,0:T(8,128)(2,1)S(1)}, bf16[1,1,4,256,256]{4,3,2,1,0:T(8,128)(2,1)}, u32[]{:S(2)}) copy-start(bf16[1,1,4,256,256]{4,3,2,1,0:T(8,128)(2,1)} %param.11) | copy-start | bytes 1572868
  20.7 21.4 %copy-start.1 = (bf16[1,1,4,256,256]{4,3,2,1,0:T(8,128)(2,1)S(1)}, bf16[1,1,4,256,256]{4,3,2,1,0:T(8,128)(2,1)}, u32[]{:S(2)}) copy-start(bf16[1,1,4,256,256]{4,3,2,1,0:T(8,128)(2,1)} %param.11) | copy-start | bytes 1572868
  22.4 9.2 %copy-start.7 = (bf16[1,1,32,256]{3,2,1,0:T(8,128)(2,1)S(1)}, bf16[1,1,32,256]{3,2,1,0:T(8,128)(2,1)}, u32[]{:S(2)}) copy-start(bf16[1,1,32,256]{3,2,1,0:T(8,128)(2,1)} %param.15) | copy-start | bytes 49156

commit v3 on v2

v3 whole, which is shorter than its diff:
```python
import functools

import jax
import jax.numpy as jnp
from jax import lax
from jax.experimental import pallas as pl
from jax.experimental.pallas import tpu as pltpu
from jax.sharding import PartitionSpec as P

VECS = 4
STEPS = 2
LANES = 128
PIECE = 16
UNROLL = 32
AXES = ("clus", "lvl")

PRECISE = lax.Precision.HIGHEST
ROWS_DIMS = (((1,), (1,)), ((), ()))
F32, BF16 = jnp.float32, jnp.bfloat16


def rows_dot(left, right, precision=None):
    return lax.dot_general(
        left, right, ROWS_DIMS, precision=precision, preferred_element_type=F32
    )


def precise_dot(left, right):
    return jnp.dot(left, right, precision=PRECISE, preferred_element_type=F32)


def three_parts(values):
    high = values.astype(BF16)
    rest = values - high.astype(F32)
    middle = rest.astype(BF16)
    low = (rest - middle.astype(F32)).astype(BF16)
    return high, middle, low


def lane_parts(values, part):
    high = values.astype(BF16).astype(F32)
    rest = values - high
    middle = rest.astype(BF16).astype(F32)
    low = rest - middle
    return jnp.where(part == 0, high, jnp.where(part == 1, middle, jnp.where(part == 2, low, 0.0)))


def wide_parts(values, count):
    return [part.astype(F32) for part in three_parts(values)[:count]]


def lanes_of(shape):
    return lax.broadcasted_iota(jnp.int32, shape, len(shape) - 1)


def over_slots(count, store):
    step = min(count, UNROLL)
    if count == step:
        for slot in range(count):
            store(slot, slot)
        return

    def body(at, carry):
        for inner in range(step):
            store(at * step + inner, inner)
        return carry

    lax.fori_loop(0, count // step, body, 0)


def split_rows(flat, rows):
    halves = flat.shape[0] // rows
    return jnp.concatenate(
        [flat[pl.ds(half, rows, stride=halves), :] for half in range(halves)], axis=1
    )


def store_rows(flat_ref, values):
    rows = values.shape[0]
    halves = flat_ref.shape[0] // rows
    for half in range(halves):
        flat_ref[pl.ds(half, rows, stride=halves), :] = values[:, half * LANES : (half + 1) * LANES]


def skeleton_of(parts, v_basis):
    rows = rows_dot(jnp.concatenate(parts, axis=0), v_basis)
    return [rows[at : at + VECS] for at in range(0, rows.shape[0], VECS)]


def begin_kernel(trees, basis_hbm, v_hbm, transfer_hbm, slots_ref, window_ref, *scratch):
    basis_ref, v_ref, transfer_ref, sems = scratch
    copies = [
        pltpu.make_async_copy(source, target, sems.at[at])
        for at, (source, target) in enumerate(
            ((basis_hbm, basis_ref), (v_hbm, v_ref), (transfer_hbm, transfer_ref))
        )
    ]
    for copy in copies:
        copy.start()
    for copy in copies:
        copy.wait()
    basis, size = window_ref.shape
    rank = v_ref.shape[0]
    window = split_rows(basis_ref, basis)
    window_ref[...] = window
    current = window[basis - VECS :]
    lowered = current.astype(BF16)
    rest = current - lowered.astype(F32)
    parts = [lowered, *three_parts(window[: basis - VECS]), *three_parts(rest)[:2]]
    rows = skeleton_of([part.astype(F32) for part in parts], v_ref[...].astype(F32))
    skeletons = jnp.concatenate([rows[0], rows[1] + rows[2] + rows[3], rows[4] + rows[5]], axis=0)
    coarse = precise_dot(skeletons, transfer_ref[...])
    own_tree = lax.axis_index("lvl")

    def tails(values):
        exact, old, extra = (values[at : at + VECS] for at in range(0, 3 * VECS, VECS))
        first = jnp.concatenate(wide_parts(exact, 3) + [extra], axis=1)
        blank = jnp.zeros((VECS, LANES - 2 * rank), F32)
        second = jnp.concatenate([blank] + wide_parts(old, 2), axis=1)
        return first.astype(BF16), second

    tree_first, tree_second = tails(skeletons)
    level_first, level_second = tails(coarse)
    lane = lanes_of((VECS, LANES))
    turns = LANES // PIECE
    tiles = [
        window[row : row + VECS, at : at + LANES]
        for row in range(0, basis, VECS)
        for at in range(0, size, LANES)
    ]
    turned = [
        [pltpu.roll(tile, (LANES - PIECE * c) % LANES, 1) if c else tile for c in range(turns)]
        for tile in tiles
    ]
    part = lane // PIECE

    def store(slot, at):
        tile = turned[at // turns % len(tiles)]
        c = at % turns
        copies_of = jnp.where(
            part == 0, tile[c], jnp.where(part == 1, tile[(c - 1) % turns], tile[(c - 2) % turns])
        )
        piece = lane_parts(copies_of, part)
        same = lax.rem(jnp.int32(slot), jnp.int32(trees)) == own_tree
        second = jnp.where(same, tree_second, level_second)
        slots_ref[slot, :, :size] = lowered
        slots_ref[slot, :, size : size + LANES] = level_first
        slots_ref[slot, :, size + LANES :] = (piece + second).astype(BF16)

    over_slots(slots_ref.shape[0], store)

    def store_tree(leaf, at):
        slots_ref[leaf * trees + own_tree, :, size : size + LANES] = tree_first

    over_slots(slots_ref.shape[0] // trees, store_tree)


def prepare_kernel(
    near_col_ref,
    near_count_ref,
    far_col_ref,
    near_hbm,
    far_coupling_ref,
    transfer_ref,
    top_ref,
    weights_ref,
    near_ref,
    sem,
):
    copy = pltpu.make_async_copy(near_hbm, near_ref, sem)
    copy.start()
    own_tree = lax.axis_index("lvl")
    far_slots = far_coupling_ref.shape[0]
    trees, rank = top_ref.shape[0], top_ref.shape[1]
    transfer = transfer_ref[...]
    for slot in range(far_slots + trees):
        if slot < far_slots:
            block = far_coupling_ref[slot]
        else:
            tree = slot - far_slots
            block = precise_dot(transfer, jnp.where(tree != own_tree, top_ref[tree], 0.0))
        wide = jnp.concatenate([block] * (LANES // rank), axis=1)
        for part, piece in enumerate(three_parts(wide)):
            weights_ref[part, :, slot * LANES : (slot + 1) * LANES] = piece
    copy.wait()


def sources_of(far_col_ref, trees):
    own_tree = lax.axis_index("lvl")
    own_leaf = lax.axis_index("clus")
    places = [far_col_ref[0, 0, slot] * trees + own_tree for slot in range(far_col_ref.shape[2])]
    return places + [own_leaf * trees + tree for tree in range(trees)]


def couple(values, weights_ref):
    lowered = values.astype(BF16)
    return sum(rows_dot(lowered, weights_ref[part]) for part in range(3))


def product_lanes(window, image):
    basis = window.shape[0]
    stacked = jnp.concatenate([window, image], axis=0)
    products = rows_dot(stacked, stacked, PRECISE)
    pieces = [products[basis:]]
    for at in range(0, basis, VECS):
        pieces.append(products[at : at + VECS, :basis])
    return jnp.concatenate(pieces, axis=1)


def framed(before, values, after):
    rows = values.shape[0]
    pieces = [jnp.zeros((rows, before), F32)] if before else []
    pieces.append(values)
    if after:
        pieces.append(jnp.zeros((rows, after), F32))
    return jnp.concatenate(pieces, axis=1)


def first_kernel(
    trees,
    near_col_ref,
    near_count_ref,
    far_col_ref,
    arrived_ref,
    window_ref,
    weights_ref,
    near_ref,
    u_ref,
    v_ref,
    transfer_ref,
    image_ref,
    slots_ref,
    window_coupled_ref,
):
    own_tree = lax.axis_index("lvl")
    size = near_ref.shape[1]
    rank = v_ref.shape[0]
    places = sources_of(far_col_ref, trees)
    first = [arrived_ref[place, :, size : size + LANES] for place in places]
    second = [arrived_ref[place, :, size + LANES :] for place in places]
    first = jnp.concatenate(first, axis=1).astype(F32)
    second = jnp.concatenate(second, axis=1).astype(F32)
    lane = lanes_of(first.shape) % LANES
    exact = jnp.where(lane < 3 * rank, first, 0.0)
    old = jnp.where(lane >= LANES - 2 * rank, second, 0.0)
    rows = couple(jnp.concatenate([exact, first, old], axis=0), weights_ref)
    window_coupled_ref[:VECS] = rows[2 * VECS :]
    window_coupled_ref[VECS:] = rows[VECS : 2 * VECS]
    image = jnp.dot(rows[:VECS].astype(BF16), u_ref[...], preferred_element_type=F32)
    count = near_count_ref[0, 0]
    for slot in range(near_ref.shape[0]):
        source = arrived_ref[near_col_ref[0, 0, slot] * trees + own_tree, :, :size]
        source = jnp.where(slot < count, source, jnp.zeros_like(source))
        image = image + rows_dot(source, near_ref[slot])
    image_ref[...] = image
    packed = product_lanes(window_ref[...], image)
    parts = [part.astype(F32) for part in three_parts(image)]
    pieces = skeleton_of(parts, v_ref[...].astype(F32))
    skeleton = pieces[0] + pieces[1] + pieces[2]
    coarse = precise_dot(skeleton, transfer_ref[...])
    room = LANES - 2 * rank
    packed = framed(PIECE, packed, room - PIECE - packed.shape[1])
    tree_tail = jnp.concatenate([packed, skeleton, skeleton], axis=1)
    level_tail = jnp.concatenate([packed, coarse, coarse], axis=1)
    narrow = lanes_of((VECS, LANES))
    from_low = narrow < PIECE
    from_high = (narrow >= 3 * PIECE) & (narrow < 4 * PIECE)
    total = slots_ref.shape[0]

    def store(slot, at):
        if isinstance(slot, int):
            low, high = max(slot - trees, 0), min(slot + trees, total - 1)
        else:
            low, high = jnp.maximum(slot - trees, 0), jnp.minimum(slot + trees, total - 1)
        low = arrived_ref[low, :, size + LANES :].astype(F32)
        high = arrived_ref[high, :, size + LANES :].astype(F32)
        both = jnp.where(narrow < 3 * PIECE, low, pltpu.roll(high, 3 * PIECE, 1))
        both = both + pltpu.roll(both, LANES - PIECE, 1) + pltpu.roll(both, LANES - 2 * PIECE, 1)
        same = lax.rem(jnp.int32(slot), jnp.int32(trees)) == own_tree
        tail = jnp.where(same, tree_tail, level_tail)
        slots_ref[slot, :, :size] = image
        slots_ref[slot, :, size:] = jnp.where(from_low | from_high, both, tail)

    over_slots(total, store)


def orthogonalized(total, window, image):
    basis = window.shape[0]
    projection = total[:, :basis]
    square = total[:, basis : basis + VECS]
    inner = jnp.zeros((VECS, basis), F32)
    remainder = image
    at = basis + VECS
    lane = lanes_of((1, basis))
    for b in range(basis):
        column = projection[:, b : b + 1]
        group = at + basis * (b // VECS)
        metric_row = total[b % VECS : b % VECS + 1, group : group + basis]
        metric_row = metric_row - jnp.where(lane == b, 2.0, 0.0)
        inner = inner + column * metric_row
        remainder = remainder - column * window[b : b + 1]
    columns = []
    for u in range(VECS):
        cross = jnp.sum(inner * projection[u : u + 1], axis=1, keepdims=True)
        columns.append(square[:, u : u + 1] + cross)
    row = lax.broadcasted_iota(jnp.int32, (VECS, 1), 0)
    factor = []
    for j in range(VECS):
        root = jnp.sqrt(columns[j][j : j + 1])
        scale = 1.0 / root
        lower = jnp.where(row > j, columns[j] * scale, 0.0)
        factor.append(jnp.where(row == j, root, lower))
        for u in range(j + 1, VECS):
            columns[u] = columns[u] - lower * lower[u : u + 1]
        solved = remainder[j : j + 1] * scale
        remainder = jnp.where(row == j, solved, remainder - lower * solved)
    record = jnp.concatenate([projection] + factor, axis=1)
    return remainder, record


def middle_kernel(
    trees,
    rows_all,
    near_col_ref,
    near_count_ref,
    far_col_ref,
    arrived_ref,
    window_ref,
    image_ref,
    window_coupled_ref,
    weights_ref,
    near_ref,
    u_ref,
    v_ref,
    transfer_ref,
    slots_ref,
    next_window_ref,
    near_part_ref,
    record_ref,
):
    own_tree = lax.axis_index("lvl")
    own_leaf = lax.axis_index("clus")
    window = window_ref[...]
    basis, size = window.shape
    rank = v_ref.shape[0]
    lane = lanes_of((VECS, LANES))
    group = lane // PIECE
    turns = LANES // PIECE
    tile_count = basis // VECS * (size // LANES)
    low_tiles, high_tiles = [], []
    total = jnp.zeros((VECS, LANES), F32)
    for slot in range(tile_count * turns):
        tail = arrived_ref[slot, :, size:]
        total = total + tail
        c = slot % turns
        turned = pltpu.roll(tail, PIECE * c, 1) if c else tail
        if c == 0:
            low_tiles.append(turned)
            high_tiles.append(turned)
        else:
            low_tiles[-1] = jnp.where(group == c, turned, low_tiles[-1])
            high_tiles[-1] = jnp.where(group == (c + 3) % turns, turned, high_tiles[-1])
    slots = arrived_ref.shape[0]
    if slots > tile_count * turns:
        total = lax.fori_loop(
            tile_count * turns, slots, lambda at, held: held + arrived_ref[at, :, size:], total
        )
    high_tiles = [pltpu.roll(tile, LANES - 3 * PIECE, 1) for tile in high_tiles]
    total = total[:, PIECE : LANES - 2 * rank] * (1.0 / rows_all)

    def rows_from(tiles):
        per_row = size // LANES
        rows = [
            jnp.concatenate(tiles[at : at + per_row], axis=1)
            for at in range(0, tile_count, per_row)
        ]
        return jnp.concatenate(rows, axis=0)

    leaves = slots // trees
    low_place = jnp.maximum(own_leaf - 1, 0) * trees + own_tree
    high_place = jnp.minimum(own_leaf + 1, leaves - 1) * trees + own_tree
    tails = jnp.concatenate(
        [arrived_ref[place, :, size:] for place in sources_of(far_col_ref, trees)], axis=1
    )
    tails = lane_parts(tails, lanes_of(tails.shape) % LANES // rank - (LANES // rank - 2))
    wide_lane = lanes_of(tails.shape) % LANES
    tails = jnp.where(wide_lane >= LANES - 2 * rank, tails, 0.0)
    coupled = couple(tails, weights_ref)
    images = jnp.concatenate(
        [
            arrived_ref[low_place, :, :size],
            image_ref[...],
            arrived_ref[high_place, :, :size],
            coupled,
        ],
        axis=1,
    )
    windows = jnp.concatenate(
        [rows_from(low_tiles), window, rows_from(high_tiles), window_coupled_ref[...]], axis=1
    )
    solved, record = orthogonalized(total, windows, images)
    record_ref[...] = record
    low_block, new_block, high_block = (solved[:, at : at + size] for at in range(0, 3 * size, size))
    next_window = jnp.concatenate([window[VECS:], new_block], axis=0)
    next_window_ref[...] = next_window
    count = near_count_ref[0, 0]
    near_part = jnp.zeros((VECS, size), F32)
    for slot in range(near_ref.shape[0]):
        leaf = near_col_ref[0, 0, slot]
        source = jnp.where(leaf < own_leaf, low_block, jnp.where(leaf > own_leaf, high_block, new_block))
        source = jnp.where(slot < count, source, 0.0).astype(BF16)
        near_part = near_part + rows_dot(source, near_ref[slot])
    near_part_ref[...] = near_part
    far_part = jnp.dot(
        solved[:, 3 * size :].astype(BF16), u_ref[...], preferred_element_type=F32
    )
    skeleton = rows_dot(new_block.astype(BF16), v_ref[...])
    coarse = precise_dot(skeleton, transfer_ref[...])
    packed = product_lanes(next_window, near_part + far_part)
    packed = framed(0, packed, rank - packed.shape[1])
    copies = LANES // rank - 1
    tree_tail = jnp.concatenate([packed] + [skeleton] * copies, axis=1)
    level_tail = jnp.concatenate([packed] + [coarse] * copies, axis=1)

    def store(slot, at):
        slots_ref[slot] = level_tail

    over_slots(slots, store)

    def store_tree(leaf, at):
        slots_ref[leaf * trees + own_tree] = tree_tail

    over_slots(leaves, store_tree)


def end_kernel(
    trees,
    rows_all,
    far_col_ref,
    arrived_ref,
    window_ref,
    near_part_ref,
    weights_ref,
    u_ref,
    first_ref,
    block_ref,
    records_ref,
):
    rank = u_ref.shape[0]
    tails = jnp.concatenate(
        [arrived_ref[place] for place in sources_of(far_col_ref, trees)], axis=1
    )
    part = lanes_of(tails.shape) % LANES // rank - 1
    coupled = couple(jnp.where(part >= 0, lane_parts(tails, part), 0.0), weights_ref)
    far_part = jnp.dot(coupled.astype(BF16), u_ref[...], preferred_element_type=F32)
    slots = arrived_ref.shape[0]
    near = min(slots, UNROLL)
    total = arrived_ref[0]
    for slot in range(1, near):
        total = total + arrived_ref[slot]
    if slots > near:
        total = lax.fori_loop(near, slots, lambda at, held: held + arrived_ref[at], total)
    total = total[:, :rank] * (1.0 / rows_all)
    new_block, record = orthogonalized(total, window_ref[...], near_part_ref[...] + far_part)
    store_rows(block_ref, new_block)
    records_ref[0] = first_ref[...]
    records_ref[1] = record


def call(kernel, name, outs, ins, places, scratch=(), vmem=16 << 20, bytes_accessed=1 << 20):
    spaces = {"s": pltpu.SMEM, "v": pltpu.VMEM, "h": pltpu.HBM}
    return pl.pallas_call(
        kernel,
        name=name,
        out_shape=[jax.ShapeDtypeStruct(shape, dtype) for shape, dtype in outs],
        in_specs=[pl.BlockSpec(memory_space=spaces[place]) for place in places],
        out_specs=[pl.BlockSpec(memory_space=pltpu.VMEM)] * len(outs),
        scratch_shapes=list(scratch),
        cost_estimate=pl.CostEstimate(flops=0, bytes_accessed=bytes_accessed, transcendentals=0),
        compiler_params=pltpu.CompilerParams(vmem_limit_bytes=vmem),
    )(*ins)


def exchange(slots):
    return lax.all_to_all(slots, AXES, 0, 0, tiled=True)


def local(
    krylov_basis,
    near_block,
    near_col,
    near_count,
    far_col,
    v_basis,
    u_basis,
    far_coupling,
    transfer,
    top_coupling,
):
    basis, _, size = krylov_basis.shape
    trees = lax.axis_size("lvl")
    devices = lax.axis_size("clus") * trees
    rows_all = float(devices * size)
    flat_basis = krylov_basis.reshape(-1, LANES)
    v_own, u_own, transfer_own = v_basis[0, 0], u_basis[0, 0], transfer[0, 0]
    rank = v_own.shape[0]
    far_own, top_own, near_own = far_coupling[0, 0], top_coupling[0, 0], near_block[0, 0]
    image_like = ((VECS, size), F32)
    window_like = ((basis, size), F32)
    record_like = ((VECS, basis + VECS), F32)
    weights_like = ((3, rank, (far_own.shape[0] + trees) * LANES), BF16)
    slots, window = call(
        functools.partial(begin_kernel, trees),
        "begin",
        [((devices, VECS, size + 2 * LANES), BF16), window_like],
        [flat_basis, v_own, transfer_own],
        "hhh",
        [
            pltpu.VMEM(flat_basis.shape, F32),
            pltpu.VMEM(v_own.shape, BF16),
            pltpu.VMEM(transfer_own.shape, F32),
            pltpu.SemaphoreType.DMA((3,)),
        ],
        vmem=None,
    )
    arrived = exchange(slots)
    weights, near_here = call(
        prepare_kernel,
        "prepare",
        [weights_like, (near_own.shape, BF16)],
        [near_col, near_count, far_col, near_own, far_own, transfer_own, top_own],
        "ssshvvv",
        [pltpu.SemaphoreType.DMA],
    )
    image, slots, window_coupled = call(
        functools.partial(first_kernel, trees),
        "first",
        [image_like, ((devices, VECS, size + LANES), F32), ((basis, rank), F32)],
        [
            near_col,
            near_count,
            far_col,
            arrived,
            window,
            weights,
            near_here,
            u_own,
            v_own,
            transfer_own,
        ],
        "sssvvvvvvv",
    )
    arrived = exchange(slots)
    slots, window, near_part, record = call(
        functools.partial(middle_kernel, trees, rows_all),
        "middle",
        [((devices, VECS, LANES), F32), window_like, image_like, record_like],
        [
            near_col,
            near_count,
            far_col,
            arrived,
            window,
            image,
            window_coupled,
            weights,
            near_here,
            u_own,
            v_own,
            transfer_own,
        ],
        "sssvvvvvvvvv",
    )
    arrived = exchange(slots)
    block, records = call(
        functools.partial(end_kernel, trees, rows_all),
        "end",
        [((VECS * size // LANES, LANES), F32), ((STEPS,) + record_like[0], F32)],
        [far_col, arrived, window, near_part, weights, u_own, record],
        "svvvvvv",
    )
    return (block.reshape(VECS, 1, size), jnp.transpose(records, (0, 2, 1)))


def solution(mesh):
    return jax.shard_map(
        local,
        mesh=mesh,
        in_specs=(
            P(None, "lvl", "clus"),
            P("lvl", "clus", None, None, None),
            P("lvl", "clus", None),
            P("lvl", "clus"),
            P("lvl", "clus", None),
            P("lvl", "clus", None, None),
            P("lvl", "clus", None, None),
            P("lvl", "clus", None, None, None),
            P("lvl", "clus", None, None),
            P("lvl", "clus", None, None, None),
        ),
        out_specs=(P(None, "lvl", "clus"), P()),
        check_vma=False,
    )
```

time: 54.5 us -> 44.3 us (0.81)
  blocking collectives: 28 us -> 20.5 us
  waiting for transfers between devices: 7.27 us -> 5.1 us
  local copies, waits for them, and re-layouts: 3.83 us -> 1.7 us
  Pallas kernels: 6.17 us -> 7.9 us
    all_to_all x3 -> x2, blocking collectives: 28 us -> 20.5 us  [exchange(): return lax.all_to_all(slots, AXES, 0, 0, tiled=True)]
    all_to_all x1, waiting for transfers between devices: 7.27 us -> 5.1 us  [exchange(): return lax.all_to_all(slots, AXES, 0, 0, tiled=True)]
    unnamed x24 -> x18, local copies, waits for them, and re-layouts: 3.83 us -> 1.7 us
    pallas_call x5, Pallas kernels: 6.17 us -> 7.9 us  [call(): pl.pallas_call(kernel, name=name, out_shape=[jax.ShapeDtypeStruct(shape,...]
  transfers between devices with their start and end apart: 1 -> 1, of which waited for: 1 -> 1; matrix products, arithmetic and copies ran while one was open for 0% -> 0% of each run, Pallas kernels for 0% -> 2%
where the time goes in v3:
time: 44.3 us; the launch traced here: 43.9 us
  blocking collectives  20.5 us (46%)
  Pallas kernels  7.9 us (18%)
  starting transfers between devices  7.33 us (17%)
  waiting for transfers between devices  5.1 us (12%)
  local copies, waits for them, and re-layouts  1.7 us (4%)
  between operations  1.39 us (3%)
    all_to_all x2, blocking collectives, exchange(): return lax.all_to_all(slots, AXES, 0, 0, tiled=True)  20.5 us
    pallas_call x5, Pallas kernels, call(): pl.pallas_call(kernel, name=name, out_shape=[jax.ShapeDtypeStruct(shape,...  7.9 us
    all_to_all x1, starting transfers between devices, exchange(): return lax.all_to_all(slots, AXES, 0, 0, tiled=True)  7.33 us
    all_to_all x1, waiting for transfers between devices, exchange(): return lax.all_to_all(slots, AXES, 0, 0, tiled=True)  5.1 us
    unnamed x18, local copies, waits for them, and re-layouts  1.7 us
  transfers between devices with their start and end apart: 1, of which 1 were waited for; matrix products, arithmetic and copies ran while one was open for 0% of the time, Pallas kernels for 2%

profile of v3, /device:TPU:0, one launch (start us, length us, event | category | flops | bytes accessed | tf_op | source)
XLA Modules:
  0.0 43.9 jit_solution(18220993111964462435)
XLA Ops:
  0.6 1.8 %begin.1 = (bf16[32,4,512]{2,1,0:T(4,128)(2,1)}, f32[8,256]{1,0:T(8,128)}) custom-call(f32[16,128]{1,0:T(8,128)} %bitcast.22, bf16[32,256]{1,0:T(8,128)(2,1)} %bitcast.14, f32[32,32]{1,0:T(8,128)} %bitcast.10), custom_call_target="tpu_custom_call" | custom-call | bytes 1048576 | tf_op jit(solution)/shard_map/begin/pallas_call | solution.py:472
  2.4 0.0 copy-start.1
  2.4 0.0 copy-start.4
  2.5 0.0 copy-start.5
  2.5 7.3 %all-to-all-start = ((bf16[32,4,512]{2,1,0:T(4,128)(2,1)}), bf16[32,4,512]{2,1,0:T(4,128)(2,1)S(1)}, u32[]{:S(2)}, u32[]{:S(2)}) async-start(bf16[32,4,512]{2,1,0:T(4,128)(2,1)} %get-tuple-element.15), calls=%async_computation | async-start | bytes 262144 | tf_op jit(solution)/shard_map/all_to_all | solution.py:485
  10.5 0.0 copy-start.7
  10.5 0.0 copy-start.8
  10.5 0.0 copy-done.1
  10.5 0.0 copy-done.4
  10.5 0.0 copy-done.5
  10.5 0.6 %copy-done.7 = s32[1,1,6]{2,1,0:T(1,128)S(1)} copy-done((s32[1,1,6]{2,1,0:T(1,128)S(1)}, s32[1,1,6]{2,1,0:T(1,128)}, u32[]{:S(2)}) %copy-start.7) | copy-done | bytes 48
  11.1 0.0 copy-done.8
  11.1 0.0 copy-start
  11.1 1.0 %copy-done = bf16[1,1,4,256,256]{4,3,2,1,0:T(8,128)(2,1)S(1)} copy-done((bf16[1,1,4,256,256]{4,3,2,1,0:T(8,128)(2,1)S(1)}, bf16[1,1,4,256,256]{4,3,2,1,0:T(8,128)(2,1)}, u32[]{:S(2)}) %copy-start) | copy-done | bytes 524312
  12.2 0.0 copy-start.2
  12.2 0.0 copy-start.3
  12.2 0.0 copy-start.6
  12.2 0.9 %prepare.1 = (bf16[3,32,1280]{2,1,0:T(8,128)(2,1)S(1)}, bf16[4,256,256]{2,1,0:T(8,128)(2,1)S(1)}) custom-call(s32[1,1,4]{2,1,0:T(1,128)S(1)} %copy-done.8, s32[1,1]{1,0:T(1,128)S(6)} %copy.13.near_count_ref, s32[1,1,6]{2,1,0:T(1,128)S(1)} %copy-done.7, bf16[4,256,256]{2,1,0:T(8,128)(2,1)S(1)} %bitcast.9, f32[6,32,32]{2,1,0:T(8,128)S(1)} %bitcast.20, ...), custom_call_target="tpu_custom_call" | custom-call | bytes 1048576 | tf_op jit(solution)/shard_map/prepare/pallas_call | solution.py:472
  13.1 5.1 %all-to-all-done.arrived_ref = bf16[32,4,512]{2,1,0:T(4,128)(2,1)S(1)} async-done(((bf16[32,4,512]{2,1,0:T(4,128)(2,1)}), bf16[32,4,512]{2,1,0:T(4,128)(2,1)S(1)}, u32[]{:S(2)}, u32[]{:S(2)}) %all-to-all-start) | async-done | bytes 131104 | tf_op jit(solution)/shard_map/all_to_all | solution.py:485
  18.2 0.0 copy-done.2
  18.2 0.0 copy-done.3
  18.2 0.0 copy-done.6
  18.2 1.5 %first.1 = (f32[4,256]{1,0:T(4,128)S(1)}, f32[32,4,384]{2,1,0:T(4,128)S(1)}, f32[8,32]{1,0:T(8,128)S(1)}) custom-call(s32[1,1,4]{2,1,0:T(1,128)S(1)} %copy-done.8, s32[1,1]{1,0:T(1,128)S(6)} %copy.13.near_count_ref, s32[1,1,6]{2,1,0:T(1,128)S(1)} %copy-done.7, bf16[32,4,512]{2,1,0:T(4,128)(2,1)S(1)} %all-to-all-done.arrived_ref, f32[8,256]{1,0:T(8,128)S(1)} %copy-done.6, ...), custom_call_target="tpu_custom_call" | custom-call | bytes 1048576 | tf_op jit(solution)/shard_map/first/pallas_call | solution.py:472
  19.7 11.2 %all_to_all.15.arrived_ref = f32[32,4,384]{2,1,0:T(4,128)S(1)} all-to-all(f32[32,4,384]{2,1,0:T(4,128)S(1)} %get-tuple-element.19), channel_id=1, replica_groups=mesh['clus'=8,'lvl'=4] {'clus','lvl'}, dimensions={0} | all-to-all | bytes 393216 | tf_op jit(solution)/shard_map/all_to_all | solution.py:485
  30.9 1.9 %middle.1 = (f32[32,4,128]{2,1,0:T(4,128)S(1)}, f32[8,256]{1,0:T(8,128)S(1)}, f32[4,256]{1,0:T(4,128)S(1)}, f32[4,12]{1,0:T(4,128)S(1)}) custom-call(s32[1,1,4]{2,1,0:T(1,128)S(1)} %copy-done.8, s32[1,1]{1,0:T(1,128)S(6)} %copy.13.near_count_ref, s32[1,1,6]{2,1,0:T(1,128)S(1)} %copy-done.7, f32[32,4,384]{2,1,0:T(4,128)S(1)} %all_to_all.15.arrived_ref, ...), custom_call_target="tpu_custom_call" | custom-call | bytes 1048576 | tf_op jit(solution)/shard_map/middle/pallas_call | solution.py:472
  32.8 9.3 %all_to_all.16.arrived_ref = f32[32,4,128]{2,1,0:T(4,128)S(1)} all-to-all(f32[32,4,128]{2,1,0:T(4,128)S(1)} %get-tuple-element.22), channel_id=1, replica_groups=mesh['clus'=8,'lvl'=4] {'clus','lvl'}, dimensions={0} | all-to-all | bytes 131072 | tf_op jit(solution)/shard_map/all_to_all | solution.py:485
  42.1 1.8 %end.1 = (f32[8,128]{1,0:T(8,128)}, f32[2,4,12]{2,1,0:T(4,128)}) custom-call(s32[1,1,6]{2,1,0:T(1,128)S(1)} %copy-done.7, f32[32,4,128]{2,1,0:T(4,128)S(1)} %all_to_all.16.arrived_ref, f32[8,256]{1,0:T(8,128)S(1)} %get-tuple-element.23.window_ref, f32[4,256]{1,0:T(4,128)S(1)} %get-tuple-element.24.near_part_ref, ...), custom_call_target="tpu_custom_call" | custom-call | bytes 1048576 | tf_op jit(solution)/shard_map/end/pallas_call | solution.py:472
Async XLA Ops:
  2.4 8.1 %copy-start.1 = (f32[1,1,32,32]{3,2,1,0:T(8,128)S(1)}, f32[1,1,32,32]{3,2,1,0:T(8,128)}, u32[]{:S(2)}) copy-start(f32[1,1,32,32]{3,2,1,0:T(8,128)} %param.18) | copy-start | bytes 12292
  2.4 8.0 %copy-start.4 = (f32[1,1,6,32,32]{4,3,2,1,0:T(8,128)S(1)}, f32[1,1,6,32,32]{4,3,2,1,0:T(8,128)}, u32[]{:S(2)}) copy-start(f32[1,1,6,32,32]{4,3,2,1,0:T(8,128)} %param.17) | copy-start | bytes 73732
  2.5 8.0 %copy-start.5 = (f32[1,1,4,32,32]{4,3,2,1,0:T(8,128)S(1)}, f32[1,1,4,32,32]{4,3,2,1,0:T(8,128)}, u32[]{:S(2)}) copy-start(f32[1,1,4,32,32]{4,3,2,1,0:T(8,128)} %param.19) | copy-start | bytes 49156
  2.5 15.7 %all-to-all-start = ((bf16[32,4,512]{2,1,0:T(4,128)(2,1)}), bf16[32,4,512]{2,1,0:T(4,128)(2,1)S(1)}, u32[]{:S(2)}, u32[]{:S(2)}) async-start(bf16[32,4,512]{2,1,0:T(4,128)(2,1)} %get-tuple-element.15), calls=%async_computation | async-start | bytes 262144 | tf_op jit(solution)/shard_map/all_to_all | solution.py:485
  10.5 0.7 %copy-start.7 = (s32[1,1,6]{2,1,0:T(1,128)S(1)}, s32[1,1,6]{2,1,0:T(1,128)}, u32[]{:S(2)}) copy-start(s32[1,1,6]{2,1,0:T(1,128)} %far_col_ref.7) | copy-start | bytes 76
  10.5 0.7 %copy-start.8 = (s32[1,1,4]{2,1,0:T(1,128)S(1)}, s32[1,1,4]{2,1,0:T(1,128)}, u32[]{:S(2)}) copy-start(s32[1,1,4]{2,1,0:T(1,128)} %near_col_ref.5) | copy-start | bytes 52
  11.1 1.0 %copy-start = (bf16[1,1,4,256,256]{4,3,2,1,0:T(8,128)(2,1)S(1)}, bf16[1,1,4,256,256]{4,3,2,1,0:T(8,128)(2,1)}, u32[]{:S(2)}) copy-start(bf16[1,1,4,256,256]{4,3,2,1,0:T(8,128)(2,1)} %param.11) | copy-start | bytes 1572868
  12.2 6.0 %copy-start.2 = (bf16[1,1,32,256]{3,2,1,0:T(8,128)(2,1)S(1)}, bf16[1,1,32,256]{3,2,1,0:T(8,128)(2,1)}, u32[]{:S(2)}) copy-start(bf16[1,1,32,256]{3,2,1,0:T(8,128)(2,1)} %param.15) | copy-start | bytes 49156
  12.2 6.0 %copy-start.3 = (bf16[1,1,32,256]{3,2,1,0:T(8,128)(2,1)S(1)}, bf16[1,1,32,256]{3,2,1,0:T(8,128)(2,1)}, u32[]{:S(2)}) copy-start(bf16[1,1,32,256]{3,2,1,0:T(8,128)(2,1)} %param.16) | copy-start | bytes 49156
  12.2 6.0 %copy-start.6 = (f32[8,256]{1,0:T(8,128)S(1)}, f32[8,256]{1,0:T(8,128)}, u32[]{:S(2)}) copy-start(f32[8,256]{1,0:T(8,128)} %get-tuple-element.16.window_ref) | copy-start | bytes 24580

commit v4 on v3

--- a/solution.py
+++ b/solution.py
@@ -45,10 +45,6 @@
     return jnp.where(part == 0, high, jnp.where(part == 1, middle, jnp.where(part == 2, low, 0.0)))
 
 
-def wide_parts(values, count):
-    return [part.astype(F32) for part in three_parts(values)[:count]]
-
-
 def lanes_of(shape):
     return lax.broadcasted_iota(jnp.int32, shape, len(shape) - 1)
 
@@ -82,9 +78,20 @@
         flat_ref[pl.ds(half, rows, stride=halves), :] = values[:, half * LANES : (half + 1) * LANES]
 
 
-def skeleton_of(parts, v_basis):
-    rows = rows_dot(jnp.concatenate(parts, axis=0), v_basis)
+def row_groups(rows):
     return [rows[at : at + VECS] for at in range(0, rows.shape[0], VECS)]
+
+
+def lane_tiles(values):
+    return [values[:, at : at + LANES] for at in range(0, values.shape[1], LANES)]
+
+
+def replicated(column):
+    return jnp.broadcast_to(column, (column.shape[0], LANES))
+
+
+def lane_sum(pairs):
+    return replicated(jnp.sum(sum(left * right for left, right in pairs), axis=1, keepdims=True))
 
 
 def begin_kernel(trees, basis_hbm, v_hbm, transfer_hbm, slots_ref, window_ref, *scratch):
@@ -107,22 +114,26 @@
     lowered = current.astype(BF16)
     rest = current - lowered.astype(F32)
     parts = [lowered, *three_parts(window[: basis - VECS]), *three_parts(rest)[:2]]
-    rows = skeleton_of([part.astype(F32) for part in parts], v_ref[...].astype(F32))
+    parts = jnp.concatenate([part.astype(F32) for part in parts], axis=0).astype(BF16)
+    repeats = LANES // rank
+    wide_basis = jnp.concatenate([v_ref[...]] * repeats, axis=0)
+    rows = row_groups(rows_dot(parts, wide_basis))
     skeletons = jnp.concatenate([rows[0], rows[1] + rows[2] + rows[3], rows[4] + rows[5]], axis=0)
-    coarse = precise_dot(skeletons, transfer_ref[...])
+    wide_transfer = jnp.concatenate([transfer_ref[...]] * repeats, axis=1)
+    coarse = precise_dot(skeletons[:, :rank], wide_transfer)
     own_tree = lax.axis_index("lvl")
 
     def tails(values):
-        exact, old, extra = (values[at : at + VECS] for at in range(0, 3 * VECS, VECS))
-        first = jnp.concatenate(wide_parts(exact, 3) + [extra], axis=1)
-        blank = jnp.zeros((VECS, LANES - 2 * rank), F32)
-        second = jnp.concatenate([blank] + wide_parts(old, 2), axis=1)
-        return first.astype(BF16), second
+        exact, old, extra = row_groups(values)
+        group = lanes_of((VECS, LANES)) // rank
+        first = jnp.where(group < 3, lane_parts(exact, group), extra)
+        return first.astype(BF16), lane_parts(old, group - (repeats - 2))
 
     tree_first, tree_second = tails(skeletons)
     level_first, level_second = tails(coarse)
     lane = lanes_of((VECS, LANES))
     turns = LANES // PIECE
+    kept = lane >= LANES - 2 * rank
     tiles = [
         window[row : row + VECS, at : at + LANES]
         for row in range(0, basis, VECS)
@@ -145,7 +156,7 @@
         second = jnp.where(same, tree_second, level_second)
         slots_ref[slot, :, :size] = lowered
         slots_ref[slot, :, size : size + LANES] = level_first
-        slots_ref[slot, :, size + LANES :] = (piece + second).astype(BF16)
+        slots_ref[slot, :, size + LANES :] = jnp.where(kept, second, piece).astype(BF16)
 
     over_slots(slots_ref.shape[0], store)
 
@@ -161,10 +172,12 @@
     far_col_ref,
     near_hbm,
     far_coupling_ref,
+    v_ref,
     transfer_ref,
     top_ref,
     weights_ref,
     near_ref,
+    maps_ref,
     sem,
 ):
     copy = pltpu.make_async_copy(near_hbm, near_ref, sem)
@@ -182,6 +195,11 @@
         wide = jnp.concatenate([block] * (LANES // rank), axis=1)
         for part, piece in enumerate(three_parts(wide)):
             weights_ref[part, :, slot * LANES : (slot + 1) * LANES] = piece
+    v_basis = v_ref[...]
+    carried = precise_dot(transfer.T, v_basis.astype(F32))
+    for part, piece in enumerate((v_basis, *three_parts(carried))):
+        for at in range(part * LANES, (part + 1) * LANES, rank):
+            maps_ref[at : at + rank] = piece
     copy.wait()
 
 
@@ -197,23 +215,31 @@
     return sum(rows_dot(lowered, weights_ref[part]) for part in range(3))
 
 
-def product_lanes(window, image):
+def product_lanes(window, image, at):
     basis = window.shape[0]
-    stacked = jnp.concatenate([window, image], axis=0)
-    products = rows_dot(stacked, stacked, PRECISE)
-    pieces = [products[basis:]]
-    for at in range(0, basis, VECS):
-        pieces.append(products[at : at + VECS, :basis])
-    return jnp.concatenate(pieces, axis=1)
-
-
-def framed(before, values, after):
-    rows = values.shape[0]
-    pieces = [jnp.zeros((rows, before), F32)] if before else []
-    pieces.append(values)
-    if after:
-        pieces.append(jnp.zeros((rows, after), F32))
-    return jnp.concatenate(pieces, axis=1)
+    window, image = lane_tiles(window), lane_tiles(image)
+    lane = lanes_of((VECS, LANES))
+    packed = jnp.zeros((VECS, LANES), F32)
+    for b in range(basis):
+        product = lane_sum([(tile, other[b : b + 1]) for tile, other in zip(image, window)])
+        packed = jnp.where(lane == at + b, product, packed)
+    at = at + basis
+    for u in range(VECS):
+        product = lane_sum([(tile, tile[u : u + 1]) for tile in image])
+        packed = jnp.where(lane == at + u, product, packed)
+    at = at + VECS
+    for b in range(basis):
+        product = lane_sum([(tile, tile[b : b + 1]) for tile in window])
+        for group in range(basis // VECS):
+            rows = product[group * VECS : (group + 1) * VECS]
+            packed = jnp.where(lane == at + group * basis + b, rows, packed)
+    return packed
+
+
+def mapped(rows, maps_ref):
+    products = lane_tiles(rows_dot(rows, maps_ref[...]))
+    skeleton, coarse = products[0], products[1] + products[2] + products[3]
+    return sum(row_groups(skeleton)), sum(row_groups(coarse))
 
 
 def first_kernel(
@@ -226,15 +252,14 @@
     weights_ref,
     near_ref,
     u_ref,
-    v_ref,
-    transfer_ref,
+    maps_ref,
     image_ref,
     slots_ref,
     window_coupled_ref,
 ):
     own_tree = lax.axis_index("lvl")
     size = near_ref.shape[1]
-    rank = v_ref.shape[0]
+    rank = u_ref.shape[0]
     places = sources_of(far_col_ref, trees)
     first = [arrived_ref[place, :, size : size + LANES] for place in places]
     second = [arrived_ref[place, :, size + LANES :] for place in places]
@@ -244,8 +269,9 @@
     exact = jnp.where(lane < 3 * rank, first, 0.0)
     old = jnp.where(lane >= LANES - 2 * rank, second, 0.0)
     rows = couple(jnp.concatenate([exact, first, old], axis=0), weights_ref)
-    window_coupled_ref[:VECS] = rows[2 * VECS :]
-    window_coupled_ref[VECS:] = rows[VECS : 2 * VECS]
+    linear = jnp.concatenate([rows[2 * VECS :], rows[VECS : 2 * VECS]], axis=0)
+    blank = jnp.zeros((2 * VECS, LANES - rank), F32)
+    window_coupled_ref[...] = jnp.concatenate([linear, blank], axis=1)
     image = jnp.dot(rows[:VECS].astype(BF16), u_ref[...], preferred_element_type=F32)
     count = near_count_ref[0, 0]
     for slot in range(near_ref.shape[0]):
@@ -253,15 +279,12 @@
         source = jnp.where(slot < count, source, jnp.zeros_like(source))
         image = image + rows_dot(source, near_ref[slot])
     image_ref[...] = image
-    packed = product_lanes(window_ref[...], image)
+    packed = product_lanes(window_ref[...], image, PIECE)
     parts = [part.astype(F32) for part in three_parts(image)]
-    pieces = skeleton_of(parts, v_ref[...].astype(F32))
-    skeleton = pieces[0] + pieces[1] + pieces[2]
-    coarse = precise_dot(skeleton, transfer_ref[...])
-    room = LANES - 2 * rank
-    packed = framed(PIECE, packed, room - PIECE - packed.shape[1])
-    tree_tail = jnp.concatenate([packed, skeleton, skeleton], axis=1)
-    level_tail = jnp.concatenate([packed, coarse, coarse], axis=1)
+    skeleton, coarse = mapped(jnp.concatenate(parts, axis=0).astype(BF16), maps_ref)
+    kept = lanes_of((VECS, LANES)) < LANES - 2 * rank
+    tree_tail = jnp.where(kept, packed, skeleton)
+    level_tail = jnp.where(kept, packed, coarse)
     narrow = lanes_of((VECS, LANES))
     from_low = narrow < PIECE
     from_high = (narrow >= 3 * PIECE) & (narrow < 4 * PIECE)
@@ -284,38 +307,48 @@
     over_slots(total, store)
 
 
-def orthogonalized(total, window, image):
-    basis = window.shape[0]
-    projection = total[:, :basis]
-    square = total[:, basis : basis + VECS]
-    inner = jnp.zeros((VECS, basis), F32)
-    remainder = image
-    at = basis + VECS
-    lane = lanes_of((1, basis))
-    for b in range(basis):
-        column = projection[:, b : b + 1]
-        group = at + basis * (b // VECS)
-        metric_row = total[b % VECS : b % VECS + 1, group : group + basis]
-        metric_row = metric_row - jnp.where(lane == b, 2.0, 0.0)
-        inner = inner + column * metric_row
-        remainder = remainder - column * window[b : b + 1]
+def orthogonalized(total, at, windows, images):
+    basis = windows[0].shape[0]
+
+    def column_of(lane):
+        return replicated(total[:, lane : lane + 1])
+
+    projection = [column_of(at + b) for b in range(basis)]
+    square = [column_of(at + basis + u) for u in range(VECS)]
+    start = at + basis + VECS
+    inner = []
+    for other in range(basis):
+        value = -2.0 * projection[other]
+        for group in range(basis // VECS):
+            metric = column_of(start + group * basis + other)
+            for v in range(VECS):
+                value = value + projection[group * VECS + v] * metric[v : v + 1]
+        inner.append(value)
     columns = []
     for u in range(VECS):
-        cross = jnp.sum(inner * projection[u : u + 1], axis=1, keepdims=True)
-        columns.append(square[:, u : u + 1] + cross)
-    row = lax.broadcasted_iota(jnp.int32, (VECS, 1), 0)
-    factor = []
+        value = square[u]
+        for b in range(basis):
+            value = value + inner[b] * projection[b][u : u + 1]
+        columns.append(value)
+    remainders = []
+    for window, image in zip(windows, images):
+        for b in range(basis):
+            image = image - projection[b] * window[b : b + 1]
+        remainders.append(image)
+    row = lax.broadcasted_iota(jnp.int32, (VECS, LANES), 0)
+    lane = lanes_of((VECS, LANES))
+    record = total if at == 0 else pltpu.roll(total, LANES - at, 1)
     for j in range(VECS):
-        root = jnp.sqrt(columns[j][j : j + 1])
-        scale = 1.0 / root
+        pivot = columns[j][j : j + 1]
+        scale = lax.rsqrt(pivot)
         lower = jnp.where(row > j, columns[j] * scale, 0.0)
-        factor.append(jnp.where(row == j, root, lower))
+        record = jnp.where(lane == basis + j, jnp.where(row == j, pivot * scale, lower), record)
         for u in range(j + 1, VECS):
             columns[u] = columns[u] - lower * lower[u : u + 1]
-        solved = remainder[j : j + 1] * scale
-        remainder = jnp.where(row == j, solved, remainder - lower * solved)
-    record = jnp.concatenate([projection] + factor, axis=1)
-    return remainder, record
+        for t, remainder in enumerate(remainders):
+            solved = remainder[j : j + 1] * scale
+            remainders[t] = jnp.where(row == j, solved, remainder - lower * solved)
+    return remainders, record
 
 
 def middle_kernel(
@@ -331,8 +364,7 @@
     weights_ref,
     near_ref,
     u_ref,
-    v_ref,
-    transfer_ref,
+    maps_ref,
     slots_ref,
     next_window_ref,
     near_part_ref,
@@ -342,7 +374,7 @@
     own_leaf = lax.axis_index("clus")
     window = window_ref[...]
     basis, size = window.shape
-    rank = v_ref.shape[0]
+    rank = u_ref.shape[0]
     lane = lanes_of((VECS, LANES))
     group = lane // PIECE
     turns = LANES // PIECE
@@ -366,15 +398,13 @@
             tile_count * turns, slots, lambda at, held: held + arrived_ref[at, :, size:], total
         )
     high_tiles = [pltpu.roll(tile, LANES - 3 * PIECE, 1) for tile in high_tiles]
-    total = total[:, PIECE : LANES - 2 * rank] * (1.0 / rows_all)
+    total = total * (1.0 / rows_all)
 
     def rows_from(tiles):
         per_row = size // LANES
-        rows = [
-            jnp.concatenate(tiles[at : at + per_row], axis=1)
-            for at in range(0, tile_count, per_row)
+        return [
+            jnp.concatenate(tiles[at::per_row], axis=0) for at in range(per_row)
         ]
-        return jnp.concatenate(rows, axis=0)
 
     leaves = slots // trees
     low_place = jnp.maximum(own_leaf - 1, 0) * trees + own_tree
@@ -386,21 +416,25 @@
     wide_lane = lanes_of(tails.shape) % LANES
     tails = jnp.where(wide_lane >= LANES - 2 * rank, tails, 0.0)
     coupled = couple(tails, weights_ref)
-    images = jnp.concatenate(
-        [
-            arrived_ref[low_place, :, :size],
-            image_ref[...],
-            arrived_ref[high_place, :, :size],
-            coupled,
-        ],
-        axis=1,
-    )
-    windows = jnp.concatenate(
-        [rows_from(low_tiles), window, rows_from(high_tiles), window_coupled_ref[...]], axis=1
-    )
-    solved, record = orthogonalized(total, windows, images)
+    images = [
+        *lane_tiles(arrived_ref[low_place, :, :size]),
+        *lane_tiles(image_ref[...]),
+        *lane_tiles(arrived_ref[high_place, :, :size]),
+        jnp.concatenate([coupled, jnp.zeros((VECS, LANES - rank), F32)], axis=1),
+    ]
+    windows = [
+        *rows_from(low_tiles),
+        *lane_tiles(window),
+        *rows_from(high_tiles),
+        window_coupled_ref[...],
+    ]
+    solved, record = orthogonalized(total, PIECE, windows, images)
     record_ref[...] = record
-    low_block, new_block, high_block = (solved[:, at : at + size] for at in range(0, 3 * size, size))
+    per_row = size // LANES
+    low_block, new_block, high_block = (
+        jnp.concatenate(solved[at : at + per_row], axis=1)
+        for at in range(0, 3 * per_row, per_row)
+    )
     next_window = jnp.concatenate([window[VECS:], new_block], axis=0)
     next_window_ref[...] = next_window
     count = near_count_ref[0, 0]
@@ -412,15 +446,12 @@
         near_part = near_part + rows_dot(source, near_ref[slot])
     near_part_ref[...] = near_part
     far_part = jnp.dot(
-        solved[:, 3 * size :].astype(BF16), u_ref[...], preferred_element_type=F32
-    )
-    skeleton = rows_dot(new_block.astype(BF16), v_ref[...])
-    coarse = precise_dot(skeleton, transfer_ref[...])
-    packed = product_lanes(next_window, near_part + far_part)
-    packed = framed(0, packed, rank - packed.shape[1])
-    copies = LANES // rank - 1
-    tree_tail = jnp.concatenate([packed] + [skeleton] * copies, axis=1)
-    level_tail = jnp.concatenate([packed] + [coarse] * copies, axis=1)
+        solved[-1][:, :rank].astype(BF16), u_ref[...], preferred_element_type=F32
+    )
+    skeleton, coarse = mapped(new_block.astype(BF16), maps_ref)
+    packed = product_lanes(next_window, near_part + far_part, 0)
+    tree_tail = jnp.where(lane < rank, packed, skeleton)
+    level_tail = jnp.where(lane < rank, packed, coarse)
 
     def store(slot, at):
         slots_ref[slot] = level_tail
@@ -460,11 +491,13 @@
         total = total + arrived_ref[slot]
     if slots > near:
         total = lax.fori_loop(near, slots, lambda at, held: held + arrived_ref[at], total)
-    total = total[:, :rank] * (1.0 / rows_all)
-    new_block, record = orthogonalized(total, window_ref[...], near_part_ref[...] + far_part)
-    store_rows(block_ref, new_block)
-    records_ref[0] = first_ref[...]
-    records_ref[1] = record
+    total = total * (1.0 / rows_all)
+    image = near_part_ref[...] + far_part
+    solved, record = orthogonalized(total, 0, lane_tiles(window_ref[...]), lane_tiles(image))
+    store_rows(block_ref, jnp.concatenate(solved, axis=1))
+    used = records_ref.shape[2]
+    records_ref[0] = first_ref[:, :used]
+    records_ref[1] = record[:, :used]
 
 
 def call(kernel, name, outs, ins, places, scratch=(), vmem=16 << 20, bytes_accessed=1 << 20):
@@ -507,7 +540,8 @@
     far_own, top_own, near_own = far_coupling[0, 0], top_coupling[0, 0], near_block[0, 0]
     image_like = ((VECS, size), F32)
     window_like = ((basis, size), F32)
-    record_like = ((VECS, basis + VECS), F32)
+    record_like = ((VECS, LANES), F32)
+    maps_like = ((4 * LANES, size), BF16)
     weights_like = ((3, rank, (far_own.shape[0] + trees) * LANES), BF16)
     slots, window = call(
         functools.partial(begin_kernel, trees),
@@ -524,18 +558,18 @@
         vmem=None,
     )
     arrived = exchange(slots)
-    weights, near_here = call(
+    weights, near_here, maps = call(
         prepare_kernel,
         "prepare",
-        [weights_like, (near_own.shape, BF16)],
-        [near_col, near_count, far_col, near_own, far_own, transfer_own, top_own],
-        "ssshvvv",
+        [weights_like, (near_own.shape, BF16), maps_like],
+        [near_col, near_count, far_col, near_own, far_own, v_own, transfer_own, top_own],
+        "ssshvvvv",
         [pltpu.SemaphoreType.DMA],
     )
     image, slots, window_coupled = call(
         functools.partial(first_kernel, trees),
         "first",
-        [image_like, ((devices, VECS, size + LANES), F32), ((basis, rank), F32)],
+        [image_like, ((devices, VECS, size + LANES), F32), ((basis, LANES), F32)],
         [
             near_col,
             near_count,
@@ -545,10 +579,9 @@
             weights,
             near_here,
             u_own,
-            v_own,
-            transfer_own,
+            maps,
         ],
-        "sssvvvvvvv",
+        "sssvvvvvv",
     )
     arrived = exchange(slots)
     slots, window, near_part, record = call(
@@ -566,16 +599,15 @@
             weights,
             near_here,
             u_own,
-            v_own,
-            transfer_own,
+            maps,
         ],
-        "sssvvvvvvvvv",
+        "sssvvvvvvvv",
     )
     arrived = exchange(slots)
     block, records = call(
         functools.partial(end_kernel, trees, rows_all),
         "end",
-        [((VECS * size // LANES, LANES), F32), ((STEPS,) + record_like[0], F32)],
+        [((VECS * size // LANES, LANES), F32), ((STEPS, VECS, basis + VECS), F32)],
         [far_col, arrived, window, near_part, weights, u_own, record],
         "svvvvvv",
     )

time: 44.3 us -> 43.1 us (0.973)
  Pallas kernels: 7.9 us -> 6.64 us
    pallas_call x5, Pallas kernels: 7.9 us -> 6.64 us  [call(): pl.pallas_call(kernel, name=name, out_shape=[jax.ShapeDtypeStruct(shape,...]
where the time goes in v4:
time: 43.1 us; the launch traced here: 42.6 us
  blocking collectives  20.5 us (48%)
  starting transfers between devices  7.33 us (17%)
  Pallas kernels  6.64 us (15%)
  waiting for transfers between devices  5.1 us (12%)
  local copies, waits for them, and re-layouts  1.69 us (4%)
  between operations  1.41 us (3%)
    all_to_all x2, blocking collectives, exchange(): return lax.all_to_all(slots, AXES, 0, 0, tiled=True)  20.5 us
    all_to_all x1, starting transfers between devices, exchange(): return lax.all_to_all(slots, AXES, 0, 0, tiled=True)  7.33 us
    pallas_call x5, Pallas kernels, call(): pl.pallas_call(kernel, name=name, out_shape=[jax.ShapeDtypeStruct(shape,...  6.64 us
    all_to_all x1, waiting for transfers between devices, exchange(): return lax.all_to_all(slots, AXES, 0, 0, tiled=True)  5.1 us
    unnamed x18, local copies, waits for them, and re-layouts  1.69 us
  transfers between devices with their start and end apart: 1, of which 1 were waited for; matrix products, arithmetic and copies ran while one was open for 0% of the time, Pallas kernels for 2%

profile of v4, /device:TPU:0, one launch (start us, length us, event | category | flops | bytes accessed | tf_op | source)
XLA Modules:
  0.0 42.6 jit_solution(144682788307451304)
XLA Ops:
  0.6 1.8 %begin.1 = (bf16[32,4,512]{2,1,0:T(4,128)(2,1)}, f32[8,256]{1,0:T(8,128)}) custom-call(f32[16,128]{1,0:T(8,128)} %bitcast.19, bf16[32,256]{1,0:T(8,128)(2,1)} %bitcast.15, f32[32,32]{1,0:T(8,128)} %bitcast.17), custom_call_target="tpu_custom_call" | custom-call | bytes 1048576 | tf_op jit(solution)/shard_map/begin/pallas_call | solution.py:505
  2.4 0.0 copy-start.2
  2.4 0.0 copy-start.3
  2.4 0.0 copy-start.4
  2.4 0.0 copy-start.5
  2.5 7.3 %all-to-all-start = ((bf16[32,4,512]{2,1,0:T(4,128)(2,1)}), bf16[32,4,512]{2,1,0:T(4,128)(2,1)S(1)}, u32[]{:S(2)}, u32[]{:S(2)}) async-start(bf16[32,4,512]{2,1,0:T(4,128)(2,1)} %get-tuple-element.16), calls=%async_computation | async-start | bytes 262144 | tf_op jit(solution)/shard_map/all_to_all | solution.py:518
  10.4 0.0 copy-start.7
  10.5 0.0 copy-start.8
  10.5 0.0 copy-done.2
  10.5 0.0 copy-done.3
  10.5 0.0 copy-done.4
  10.5 0.0 copy-done.5
  10.5 0.6 %copy-done.7 = s32[1,1,6]{2,1,0:T(1,128)S(1)} copy-done((s32[1,1,6]{2,1,0:T(1,128)S(1)}, s32[1,1,6]{2,1,0:T(1,128)}, u32[]{:S(2)}) %copy-start.7) | copy-done | bytes 48
  11.1 0.0 copy-done.8
  11.1 0.0 copy-start
  11.1 1.0 %copy-done = bf16[1,1,4,256,256]{4,3,2,1,0:T(8,128)(2,1)S(1)} copy-done((bf16[1,1,4,256,256]{4,3,2,1,0:T(8,128)(2,1)S(1)}, bf16[1,1,4,256,256]{4,3,2,1,0:T(8,128)(2,1)}, u32[]{:S(2)}) %copy-start) | copy-done | bytes 524312
  12.2 0.0 copy-start.1
  12.2 0.9 %prepare.1 = (bf16[3,32,1280]{2,1,0:T(8,128)(2,1)S(1)}, bf16[4,256,256]{2,1,0:T(8,128)(2,1)S(1)}, bf16[512,256]{1,0:T(8,128)(2,1)S(1)}) custom-call(s32[1,1,4]{2,1,0:T(1,128)S(1)} %copy-done.8, s32[1,1]{1,0:T(1,128)S(6)} %copy.13.near_count_ref, s32[1,1,6]{2,1,0:T(1,128)S(1)} %copy-done.7, bf16[4,256,256]{2,1,0:T(8,128)(2,1)S(1)} %bitcast.9, ...), custom_call_target="tpu_custom_call" | custom-call | bytes 1048576 | tf_op jit(solution)/shard_map/prepare/pallas_call | solution.py:505
  13.1 0.0 copy-start.6
  13.1 5.1 %all-to-all-done.arrived_ref = bf16[32,4,512]{2,1,0:T(4,128)(2,1)S(1)} async-done(((bf16[32,4,512]{2,1,0:T(4,128)(2,1)}), bf16[32,4,512]{2,1,0:T(4,128)(2,1)S(1)}, u32[]{:S(2)}, u32[]{:S(2)}) %all-to-all-start) | async-done | bytes 131104 | tf_op jit(solution)/shard_map/all_to_all | solution.py:518
  18.2 0.0 copy-done.1
  18.2 0.0 copy-done.6
  18.2 1.1 %first.1 = (f32[4,256]{1,0:T(4,128)S(1)}, f32[32,4,384]{2,1,0:T(4,128)S(1)}, f32[8,128]{1,0:T(8,128)S(1)}) custom-call(s32[1,1,4]{2,1,0:T(1,128)S(1)} %copy-done.8, s32[1,1]{1,0:T(1,128)S(6)} %copy.13.near_count_ref, s32[1,1,6]{2,1,0:T(1,128)S(1)} %copy-done.7, bf16[32,4,512]{2,1,0:T(4,128)(2,1)S(1)} %all-to-all-done.arrived_ref, f32[8,256]{1,0:T(8,128)S(1)} %copy-done.6, ...), custom_call_target="tpu_custom_call" | custom-call | bytes 1048576 | tf_op jit(solution)/shard_map/first/pallas_call | solution.py:505
  19.3 11.2 %all_to_all.15.arrived_ref = f32[32,4,384]{2,1,0:T(4,128)S(1)} all-to-all(f32[32,4,384]{2,1,0:T(4,128)S(1)} %get-tuple-element.21), channel_id=1, replica_groups=mesh['clus'=8,'lvl'=4] {'clus','lvl'}, dimensions={0} | all-to-all | bytes 393216 | tf_op jit(solution)/shard_map/all_to_all | solution.py:518
  30.5 1.3 %middle.1 = (f32[32,4,128]{2,1,0:T(4,128)S(1)}, f32[8,256]{1,0:T(8,128)S(1)}, f32[4,256]{1,0:T(4,128)S(1)}, f32[4,128]{1,0:T(4,128)S(1)}) custom-call(s32[1,1,4]{2,1,0:T(1,128)S(1)} %copy-done.8, s32[1,1]{1,0:T(1,128)S(6)} %copy.13.near_count_ref, s32[1,1,6]{2,1,0:T(1,128)S(1)} %copy-done.7, f32[32,4,384]{2,1,0:T(4,128)S(1)} %all_to_all.15.arrived_ref, ...), custom_call_target="tpu_custom_call" | custom-call | bytes 1048576 | tf_op jit(solution)/shard_map/middle/pallas_call | solution.py:505
  31.8 9.3 %all_to_all.16.arrived_ref = f32[32,4,128]{2,1,0:T(4,128)S(1)} all-to-all(f32[32,4,128]{2,1,0:T(4,128)S(1)} %get-tuple-element.24), channel_id=1, replica_groups=mesh['clus'=8,'lvl'=4] {'clus','lvl'}, dimensions={0} | all-to-all | bytes 131072 | tf_op jit(solution)/shard_map/all_to_all | solution.py:518
  41.2 1.5 %end.1 = (f32[8,128]{1,0:T(8,128)}, f32[2,4,12]{2,1,0:T(4,128)}) custom-call(s32[1,1,6]{2,1,0:T(1,128)S(1)} %copy-done.7, f32[32,4,128]{2,1,0:T(4,128)S(1)} %all_to_all.16.arrived_ref, f32[8,256]{1,0:T(8,128)S(1)} %get-tuple-element.25.window_ref, f32[4,256]{1,0:T(4,128)S(1)} %get-tuple-element.26.near_part_ref, ...), custom_call_target="tpu_custom_call" | custom-call | bytes 1048576 | tf_op jit(solution)/shard_map/end/pallas_call | solution.py:505
Async XLA Ops:
  2.4 8.1 %copy-start.2 = (f32[1,1,6,32,32]{4,3,2,1,0:T(8,128)S(1)}, f32[1,1,6,32,32]{4,3,2,1,0:T(8,128)}, u32[]{:S(2)}) copy-start(f32[1,1,6,32,32]{4,3,2,1,0:T(8,128)} %param.17) | copy-start | bytes 73732
  2.4 8.1 %copy-start.3 = (f32[1,1,4,32,32]{4,3,2,1,0:T(8,128)S(1)}, f32[1,1,4,32,32]{4,3,2,1,0:T(8,128)}, u32[]{:S(2)}) copy-start(f32[1,1,4,32,32]{4,3,2,1,0:T(8,128)} %param.19) | copy-start | bytes 49156
  2.4 8.1 %copy-start.4 = (bf16[1,1,32,256]{3,2,1,0:T(8,128)(2,1)S(1)}, bf16[1,1,32,256]{3,2,1,0:T(8,128)(2,1)}, u32[]{:S(2)}) copy-start(bf16[1,1,32,256]{3,2,1,0:T(8,128)(2,1)} %param.15) | copy-start | bytes 49156
  2.4 8.1 %copy-start.5 = (f32[1,1,32,32]{3,2,1,0:T(8,128)S(1)}, f32[1,1,32,32]{3,2,1,0:T(8,128)}, u32[]{:S(2)}) copy-start(f32[1,1,32,32]{3,2,1,0:T(8,128)} %param.18) | copy-start | bytes 12292
  2.5 15.7 %all-to-all-start = ((bf16[32,4,512]{2,1,0:T(4,128)(2,1)}), bf16[32,4,512]{2,1,0:T(4,128)(2,1)S(1)}, u32[]{:S(2)}, u32[]{:S(2)}) async-start(bf16[32,4,512]{2,1,0:T(4,128)(2,1)} %get-tuple-element.16), calls=%async_computation | async-start | bytes 262144 | tf_op jit(solution)/shard_map/all_to_all | solution.py:518
  10.4 0.7 %copy-start.7 = (s32[1,1,6]{2,1,0:T(1,128)S(1)}, s32[1,1,6]{2,1,0:T(1,128)}, u32[]{:S(2)}) copy-start(s32[1,1,6]{2,1,0:T(1,128)} %far_col_ref.7) | copy-start | bytes 76
  10.5 0.7 %copy-start.8 = (s32[1,1,4]{2,1,0:T(1,128)S(1)}, s32[1,1,4]{2,1,0:T(1,128)}, u32[]{:S(2)}) copy-start(s32[1,1,4]{2,1,0:T(1,128)} %near_col_ref.5) | copy-start | bytes 52
  11.1 1.0 %copy-start = (bf16[1,1,4,256,256]{4,3,2,1,0:T(8,128)(2,1)S(1)}, bf16[1,1,4,256,256]{4,3,2,1,0:T(8,128)(2,1)}, u32[]{:S(2)}) copy-start(bf16[1,1,4,256,256]{4,3,2,1,0:T(8,128)(2,1)} %param.11) | copy-start | bytes 1572868
  12.2 6.0 %copy-start.1 = (bf16[1,1,32,256]{3,2,1,0:T(8,128)(2,1)S(1)}, bf16[1,1,32,256]{3,2,1,0:T(8,128)(2,1)}, u32[]{:S(2)}) copy-start(bf16[1,1,32,256]{3,2,1,0:T(8,128)(2,1)} %param.16) | copy-start | bytes 49156
  13.1 5.1 %copy-start.6 = (f32[8,256]{1,0:T(8,128)S(1)}, f32[8,256]{1,0:T(8,128)}, u32[]{:S(2)}) copy-start(f32[8,256]{1,0:T(8,128)} %get-tuple-element.17.window_ref) | copy-start | bytes 24580

commit v5 on v4

--- a/solution.py
+++ b/solution.py
@@ -167,6 +167,7 @@
 
 
 def prepare_kernel(
+    leaves,
     near_col_ref,
     near_count_ref,
     far_col_ref,
@@ -178,6 +179,7 @@
     weights_ref,
     near_ref,
     maps_ref,
+    choice_ref,
     sem,
 ):
     copy = pltpu.make_async_copy(near_hbm, near_ref, sem)
@@ -186,11 +188,13 @@
     far_slots = far_coupling_ref.shape[0]
     trees, rank = top_ref.shape[0], top_ref.shape[1]
     transfer = transfer_ref[...]
-    for slot in range(far_slots + trees):
-        if slot < far_slots:
-            block = far_coupling_ref[slot]
+    for slot in range(leaves + trees):
+        if slot < leaves:
+            block = jnp.zeros((rank, rank), F32)
+            for at in range(far_slots):
+                block = block + jnp.where(far_col_ref[0, 0, at] == slot, far_coupling_ref[at], 0.0)
         else:
-            tree = slot - far_slots
+            tree = slot - leaves
             block = precise_dot(transfer, jnp.where(tree != own_tree, top_ref[tree], 0.0))
         wide = jnp.concatenate([block] * (LANES // rank), axis=1)
         for part, piece in enumerate(three_parts(wide)):
@@ -200,14 +204,43 @@
     for part, piece in enumerate((v_basis, *three_parts(carried))):
         for at in range(part * LANES, (part + 1) * LANES, rank):
             maps_ref[at : at + rank] = piece
+    own_leaf = lax.axis_index("clus")
+    count = near_count_ref[0, 0]
+    rows = lax.broadcasted_iota(jnp.int32, choice_ref.shape, 0)
+    choice = jnp.zeros(choice_ref.shape, F32)
+    for slot in range(near_ref.shape[0]):
+        for side in range(3):
+            wanted = (near_col_ref[0, 0, slot] == own_leaf + side - 1) & (slot < count)
+            choice = jnp.where(rows == 3 * slot + side, jnp.where(wanted, 1.0, 0.0), choice)
+    choice_ref[...] = choice
     copy.wait()
 
 
-def sources_of(far_col_ref, trees):
+def places_of(leaves, trees):
     own_tree = lax.axis_index("lvl")
     own_leaf = lax.axis_index("clus")
-    places = [far_col_ref[0, 0, slot] * trees + own_tree for slot in range(far_col_ref.shape[2])]
+    places = [leaf * trees + own_tree for leaf in range(leaves)]
     return places + [own_leaf * trees + tree for tree in range(trees)]
+
+
+def near_places(leaves, trees):
+    own_tree = lax.axis_index("lvl")
+    own_leaf = lax.axis_index("clus")
+    low = jnp.maximum(own_leaf - 1, 0)
+    high = jnp.minimum(own_leaf + 1, leaves - 1)
+    return [leaf * trees + own_tree for leaf in (low, own_leaf, high)]
+
+
+def near_field(blocks, choice_ref, near_ref):
+    choice = choice_ref[...]
+    blocks = [[tile.astype(F32) for tile in lane_tiles(block)] for block in blocks]
+    result = None
+    for slot in range(near_ref.shape[0]):
+        rows = [choice[3 * slot + side : 3 * slot + side + 1] for side in range(3)]
+        tiles = [sum(tile * row for tile, row in zip(sides, rows)) for sides in zip(*blocks)]
+        part = rows_dot(jnp.concatenate(tiles, axis=1).astype(BF16), near_ref[slot])
+        result = part if result is None else result + part
+    return result
 
 
 def couple(values, weights_ref):
@@ -244,13 +277,11 @@
 
 def first_kernel(
     trees,
-    near_col_ref,
-    near_count_ref,
-    far_col_ref,
     arrived_ref,
     window_ref,
     weights_ref,
     near_ref,
+    choice_ref,
     u_ref,
     maps_ref,
     image_ref,
@@ -260,7 +291,8 @@
     own_tree = lax.axis_index("lvl")
     size = near_ref.shape[1]
     rank = u_ref.shape[0]
-    places = sources_of(far_col_ref, trees)
+    leaves = arrived_ref.shape[0] // trees
+    places = places_of(leaves, trees)
     first = [arrived_ref[place, :, size : size + LANES] for place in places]
     second = [arrived_ref[place, :, size + LANES :] for place in places]
     first = jnp.concatenate(first, axis=1).astype(F32)
@@ -273,11 +305,8 @@
     blank = jnp.zeros((2 * VECS, LANES - rank), F32)
     window_coupled_ref[...] = jnp.concatenate([linear, blank], axis=1)
     image = jnp.dot(rows[:VECS].astype(BF16), u_ref[...], preferred_element_type=F32)
-    count = near_count_ref[0, 0]
-    for slot in range(near_ref.shape[0]):
-        source = arrived_ref[near_col_ref[0, 0, slot] * trees + own_tree, :, :size]
-        source = jnp.where(slot < count, source, jnp.zeros_like(source))
-        image = image + rows_dot(source, near_ref[slot])
+    blocks = [arrived_ref[place, :, :size] for place in near_places(leaves, trees)]
+    image = image + near_field(blocks, choice_ref, near_ref)
     image_ref[...] = image
     packed = product_lanes(window_ref[...], image, PIECE)
     parts = [part.astype(F32) for part in three_parts(image)]
@@ -354,15 +383,13 @@
 def middle_kernel(
     trees,
     rows_all,
-    near_col_ref,
-    near_count_ref,
-    far_col_ref,
     arrived_ref,
     window_ref,
     image_ref,
     window_coupled_ref,
     weights_ref,
     near_ref,
+    choice_ref,
     u_ref,
     maps_ref,
     slots_ref,
@@ -371,7 +398,6 @@
     record_ref,
 ):
     own_tree = lax.axis_index("lvl")
-    own_leaf = lax.axis_index("clus")
     window = window_ref[...]
     basis, size = window.shape
     rank = u_ref.shape[0]
@@ -407,10 +433,9 @@
         ]
 
     leaves = slots // trees
-    low_place = jnp.maximum(own_leaf - 1, 0) * trees + own_tree
-    high_place = jnp.minimum(own_leaf + 1, leaves - 1) * trees + own_tree
+    low_place, _, high_place = near_places(leaves, trees)
     tails = jnp.concatenate(
-        [arrived_ref[place, :, size:] for place in sources_of(far_col_ref, trees)], axis=1
+        [arrived_ref[place, :, size:] for place in places_of(leaves, trees)], axis=1
     )
     tails = lane_parts(tails, lanes_of(tails.shape) % LANES // rank - (LANES // rank - 2))
     wide_lane = lanes_of(tails.shape) % LANES
@@ -437,13 +462,8 @@
     )
     next_window = jnp.concatenate([window[VECS:], new_block], axis=0)
     next_window_ref[...] = next_window
-    count = near_count_ref[0, 0]
-    near_part = jnp.zeros((VECS, size), F32)
-    for slot in range(near_ref.shape[0]):
-        leaf = near_col_ref[0, 0, slot]
-        source = jnp.where(leaf < own_leaf, low_block, jnp.where(leaf > own_leaf, high_block, new_block))
-        source = jnp.where(slot < count, source, 0.0).astype(BF16)
-        near_part = near_part + rows_dot(source, near_ref[slot])
+    blocks = [block.astype(BF16) for block in (low_block, new_block, high_block)]
+    near_part = near_field(blocks, choice_ref, near_ref)
     near_part_ref[...] = near_part
     far_part = jnp.dot(
         solved[-1][:, :rank].astype(BF16), u_ref[...], preferred_element_type=F32
@@ -467,7 +487,6 @@
 def end_kernel(
     trees,
     rows_all,
-    far_col_ref,
     arrived_ref,
     window_ref,
     near_part_ref,
@@ -478,8 +497,9 @@
     records_ref,
 ):
     rank = u_ref.shape[0]
+    leaves = arrived_ref.shape[0] // trees
     tails = jnp.concatenate(
-        [arrived_ref[place] for place in sources_of(far_col_ref, trees)], axis=1
+        [arrived_ref[place] for place in places_of(leaves, trees)], axis=1
     )
     part = lanes_of(tails.shape) % LANES // rank - 1
     coupled = couple(jnp.where(part >= 0, lane_parts(tails, part), 0.0), weights_ref)
@@ -532,7 +552,8 @@
 ):
     basis, _, size = krylov_basis.shape
     trees = lax.axis_size("lvl")
-    devices = lax.axis_size("clus") * trees
+    leaves = lax.axis_size("clus")
+    devices = leaves * trees
     rows_all = float(devices * size)
     flat_basis = krylov_basis.reshape(-1, LANES)
     v_own, u_own, transfer_own = v_basis[0, 0], u_basis[0, 0], transfer[0, 0]
@@ -542,7 +563,8 @@
     window_like = ((basis, size), F32)
     record_like = ((VECS, LANES), F32)
     maps_like = ((4 * LANES, size), BF16)
-    weights_like = ((3, rank, (far_own.shape[0] + trees) * LANES), BF16)
+    choice_like = ((-(-3 * near_own.shape[0] // 8) * 8, LANES), F32)
+    weights_like = ((3, rank, (leaves + trees) * LANES), BF16)
     slots, window = call(
         functools.partial(begin_kernel, trees),
         "begin",
@@ -558,10 +580,10 @@
         vmem=None,
     )
     arrived = exchange(slots)
-    weights, near_here, maps = call(
-        prepare_kernel,
+    weights, near_here, maps, choice = call(
+        functools.partial(prepare_kernel, leaves),
         "prepare",
-        [weights_like, (near_own.shape, BF16), maps_like],
+        [weights_like, (near_own.shape, BF16), maps_like, choice_like],
         [near_col, near_count, far_col, near_own, far_own, v_own, transfer_own, top_own],
         "ssshvvvv",
         [pltpu.SemaphoreType.DMA],
@@ -571,17 +593,15 @@
         "first",
         [image_like, ((devices, VECS, size + LANES), F32), ((basis, LANES), F32)],
         [
-            near_col,
-            near_count,
-            far_col,
             arrived,
             window,
             weights,
             near_here,
+            choice,
             u_own,
             maps,
         ],
-        "sssvvvvvv",
+        "v" * 7,
     )
     arrived = exchange(slots)
     slots, window, near_part, record = call(
@@ -589,27 +609,25 @@
         "middle",
         [((devices, VECS, LANES), F32), window_like, image_like, record_like],
         [
-            near_col,
-            near_count,
-            far_col,
             arrived,
             window,
             image,
             window_coupled,
             weights,
             near_here,
+            choice,
             u_own,
             maps,
         ],
-        "sssvvvvvvvv",
+        "v" * 9,
     )
     arrived = exchange(slots)
     block, records = call(
         functools.partial(end_kernel, trees, rows_all),
         "end",
         [((VECS * size // LANES, LANES), F32), ((STEPS, VECS, basis + VECS), F32)],
-        [far_col, arrived, window, near_part, weights, u_own, record],
-        "svvvvvv",
+        [arrived, window, near_part, weights, u_own, record],
+        "v" * 6,
     )
     return (block.reshape(VECS, 1, size), jnp.transpose(records, (0, 2, 1)))
 

time: 43.1 us -> 41.5 us (0.963)
  Pallas kernels: 6.64 us -> 5.08 us
    pallas_call x5, Pallas kernels: 6.64 us -> 5.08 us  [call(): pl.pallas_call(kernel, name=name, out_shape=[jax.ShapeDtypeStruct(shape,...]
where the time goes in v5:
time: 41.5 us; the launch traced here: 41.1 us
  blocking collectives  20.5 us (49%)
  starting transfers between devices  7.33 us (18%)
  waiting for transfers between devices  5.09 us (12%)
  Pallas kernels  5.08 us (12%)
  local copies, waits for them, and re-layouts  1.69 us (4%)
  between operations  1.41 us (3%)
    all_to_all x2, blocking collectives, exchange(): return lax.all_to_all(slots, AXES, 0, 0, tiled=True)  20.5 us
    all_to_all x1, starting transfers between devices, exchange(): return lax.all_to_all(slots, AXES, 0, 0, tiled=True)  7.33 us
    all_to_all x1, waiting for transfers between devices, exchange(): return lax.all_to_all(slots, AXES, 0, 0, tiled=True)  5.09 us
    pallas_call x5, Pallas kernels, call(): pl.pallas_call(kernel, name=name, out_shape=[jax.ShapeDtypeStruct(shape,...  5.08 us
    unnamed x18, local copies, waits for them, and re-layouts  1.69 us
  transfers between devices with their start and end apart: 1, of which 1 were waited for; matrix products, arithmetic and copies ran while one was open for 0% of the time, Pallas kernels for 2%

profile of v5, /device:TPU:0, one launch (start us, length us, event | category | flops | bytes accessed | tf_op | source)
XLA Modules:
  0.0 41.1 jit_solution(12101185667654195633)
XLA Ops:
  0.6 1.8 %begin.1 = (bf16[32,4,512]{2,1,0:T(4,128)(2,1)}, f32[8,256]{1,0:T(8,128)}) custom-call(f32[16,128]{1,0:T(8,128)} %bitcast.19, bf16[32,256]{1,0:T(8,128)(2,1)} %bitcast.15, f32[32,32]{1,0:T(8,128)} %bitcast.17), custom_call_target="tpu_custom_call" | custom-call | bytes 1048576 | tf_op jit(solution)/shard_map/begin/pallas_call | solution.py:525
  2.4 0.0 copy-start.2
  2.4 0.0 copy-start.3
  2.4 0.0 copy-start.4
  2.4 0.0 copy-start.5
  2.5 7.3 %all-to-all-start = ((bf16[32,4,512]{2,1,0:T(4,128)(2,1)}), bf16[32,4,512]{2,1,0:T(4,128)(2,1)S(1)}, u32[]{:S(2)}, u32[]{:S(2)}) async-start(bf16[32,4,512]{2,1,0:T(4,128)(2,1)} %get-tuple-element.17), calls=%async_computation | async-start | bytes 262144 | tf_op jit(solution)/shard_map/all_to_all | solution.py:538
  10.4 0.0 copy-start.7
  10.5 0.0 copy-start.8
  10.5 0.0 copy-done.2
  10.5 0.0 copy-done.3
  10.5 0.0 copy-done.4
  10.5 0.0 copy-done.5
  10.5 0.6 %copy-done.7 = s32[1,1,4]{2,1,0:T(1,128)S(1)} copy-done((s32[1,1,4]{2,1,0:T(1,128)S(1)}, s32[1,1,4]{2,1,0:T(1,128)}, u32[]{:S(2)}) %copy-start.7) | copy-done | bytes 40
  11.1 0.0 copy-done.8
  11.1 0.0 copy-start
  11.1 1.0 %copy-done = bf16[1,1,4,256,256]{4,3,2,1,0:T(8,128)(2,1)S(1)} copy-done((bf16[1,1,4,256,256]{4,3,2,1,0:T(8,128)(2,1)S(1)}, bf16[1,1,4,256,256]{4,3,2,1,0:T(8,128)(2,1)}, u32[]{:S(2)}) %copy-start) | copy-done | bytes 524312
  12.2 0.0 copy-start.1
  12.2 0.9 %prepare.1 = (bf16[3,32,1536]{2,1,0:T(8,128)(2,1)S(1)}, bf16[4,256,256]{2,1,0:T(8,128)(2,1)S(1)}, bf16[512,256]{1,0:T(8,128)(2,1)S(1)}, f32[16,128]{1,0:T(8,128)S(1)}) custom-call(s32[1,1,4]{2,1,0:T(1,128)S(1)} %copy-done.7, s32[1,1]{1,0:T(1,128)S(6)} %copy.13.near_count_ref, s32[1,1,6]{2,1,0:T(1,128)S(1)} %copy-done.8, bf16[4,256,256]{2,1,0:T(8,128)(2,1)S(1)} %bitcast.9, ...), custom_call_target="tpu_custom_call" | custom-call | bytes 1048576 | tf_op jit(solution)/shard_map/prepare/pallas_call | solution.py:525
  13.1 0.0 copy-start.6
  13.1 5.1 %all-to-all-done.arrived_ref = bf16[32,4,512]{2,1,0:T(4,128)(2,1)S(1)} async-done(((bf16[32,4,512]{2,1,0:T(4,128)(2,1)}), bf16[32,4,512]{2,1,0:T(4,128)(2,1)S(1)}, u32[]{:S(2)}, u32[]{:S(2)}) %all-to-all-start) | async-done | bytes 131104 | tf_op jit(solution)/shard_map/all_to_all | solution.py:538
  18.2 0.0 copy-done.1
  18.2 0.0 copy-done.6
  18.2 0.6 %first.1 = (f32[4,256]{1,0:T(4,128)S(1)}, f32[32,4,384]{2,1,0:T(4,128)S(1)}, f32[8,128]{1,0:T(8,128)S(1)}) custom-call(bf16[32,4,512]{2,1,0:T(4,128)(2,1)S(1)} %all-to-all-done.arrived_ref, f32[8,256]{1,0:T(8,128)S(1)} %copy-done.6, bf16[3,32,1536]{2,1,0:T(8,128)(2,1)S(1)} %get-tuple-element.19.weights_ref, ...), custom_call_target="tpu_custom_call" | custom-call | bytes 1048576 | tf_op jit(solution)/shard_map/first/pallas_call | solution.py:525
  18.8 11.2 %all_to_all.15.arrived_ref = f32[32,4,384]{2,1,0:T(4,128)S(1)} all-to-all(f32[32,4,384]{2,1,0:T(4,128)S(1)} %get-tuple-element.23), channel_id=1, replica_groups=mesh['clus'=8,'lvl'=4] {'clus','lvl'}, dimensions={0} | all-to-all | bytes 393216 | tf_op jit(solution)/shard_map/all_to_all | solution.py:538
  30.0 0.8 %middle.1 = (f32[32,4,128]{2,1,0:T(4,128)S(1)}, f32[8,256]{1,0:T(8,128)S(1)}, f32[4,256]{1,0:T(4,128)S(1)}, f32[4,128]{1,0:T(4,128)S(1)}) custom-call(f32[32,4,384]{2,1,0:T(4,128)S(1)} %all_to_all.15.arrived_ref, f32[8,256]{1,0:T(8,128)S(1)} %copy-done.6, f32[4,256]{1,0:T(4,128)S(1)} %get-tuple-element.24.image_ref, ...), custom_call_target="tpu_custom_call" | custom-call | bytes 1048576 | tf_op jit(solution)/shard_map/middle/pallas_call | solution.py:525
  30.8 9.3 %all_to_all.16.arrived_ref = f32[32,4,128]{2,1,0:T(4,128)S(1)} all-to-all(f32[32,4,128]{2,1,0:T(4,128)S(1)} %get-tuple-element.26), channel_id=1, replica_groups=mesh['clus'=8,'lvl'=4] {'clus','lvl'}, dimensions={0} | all-to-all | bytes 131072 | tf_op jit(solution)/shard_map/all_to_all | solution.py:538
  40.1 1.0 %end.1 = (f32[8,128]{1,0:T(8,128)}, f32[2,4,12]{2,1,0:T(4,128)}) custom-call(f32[32,4,128]{2,1,0:T(4,128)S(1)} %all_to_all.16.arrived_ref, f32[8,256]{1,0:T(8,128)S(1)} %get-tuple-element.27.window_ref, f32[4,256]{1,0:T(4,128)S(1)} %get-tuple-element.28.near_part_ref, bf16[3,32,1536]{2,1,0:T(8,128)(2,1)S(1)} %get-tuple-element.19.weights_ref, ...), custom_call_target="tpu_custom_call" | custom-call | bytes 1048576 | tf_op jit(solution)/shard_map/end/pallas_call | solution.py:525
Async XLA Ops:
  2.4 8.1 %copy-start.2 = (f32[1,1,6,32,32]{4,3,2,1,0:T(8,128)S(1)}, f32[1,1,6,32,32]{4,3,2,1,0:T(8,128)}, u32[]{:S(2)}) copy-start(f32[1,1,6,32,32]{4,3,2,1,0:T(8,128)} %param.17) | copy-start | bytes 73732
  2.4 8.1 %copy-start.3 = (f32[1,1,4,32,32]{4,3,2,1,0:T(8,128)S(1)}, f32[1,1,4,32,32]{4,3,2,1,0:T(8,128)}, u32[]{:S(2)}) copy-start(f32[1,1,4,32,32]{4,3,2,1,0:T(8,128)} %param.19) | copy-start | bytes 49156
  2.4 8.1 %copy-start.4 = (bf16[1,1,32,256]{3,2,1,0:T(8,128)(2,1)S(1)}, bf16[1,1,32,256]{3,2,1,0:T(8,128)(2,1)}, u32[]{:S(2)}) copy-start(bf16[1,1,32,256]{3,2,1,0:T(8,128)(2,1)} %param.15) | copy-start | bytes 49156
  2.4 8.1 %copy-start.5 = (f32[1,1,32,32]{3,2,1,0:T(8,128)S(1)}, f32[1,1,32,32]{3,2,1,0:T(8,128)}, u32[]{:S(2)}) copy-start(f32[1,1,32,32]{3,2,1,0:T(8,128)} %param.18) | copy-start | bytes 12292
  2.5 15.7 %all-to-all-start = ((bf16[32,4,512]{2,1,0:T(4,128)(2,1)}), bf16[32,4,512]{2,1,0:T(4,128)(2,1)S(1)}, u32[]{:S(2)}, u32[]{:S(2)}) async-start(bf16[32,4,512]{2,1,0:T(4,128)(2,1)} %get-tuple-element.17), calls=%async_computation | async-start | bytes 262144 | tf_op jit(solution)/shard_map/all_to_all | solution.py:538
  10.4 0.7 %copy-start.7 = (s32[1,1,4]{2,1,0:T(1,128)S(1)}, s32[1,1,4]{2,1,0:T(1,128)}, u32[]{:S(2)}) copy-start(s32[1,1,4]{2,1,0:T(1,128)} %near_col_ref.1) | copy-start | bytes 52
  10.5 0.7 %copy-start.8 = (s32[1,1,6]{2,1,0:T(1,128)S(1)}, s32[1,1,6]{2,1,0:T(1,128)}, u32[]{:S(2)}) copy-start(s32[1,1,6]{2,1,0:T(1,128)} %far_col_ref.1) | copy-start | bytes 76
  11.1 1.0 %copy-start = (bf16[1,1,4,256,256]{4,3,2,1,0:T(8,128)(2,1)S(1)}, bf16[1,1,4,256,256]{4,3,2,1,0:T(8,128)(2,1)}, u32[]{:S(2)}) copy-start(bf16[1,1,4,256,256]{4,3,2,1,0:T(8,128)(2,1)} %param.11) | copy-start | bytes 1572868
  12.2 6.0 %copy-start.1 = (bf16[1,1,32,256]{3,2,1,0:T(8,128)(2,1)S(1)}, bf16[1,1,32,256]{3,2,1,0:T(8,128)(2,1)}, u32[]{:S(2)}) copy-start(bf16[1,1,32,256]{3,2,1,0:T(8,128)(2,1)} %param.16) | copy-start | bytes 49156
  13.1 5.1 %copy-start.6 = (f32[8,256]{1,0:T(8,128)S(1)}, f32[8,256]{1,0:T(8,128)}, u32[]{:S(2)}) copy-start(f32[8,256]{1,0:T(8,128)} %get-tuple-element.18.window_ref) | copy-start | bytes 24580

commit v6 on v5

--- a/solution.py
+++ b/solution.py
@@ -12,7 +12,7 @@
 LANES = 128
 PIECE = 16
 UNROLL = 32
-AXES = ("clus", "lvl")
+AXES = ("lvl", "clus")
 
 PRECISE = lax.Precision.HIGHEST
 ROWS_DIMS = (((1,), (1,)), ((), ()))
@@ -94,7 +94,7 @@
     return replicated(jnp.sum(sum(left * right for left, right in pairs), axis=1, keepdims=True))
 
 
-def begin_kernel(trees, basis_hbm, v_hbm, transfer_hbm, slots_ref, window_ref, *scratch):
+def begin_kernel(leaves, basis_hbm, v_hbm, transfer_hbm, slots_ref, window_ref, *scratch):
     basis_ref, v_ref, transfer_ref, sems = scratch
     copies = [
         pltpu.make_async_copy(source, target, sems.at[at])
@@ -152,7 +152,7 @@
             part == 0, tile[c], jnp.where(part == 1, tile[(c - 1) % turns], tile[(c - 2) % turns])
         )
         piece = lane_parts(copies_of, part)
-        same = lax.rem(jnp.int32(slot), jnp.int32(trees)) == own_tree
+        same = lax.div(jnp.int32(slot), jnp.int32(leaves)) == own_tree
         second = jnp.where(same, tree_second, level_second)
         slots_ref[slot, :, :size] = lowered
         slots_ref[slot, :, size : size + LANES] = level_first
@@ -161,9 +161,9 @@
     over_slots(slots_ref.shape[0], store)
 
     def store_tree(leaf, at):
-        slots_ref[leaf * trees + own_tree, :, size : size + LANES] = tree_first
-
-    over_slots(slots_ref.shape[0] // trees, store_tree)
+        slots_ref[own_tree * leaves + leaf, :, size : size + LANES] = tree_first
+
+    over_slots(leaves, store_tree)
 
 
 def prepare_kernel(
@@ -219,16 +219,16 @@
 def places_of(leaves, trees):
     own_tree = lax.axis_index("lvl")
     own_leaf = lax.axis_index("clus")
-    places = [leaf * trees + own_tree for leaf in range(leaves)]
-    return places + [own_leaf * trees + tree for tree in range(trees)]
-
-
-def near_places(leaves, trees):
-    own_tree = lax.axis_index("lvl")
+    places = [own_tree * leaves + leaf for leaf in range(leaves)]
+    return places + [tree * leaves + own_leaf for tree in range(trees)]
+
+
+def near_places(leaves):
+    start = lax.axis_index("lvl") * leaves
     own_leaf = lax.axis_index("clus")
     low = jnp.maximum(own_leaf - 1, 0)
     high = jnp.minimum(own_leaf + 1, leaves - 1)
-    return [leaf * trees + own_tree for leaf in (low, own_leaf, high)]
+    return [start + leaf for leaf in (low, own_leaf, high)]
 
 
 def near_field(blocks, choice_ref, near_ref):
@@ -248,10 +248,10 @@
     return sum(rows_dot(lowered, weights_ref[part]) for part in range(3))
 
 
-def product_lanes(window, image, at):
+def product_lanes(window, image, at, period=LANES):
     basis = window.shape[0]
     window, image = lane_tiles(window), lane_tiles(image)
-    lane = lanes_of((VECS, LANES))
+    lane = lanes_of((VECS, LANES)) % period
     packed = jnp.zeros((VECS, LANES), F32)
     for b in range(basis):
         product = lane_sum([(tile, other[b : b + 1]) for tile, other in zip(image, window)])
@@ -267,6 +267,12 @@
             rows = product[group * VECS : (group + 1) * VECS]
             packed = jnp.where(lane == at + group * basis + b, rows, packed)
     return packed
+
+
+def one_row(values):
+    width = LANES // VECS
+    own = lanes_of(values.shape) // width == lax.broadcasted_iota(jnp.int32, values.shape, 0)
+    return jnp.sum(jnp.where(own, values, 0.0), axis=0, keepdims=True)
 
 
 def mapped(rows, maps_ref):
@@ -305,7 +311,7 @@
     blank = jnp.zeros((2 * VECS, LANES - rank), F32)
     window_coupled_ref[...] = jnp.concatenate([linear, blank], axis=1)
     image = jnp.dot(rows[:VECS].astype(BF16), u_ref[...], preferred_element_type=F32)
-    blocks = [arrived_ref[place, :, :size] for place in near_places(leaves, trees)]
+    blocks = [arrived_ref[place, :, :size] for place in near_places(leaves)]
     image = image + near_field(blocks, choice_ref, near_ref)
     image_ref[...] = image
     packed = product_lanes(window_ref[...], image, PIECE)
@@ -321,14 +327,14 @@
 
     def store(slot, at):
         if isinstance(slot, int):
-            low, high = max(slot - trees, 0), min(slot + trees, total - 1)
+            low, high = max(slot - 1, 0), min(slot + 1, total - 1)
         else:
-            low, high = jnp.maximum(slot - trees, 0), jnp.minimum(slot + trees, total - 1)
+            low, high = jnp.maximum(slot - 1, 0), jnp.minimum(slot + 1, total - 1)
         low = arrived_ref[low, :, size + LANES :].astype(F32)
         high = arrived_ref[high, :, size + LANES :].astype(F32)
         both = jnp.where(narrow < 3 * PIECE, low, pltpu.roll(high, 3 * PIECE, 1))
         both = both + pltpu.roll(both, LANES - PIECE, 1) + pltpu.roll(both, LANES - 2 * PIECE, 1)
-        same = lax.rem(jnp.int32(slot), jnp.int32(trees)) == own_tree
+        same = lax.div(jnp.int32(slot), jnp.int32(leaves)) == own_tree
         tail = jnp.where(same, tree_tail, level_tail)
         slots_ref[slot, :, :size] = image
         slots_ref[slot, :, size:] = jnp.where(from_low | from_high, both, tail)
@@ -433,7 +439,7 @@
         ]
 
     leaves = slots // trees
-    low_place, _, high_place = near_places(leaves, trees)
+    low_place, _, high_place = near_places(leaves)
     tails = jnp.concatenate(
         [arrived_ref[place, :, size:] for place in places_of(leaves, trees)], axis=1
     )
@@ -469,17 +475,18 @@
         solved[-1][:, :rank].astype(BF16), u_ref[...], preferred_element_type=F32
     )
     skeleton, coarse = mapped(new_block.astype(BF16), maps_ref)
-    packed = product_lanes(next_window, near_part + far_part, 0)
-    tree_tail = jnp.where(lane < rank, packed, skeleton)
-    level_tail = jnp.where(lane < rank, packed, coarse)
+    width = LANES // VECS
+    packed = one_row(product_lanes(next_window, near_part + far_part, 0, width))
+    tree_rows = jnp.concatenate([one_row(skeleton), packed], axis=0)
+    level_rows = jnp.concatenate([one_row(coarse), packed], axis=0)
 
     def store(slot, at):
-        slots_ref[slot] = level_tail
+        slots_ref[slot] = level_rows
 
     over_slots(slots, store)
 
     def store_tree(leaf, at):
-        slots_ref[leaf * trees + own_tree] = tree_tail
+        slots_ref[own_tree * leaves + leaf] = tree_rows
 
     over_slots(leaves, store_tree)
 
@@ -488,6 +495,7 @@
     trees,
     rows_all,
     arrived_ref,
+    flat_ref,
     window_ref,
     near_part_ref,
     weights_ref,
@@ -496,21 +504,32 @@
     block_ref,
     records_ref,
 ):
-    rank = u_ref.shape[0]
     leaves = arrived_ref.shape[0] // trees
-    tails = jnp.concatenate(
-        [arrived_ref[place] for place in places_of(leaves, trees)], axis=1
-    )
-    part = lanes_of(tails.shape) % LANES // rank - 1
-    coupled = couple(jnp.where(part >= 0, lane_parts(tails, part), 0.0), weights_ref)
+    width = LANES // VECS
+    rows = jnp.concatenate(
+        [arrived_ref[place, 0:1, :] for place in places_of(leaves, trees)], axis=0
+    )
+    shape = (VECS, LANES)
+    row = lax.broadcasted_iota(jnp.int32, shape, 0)
+    own = lanes_of(shape) // width == row
+    parts = [
+        jnp.concatenate(
+            [jnp.where(own, part[at : at + 1], 0.0) for at in range(rows.shape[0])], axis=1
+        )
+        for part in (piece.astype(F32) for piece in three_parts(rows))
+    ]
+    coupled = sum(row_groups(couple(jnp.concatenate(parts, axis=0), weights_ref)))
     far_part = jnp.dot(coupled.astype(BF16), u_ref[...], preferred_element_type=F32)
-    slots = arrived_ref.shape[0]
-    near = min(slots, UNROLL)
-    total = arrived_ref[0]
-    for slot in range(1, near):
-        total = total + arrived_ref[slot]
-    if slots > near:
-        total = lax.fori_loop(near, slots, lambda at, held: held + arrived_ref[at], total)
+    step = flat_ref.shape[0] // arrived_ref.shape[0] * VECS
+    total = flat_ref[0:step]
+    for at in range(step, flat_ref.shape[0], step):
+        total = total + flat_ref[at : at + step]
+    total = sum(total[at : at + 1] for at in range(1, step, step // VECS))
+    turned = jnp.zeros(shape, F32)
+    for v in range(VECS):
+        moved = pltpu.roll(total, LANES - width * v, 1) if v else total
+        turned = jnp.where(row == v, moved, turned)
+    total = turned
     total = total * (1.0 / rows_all)
     image = near_part_ref[...] + far_part
     solved, record = orthogonalized(total, 0, lane_tiles(window_ref[...]), lane_tiles(image))
@@ -566,7 +585,7 @@
     choice_like = ((-(-3 * near_own.shape[0] // 8) * 8, LANES), F32)
     weights_like = ((3, rank, (leaves + trees) * LANES), BF16)
     slots, window = call(
-        functools.partial(begin_kernel, trees),
+        functools.partial(begin_kernel, leaves),
         "begin",
         [((devices, VECS, size + 2 * LANES), BF16), window_like],
         [flat_basis, v_own, transfer_own],
@@ -607,7 +626,7 @@
     slots, window, near_part, record = call(
         functools.partial(middle_kernel, trees, rows_all),
         "middle",
-        [((devices, VECS, LANES), F32), window_like, image_like, record_like],
+        [((devices, 2, LANES), F32), window_like, image_like, record_like],
         [
             arrived,
             window,
@@ -626,8 +645,8 @@
         functools.partial(end_kernel, trees, rows_all),
         "end",
         [((VECS * size // LANES, LANES), F32), ((STEPS, VECS, basis + VECS), F32)],
-        [arrived, window, near_part, weights, u_own, record],
-        "v" * 6,
+        [arrived, arrived.reshape(-1, LANES), window, near_part, weights, u_own, record],
+        "v" * 7,
     )
     return (block.reshape(VECS, 1, size), jnp.transpose(records, (0, 2, 1)))
 

time: 41.5 us -> 41 us (0.988)
  no operation moved by 1% of the time
where the time goes in v6:
time: 41 us; the launch traced here: 40.6 us
  blocking collectives  20.2 us (49%)
  starting transfers between devices  7.33 us (18%)
  Pallas kernels  5.1 us (12%)
  waiting for transfers between devices  4.87 us (12%)
  local copies, waits for them, and re-layouts  1.69 us (4%)
  between operations  1.41 us (3%)
    all_to_all x2, blocking collectives, exchange(): return lax.all_to_all(slots, AXES, 0, 0, tiled=True)  20.2 us
    all_to_all x1, starting transfers between devices, exchange(): return lax.all_to_all(slots, AXES, 0, 0, tiled=True)  7.33 us
    pallas_call x5, Pallas kernels, call(): pl.pallas_call(kernel, name=name, out_shape=[jax.ShapeDtypeStruct(shape,...  5.1 us
    all_to_all x1, waiting for transfers between devices, exchange(): return lax.all_to_all(slots, AXES, 0, 0, tiled=True)  4.87 us
    unnamed x18, local copies, waits for them, and re-layouts  1.69 us
  transfers between devices with their start and end apart: 1, of which 1 were waited for; matrix products, arithmetic and copies ran while one was open for 0% of the time, Pallas kernels for 2%

profile of v6, /device:TPU:0, one launch (start us, length us, event | category | flops | bytes accessed | tf_op | source)
XLA Modules:
  0.0 40.6 jit_solution(14218225248820007536)
XLA Ops:
  0.6 1.8 %begin.1 = (bf16[32,4,512]{2,1,0:T(4,128)(2,1)}, f32[8,256]{1,0:T(8,128)}) custom-call(f32[16,128]{1,0:T(8,128)} %bitcast.21, bf16[32,256]{1,0:T(8,128)(2,1)} %bitcast.17, f32[32,32]{1,0:T(8,128)} %bitcast.19), custom_call_target="tpu_custom_call" | custom-call | bytes 1048576 | tf_op jit(solution)/shard_map/begin/pallas_call | solution.py:544
  2.4 0.0 copy-start.2
  2.4 0.0 copy-start.3
  2.4 0.0 copy-start.4
  2.4 0.0 copy-start.5
  2.5 7.3 %all-to-all-start = ((bf16[32,4,512]{2,1,0:T(4,128)(2,1)}), bf16[32,4,512]{2,1,0:T(4,128)(2,1)S(1)}, u32[]{:S(2)}, u32[]{:S(2)}) async-start(bf16[32,4,512]{2,1,0:T(4,128)(2,1)} %get-tuple-element.17), calls=%async_computation | async-start | bytes 262144 | tf_op jit(solution)/shard_map/all_to_all | solution.py:557
  10.4 0.0 copy-start.7
  10.5 0.0 copy-start.8
  10.5 0.0 copy-done.2
  10.5 0.0 copy-done.3
  10.5 0.0 copy-done.4
  10.5 0.0 copy-done.5
  10.5 0.6 %copy-done.7 = s32[1,1,4]{2,1,0:T(1,128)S(1)} copy-done((s32[1,1,4]{2,1,0:T(1,128)S(1)}, s32[1,1,4]{2,1,0:T(1,128)}, u32[]{:S(2)}) %copy-start.7) | copy-done | bytes 40
  11.1 0.0 copy-done.8
  11.1 0.0 copy-start
  11.1 1.0 %copy-done = bf16[1,1,4,256,256]{4,3,2,1,0:T(8,128)(2,1)S(1)} copy-done((bf16[1,1,4,256,256]{4,3,2,1,0:T(8,128)(2,1)S(1)}, bf16[1,1,4,256,256]{4,3,2,1,0:T(8,128)(2,1)}, u32[]{:S(2)}) %copy-start) | copy-done | bytes 524312
  12.2 0.0 copy-start.1
  12.2 0.9 %prepare.1 = (bf16[3,32,1536]{2,1,0:T(8,128)(2,1)S(1)}, bf16[4,256,256]{2,1,0:T(8,128)(2,1)S(1)}, bf16[512,256]{1,0:T(8,128)(2,1)S(1)}, f32[16,128]{1,0:T(8,128)S(1)}) custom-call(s32[1,1,4]{2,1,0:T(1,128)S(1)} %copy-done.7, s32[1,1]{1,0:T(1,128)S(6)} %copy.13.near_count_ref, s32[1,1,6]{2,1,0:T(1,128)S(1)} %copy-done.8, bf16[4,256,256]{2,1,0:T(8,128)(2,1)S(1)} %bitcast.10, ...), custom_call_target="tpu_custom_call" | custom-call | bytes 1048576 | tf_op jit(solution)/shard_map/prepare/pallas_call | solution.py:544
  13.1 0.0 copy-start.6
  13.1 4.9 %all-to-all-done.arrived_ref = bf16[32,4,512]{2,1,0:T(4,128)(2,1)S(1)} async-done(((bf16[32,4,512]{2,1,0:T(4,128)(2,1)}), bf16[32,4,512]{2,1,0:T(4,128)(2,1)S(1)}, u32[]{:S(2)}, u32[]{:S(2)}) %all-to-all-start) | async-done | bytes 131104 | tf_op jit(solution)/shard_map/all_to_all | solution.py:557
  18.0 0.0 copy-done.1
  18.0 0.0 copy-done.6
  18.0 0.6 %first.1 = (f32[4,256]{1,0:T(4,128)S(1)}, f32[32,4,384]{2,1,0:T(4,128)S(1)}, f32[8,128]{1,0:T(8,128)S(1)}) custom-call(bf16[32,4,512]{2,1,0:T(4,128)(2,1)S(1)} %all-to-all-done.arrived_ref, f32[8,256]{1,0:T(8,128)S(1)} %copy-done.6, bf16[3,32,1536]{2,1,0:T(8,128)(2,1)S(1)} %get-tuple-element.19.weights_ref, ...), custom_call_target="tpu_custom_call" | custom-call | bytes 1048576 | tf_op jit(solution)/shard_map/first/pallas_call | solution.py:544
  18.6 10.5 %all_to_all.15.arrived_ref = f32[32,4,384]{2,1,0:T(4,128)S(1)} all-to-all(f32[32,4,384]{2,1,0:T(4,128)S(1)} %get-tuple-element.23), channel_id=1, replica_groups=mesh['clus'=8,'lvl'=4] {'lvl','clus'}, dimensions={0} | all-to-all | bytes 393216 | tf_op jit(solution)/shard_map/all_to_all | solution.py:557
  29.1 0.8 %middle.1 = (f32[32,2,128]{2,1,0:T(2,128)S(1)}, f32[8,256]{1,0:T(8,128)S(1)}, f32[4,256]{1,0:T(4,128)S(1)}, f32[4,128]{1,0:T(4,128)S(1)}) custom-call(f32[32,4,384]{2,1,0:T(4,128)S(1)} %all_to_all.15.arrived_ref, f32[8,256]{1,0:T(8,128)S(1)} %copy-done.6, f32[4,256]{1,0:T(4,128)S(1)} %get-tuple-element.24.image_ref, ...), custom_call_target="tpu_custom_call" | custom-call | bytes 1048576 | tf_op jit(solution)/shard_map/middle/pallas_call | solution.py:544
  29.9 9.6 %all_to_all.16.arrived_ref = f32[32,2,128]{2,1,0:T(2,128)S(1)} all-to-all(f32[32,2,128]{2,1,0:T(2,128)S(1)} %get-tuple-element.26), channel_id=1, replica_groups=mesh['clus'=8,'lvl'=4] {'lvl','clus'}, dimensions={0} | all-to-all | bytes 65536 | tf_op jit(solution)/shard_map/all_to_all | solution.py:557
  39.6 1.0 %end.1 = (f32[8,128]{1,0:T(8,128)}, f32[2,4,12]{2,1,0:T(4,128)}) custom-call(f32[32,2,128]{2,1,0:T(2,128)S(1)} %all_to_all.16.arrived_ref, f32[64,128]{1,0:T(8,128)S(1)} %bitcast.11, f32[8,256]{1,0:T(8,128)S(1)} %get-tuple-element.27.window_ref, f32[4,256]{1,0:T(4,128)S(1)} %get-tuple-element.28.near_part_ref, ...), custom_call_target="tpu_custom_call" | custom-call | bytes 1048576 | tf_op jit(solution)/shard_map/end/pallas_call | solution.py:544
Async XLA Ops:
  2.4 8.1 %copy-start.2 = (f32[1,1,6,32,32]{4,3,2,1,0:T(8,128)S(1)}, f32[1,1,6,32,32]{4,3,2,1,0:T(8,128)}, u32[]{:S(2)}) copy-start(f32[1,1,6,32,32]{4,3,2,1,0:T(8,128)} %param.17) | copy-start | bytes 73732
  2.4 8.1 %copy-start.3 = (f32[1,1,4,32,32]{4,3,2,1,0:T(8,128)S(1)}, f32[1,1,4,32,32]{4,3,2,1,0:T(8,128)}, u32[]{:S(2)}) copy-start(f32[1,1,4,32,32]{4,3,2,1,0:T(8,128)} %param.19) | copy-start | bytes 49156
  2.4 8.1 %copy-start.4 = (bf16[1,1,32,256]{3,2,1,0:T(8,128)(2,1)S(1)}, bf16[1,1,32,256]{3,2,1,0:T(8,128)(2,1)}, u32[]{:S(2)}) copy-start(bf16[1,1,32,256]{3,2,1,0:T(8,128)(2,1)} %param.15) | copy-start | bytes 49156
  2.4 8.1 %copy-start.5 = (f32[1,1,32,32]{3,2,1,0:T(8,128)S(1)}, f32[1,1,32,32]{3,2,1,0:T(8,128)}, u32[]{:S(2)}) copy-start(f32[1,1,32,32]{3,2,1,0:T(8,128)} %param.18) | copy-start | bytes 12292
  2.5 15.5 %all-to-all-start = ((bf16[32,4,512]{2,1,0:T(4,128)(2,1)}), bf16[32,4,512]{2,1,0:T(4,128)(2,1)S(1)}, u32[]{:S(2)}, u32[]{:S(2)}) async-start(bf16[32,4,512]{2,1,0:T(4,128)(2,1)} %get-tuple-element.17), calls=%async_computation | async-start | bytes 262144 | tf_op jit(solution)/shard_map/all_to_all | solution.py:557
  10.4 0.7 %copy-start.7 = (s32[1,1,4]{2,1,0:T(1,128)S(1)}, s32[1,1,4]{2,1,0:T(1,128)}, u32[]{:S(2)}) copy-start(s32[1,1,4]{2,1,0:T(1,128)} %near_col_ref.1) | copy-start | bytes 52
  10.5 0.7 %copy-start.8 = (s32[1,1,6]{2,1,0:T(1,128)S(1)}, s32[1,1,6]{2,1,0:T(1,128)}, u32[]{:S(2)}) copy-start(s32[1,1,6]{2,1,0:T(1,128)} %far_col_ref.1) | copy-start | bytes 76
  11.1 1.0 %copy-start = (bf16[1,1,4,256,256]{4,3,2,1,0:T(8,128)(2,1)S(1)}, bf16[1,1,4,256,256]{4,3,2,1,0:T(8,128)(2,1)}, u32[]{:S(2)}) copy-start(bf16[1,1,4,256,256]{4,3,2,1,0:T(8,128)(2,1)} %param.11) | copy-start | bytes 1572868
  12.2 5.8 %copy-start.1 = (bf16[1,1,32,256]{3,2,1,0:T(8,128)(2,1)S(1)}, bf16[1,1,32,256]{3,2,1,0:T(8,128)(2,1)}, u32[]{:S(2)}) copy-start(bf16[1,1,32,256]{3,2,1,0:T(8,128)(2,1)} %param.16) | copy-start | bytes 49156
  13.1 4.9 %copy-start.6 = (f32[8,256]{1,0:T(8,128)S(1)}, f32[8,256]{1,0:T(8,128)}, u32[]{:S(2)}) copy-start(f32[8,256]{1,0:T(8,128)} %get-tuple-element.18.window_ref) | copy-start | bytes 24580

commit v7 on v6

--- a/solution.py
+++ b/solution.py
@@ -131,32 +131,30 @@
 
     tree_first, tree_second = tails(skeletons)
     level_first, level_second = tails(coarse)
-    lane = lanes_of((VECS, LANES))
+    kept = lanes_of((VECS, LANES)) >= LANES - 2 * rank
+    flat = basis_ref[...]
     turns = LANES // PIECE
-    kept = lane >= LANES - 2 * rank
-    tiles = [
-        window[row : row + VECS, at : at + LANES]
-        for row in range(0, basis, VECS)
-        for at in range(0, size, LANES)
+    turned = [pltpu.roll(flat, LANES - PIECE * c, 1) if c else flat for c in range(turns)]
+    part = lanes_of(flat.shape) // PIECE
+    pieces = [
+        lane_parts(
+            jnp.where(
+                part == 0, turned[c], jnp.where(part == 1, turned[c - 1], turned[c - 2])
+            ),
+            part,
+        )
+        for c in range(turns)
     ]
-    turned = [
-        [pltpu.roll(tile, (LANES - PIECE * c) % LANES, 1) if c else tile for c in range(turns)]
-        for tile in tiles
-    ]
-    part = lane // PIECE
 
     def store(slot, at):
-        tile = turned[at // turns % len(tiles)]
-        c = at % turns
-        copies_of = jnp.where(
-            part == 0, tile[c], jnp.where(part == 1, tile[(c - 1) % turns], tile[(c - 2) % turns])
-        )
-        piece = lane_parts(copies_of, part)
+        row, side = at * VECS // turns % flat.shape[0], at * VECS % turns
+        piece = [pieces[side + v][row : row + 1] for v in range(VECS)]
         same = lax.div(jnp.int32(slot), jnp.int32(leaves)) == own_tree
         second = jnp.where(same, tree_second, level_second)
+        piece = jnp.where(kept, second, jnp.concatenate(piece, axis=0))
         slots_ref[slot, :, :size] = lowered
         slots_ref[slot, :, size : size + LANES] = level_first
-        slots_ref[slot, :, size + LANES :] = jnp.where(kept, second, piece).astype(BF16)
+        slots_ref[slot, :, size + LANES :] = piece.astype(BF16)
 
     over_slots(slots_ref.shape[0], store)
 
@@ -231,16 +229,21 @@
     return [start + leaf for leaf in (low, own_leaf, high)]
 
 
+def tree_sum(values):
+    while len(values) > 1:
+        values = [sum(values[at : at + 2]) for at in range(0, len(values), 2)]
+    return values[0]
+
+
 def near_field(blocks, choice_ref, near_ref):
     choice = choice_ref[...]
     blocks = [[tile.astype(F32) for tile in lane_tiles(block)] for block in blocks]
-    result = None
+    parts = []
     for slot in range(near_ref.shape[0]):
         rows = [choice[3 * slot + side : 3 * slot + side + 1] for side in range(3)]
         tiles = [sum(tile * row for tile, row in zip(sides, rows)) for sides in zip(*blocks)]
-        part = rows_dot(jnp.concatenate(tiles, axis=1).astype(BF16), near_ref[slot])
-        result = part if result is None else result + part
-    return result
+        parts.append(rows_dot(jnp.concatenate(tiles, axis=1).astype(BF16), near_ref[slot]))
+    return tree_sum(parts)
 
 
 def couple(values, weights_ref):
@@ -248,15 +251,15 @@
     return sum(rows_dot(lowered, weights_ref[part]) for part in range(3))
 
 
-def product_lanes(window, image, at, period=LANES):
+def product_lanes(window, image, period):
     basis = window.shape[0]
     window, image = lane_tiles(window), lane_tiles(image)
     lane = lanes_of((VECS, LANES)) % period
     packed = jnp.zeros((VECS, LANES), F32)
     for b in range(basis):
         product = lane_sum([(tile, other[b : b + 1]) for tile, other in zip(image, window)])
-        packed = jnp.where(lane == at + b, product, packed)
-    at = at + basis
+        packed = jnp.where(lane == b, product, packed)
+    at = basis
     for u in range(VECS):
         product = lane_sum([(tile, tile[u : u + 1]) for tile in image])
         packed = jnp.where(lane == at + u, product, packed)
@@ -267,6 +270,18 @@
             rows = product[group * VECS : (group + 1) * VECS]
             packed = jnp.where(lane == at + group * basis + b, rows, packed)
     return packed
+
+
+def couple_rows(rows, weights_ref):
+    shape = (VECS, LANES)
+    own = lanes_of(shape) // (LANES // VECS) == lax.broadcasted_iota(jnp.int32, shape, 0)
+    parts = [
+        jnp.concatenate(
+            [jnp.where(own, part[at : at + 1], 0.0) for at in range(rows.shape[0])], axis=1
+        )
+        for part in (piece.astype(F32) for piece in three_parts(rows))
+    ]
+    return sum(row_groups(couple(jnp.concatenate(parts, axis=0), weights_ref)))
 
 
 def one_row(values):
@@ -314,43 +329,73 @@
     blocks = [arrived_ref[place, :, :size] for place in near_places(leaves)]
     image = image + near_field(blocks, choice_ref, near_ref)
     image_ref[...] = image
-    packed = product_lanes(window_ref[...], image, PIECE)
+    width = LANES // VECS
+    packed = one_row(product_lanes(window_ref[...], image, width))
     parts = [part.astype(F32) for part in three_parts(image)]
     skeleton, coarse = mapped(jnp.concatenate(parts, axis=0).astype(BF16), maps_ref)
-    kept = lanes_of((VECS, LANES)) < LANES - 2 * rank
-    tree_tail = jnp.where(kept, packed, skeleton)
-    level_tail = jnp.where(kept, packed, coarse)
-    narrow = lanes_of((VECS, LANES))
-    from_low = narrow < PIECE
-    from_high = (narrow >= 3 * PIECE) & (narrow < 4 * PIECE)
-    total = slots_ref.shape[0]
-
-    def store(slot, at):
-        if isinstance(slot, int):
-            low, high = max(slot - 1, 0), min(slot + 1, total - 1)
-        else:
-            low, high = jnp.maximum(slot - 1, 0), jnp.minimum(slot + 1, total - 1)
-        low = arrived_ref[low, :, size + LANES :].astype(F32)
-        high = arrived_ref[high, :, size + LANES :].astype(F32)
-        both = jnp.where(narrow < 3 * PIECE, low, pltpu.roll(high, 3 * PIECE, 1))
-        both = both + pltpu.roll(both, LANES - PIECE, 1) + pltpu.roll(both, LANES - 2 * PIECE, 1)
-        same = lax.div(jnp.int32(slot), jnp.int32(leaves)) == own_tree
-        tail = jnp.where(same, tree_tail, level_tail)
-        slots_ref[slot, :, :size] = image
-        slots_ref[slot, :, size:] = jnp.where(from_low | from_high, both, tail)
-
-    over_slots(total, store)
-
-
-def orthogonalized(total, at, windows, images):
+    tree_row, level_row = one_row(skeleton), one_row(coarse)
+    image_rows = jnp.concatenate(lane_tiles(image), axis=0)
+    per_slot = image_rows.shape[0] + 3
+    total = slots_ref.shape[0] // per_slot
+    step = min(total, UNROLL)
+    shape = (2 * VECS, LANES)
+    lane = lanes_of(shape)
+    row = lax.broadcasted_iota(jnp.int32, shape, 0)
+    own = lane // PIECE % VECS == row % VECS
+
+    def fill(part_ref, start):
+        for inner in range(0, step, 2):
+            sides = []
+            for shift in (-1, 1):
+                near = [start + inner + at + shift for at in range(2)]
+                if isinstance(start, int):
+                    near = [min(max(slot, 0), total - 1) for slot in near]
+                else:
+                    near = [jnp.clip(slot, 0, total - 1) for slot in near]
+                near = [arrived_ref[slot, :, size + LANES :].astype(F32) for slot in near]
+                sides.append(jnp.concatenate(near, axis=0))
+            both = jnp.where(lane < LANES // 2, sides[0], pltpu.roll(sides[1], LANES // 2, 1))
+            both = (
+                both
+                + pltpu.roll(both, LANES - PIECE, 1)
+                + pltpu.roll(both, LANES - 2 * PIECE, 1)
+            )
+            both = jnp.where(own, pltpu.roll(both, 0, 1, stride=PIECE, stride_axis=0), 0.0)
+            for at in range(2):
+                relay = jnp.sum(both[at * VECS : (at + 1) * VECS], axis=0, keepdims=True)
+                slot = jnp.int32(start + inner + at)
+                same = lax.div(slot, jnp.int32(leaves)) == own_tree
+                far = jnp.where(same, tree_row, level_row)
+                first_row = (inner + at) * per_slot
+                part_ref[first_row : first_row + per_slot] = jnp.concatenate(
+                    [image_rows, far, relay, packed], axis=0
+                )
+
+    if total == step:
+        fill(slots_ref, 0)
+    else:
+
+        def body(at, carry):
+            start = pl.multiple_of(at * (step * per_slot), 8)
+            fill(slots_ref.at[pl.ds(start, step * per_slot)], at * step)
+            return carry
+
+        lax.fori_loop(0, total // step, body, 0)
+
+
+def orthogonalized(total, windows, images):
     basis = windows[0].shape[0]
-
-    def column_of(lane):
-        return replicated(total[:, lane : lane + 1])
-
-    projection = [column_of(at + b) for b in range(basis)]
-    square = [column_of(at + basis + u) for u in range(VECS)]
-    start = at + basis + VECS
+    shape = (VECS, LANES)
+    row, lane = lax.broadcasted_iota(jnp.int32, shape, 0), lanes_of(shape)
+    total = jnp.broadcast_to(total, shape)
+
+    def column_of(at):
+        places = row * (LANES // VECS) + at
+        return jnp.take_along_axis(total, places, axis=1, mode="promise_in_bounds")
+
+    projection = [column_of(b) for b in range(basis)]
+    square = [column_of(basis + u) for u in range(VECS)]
+    start = basis + VECS
     inner = []
     for other in range(basis):
         value = -2.0 * projection[other]
@@ -370,9 +415,9 @@
         for b in range(basis):
             image = image - projection[b] * window[b : b + 1]
         remainders.append(image)
-    row = lax.broadcasted_iota(jnp.int32, (VECS, LANES), 0)
-    lane = lanes_of((VECS, LANES))
-    record = total if at == 0 else pltpu.roll(total, LANES - at, 1)
+    record = jnp.zeros(shape, F32)
+    for b in range(basis):
+        record = jnp.where(lane == b, projection[b], record)
     for j in range(VECS):
         pivot = columns[j][j : j + 1]
         scale = lax.rsqrt(pivot)
@@ -390,6 +435,7 @@
     trees,
     rows_all,
     arrived_ref,
+    flat_ref,
     window_ref,
     image_ref,
     window_coupled_ref,
@@ -408,60 +454,64 @@
     basis, size = window.shape
     rank = u_ref.shape[0]
     lane = lanes_of((VECS, LANES))
-    group = lane // PIECE
-    turns = LANES // PIECE
-    tile_count = basis // VECS * (size // LANES)
-    low_tiles, high_tiles = [], []
-    total = jnp.zeros((VECS, LANES), F32)
-    for slot in range(tile_count * turns):
-        tail = arrived_ref[slot, :, size:]
-        total = total + tail
-        c = slot % turns
-        turned = pltpu.roll(tail, PIECE * c, 1) if c else tail
-        if c == 0:
-            low_tiles.append(turned)
-            high_tiles.append(turned)
-        else:
-            low_tiles[-1] = jnp.where(group == c, turned, low_tiles[-1])
-            high_tiles[-1] = jnp.where(group == (c + 3) % turns, turned, high_tiles[-1])
     slots = arrived_ref.shape[0]
-    if slots > tile_count * turns:
-        total = lax.fori_loop(
-            tile_count * turns, slots, lambda at, held: held + arrived_ref[at, :, size:], total
+    leaves = slots // trees
+    per_slot = flat_ref.shape[0] // slots
+    per_row = size // LANES
+    image_count = VECS * per_row
+    rows = [
+        flat_ref[pl.ds(per_slot * at + image_count + 2, 8, stride=per_slot), :]
+        for at in range(0, slots, 8)
+    ]
+    total = jnp.sum(tree_sum(rows), axis=0, keepdims=True) * (1.0 / rows_all)
+    first_tiles, other_tiles = [], []
+    left = lanes_of((basis, LANES)) < LANES // 2
+    for half in range(per_row):
+        even, odd = (
+            flat_ref[
+                pl.ds(
+                    per_slot * (2 * half + side) + image_count + 1,
+                    basis,
+                    stride=2 * per_row * per_slot,
+                ),
+                :,
+            ]
+            for side in range(2)
         )
-    high_tiles = [pltpu.roll(tile, LANES - 3 * PIECE, 1) for tile in high_tiles]
-    total = total * (1.0 / rows_all)
-
-    def rows_from(tiles):
-        per_row = size // LANES
-        return [
-            jnp.concatenate(tiles[at::per_row], axis=0) for at in range(per_row)
-        ]
-
-    leaves = slots // trees
+        first_tiles.append(jnp.where(left, even, pltpu.roll(odd, LANES // 2, 1)))
+        other_tiles.append(jnp.where(left, pltpu.roll(even, LANES // 2, 1), odd))
+    own_slot = own_tree * leaves + lax.axis_index("clus")
+    even_slot = lax.rem(own_slot, jnp.int32(2)) == 0
+    low_tiles = [jnp.where(even_slot, a, b) for a, b in zip(first_tiles, other_tiles)]
+    high_tiles = [jnp.where(even_slot, b, a) for a, b in zip(first_tiles, other_tiles)]
+
+    def rows_of(place, start, count):
+        at = [(start + row) * LANES for row in range(count)]
+        return jnp.concatenate(
+            [arrived_ref[place, 0:1, lane : lane + LANES] for lane in at], axis=0
+        )
+
     low_place, _, high_place = near_places(leaves)
-    tails = jnp.concatenate(
-        [arrived_ref[place, :, size:] for place in places_of(leaves, trees)], axis=1
-    )
-    tails = lane_parts(tails, lanes_of(tails.shape) % LANES // rank - (LANES // rank - 2))
-    wide_lane = lanes_of(tails.shape) % LANES
-    tails = jnp.where(wide_lane >= LANES - 2 * rank, tails, 0.0)
-    coupled = couple(tails, weights_ref)
+    coupled = couple_rows(
+        jnp.concatenate(
+            [rows_of(place, image_count, 1) for place in places_of(leaves, trees)], axis=0
+        ),
+        weights_ref,
+    )
     images = [
-        *lane_tiles(arrived_ref[low_place, :, :size]),
+        *row_groups(rows_of(low_place, 0, image_count)),
         *lane_tiles(image_ref[...]),
-        *lane_tiles(arrived_ref[high_place, :, :size]),
+        *row_groups(rows_of(high_place, 0, image_count)),
         jnp.concatenate([coupled, jnp.zeros((VECS, LANES - rank), F32)], axis=1),
     ]
     windows = [
-        *rows_from(low_tiles),
+        *low_tiles,
         *lane_tiles(window),
-        *rows_from(high_tiles),
+        *high_tiles,
         window_coupled_ref[...],
     ]
-    solved, record = orthogonalized(total, PIECE, windows, images)
+    solved, record = orthogonalized(total, windows, images)
     record_ref[...] = record
-    per_row = size // LANES
     low_block, new_block, high_block = (
         jnp.concatenate(solved[at : at + per_row], axis=1)
         for at in range(0, 3 * per_row, per_row)
@@ -476,7 +526,7 @@
     )
     skeleton, coarse = mapped(new_block.astype(BF16), maps_ref)
     width = LANES // VECS
-    packed = one_row(product_lanes(next_window, near_part + far_part, 0, width))
+    packed = one_row(product_lanes(next_window, near_part + far_part, width))
     tree_rows = jnp.concatenate([one_row(skeleton), packed], axis=0)
     level_rows = jnp.concatenate([one_row(coarse), packed], axis=0)
 
@@ -505,34 +555,19 @@
     records_ref,
 ):
     leaves = arrived_ref.shape[0] // trees
-    width = LANES // VECS
     rows = jnp.concatenate(
         [arrived_ref[place, 0:1, :] for place in places_of(leaves, trees)], axis=0
     )
-    shape = (VECS, LANES)
-    row = lax.broadcasted_iota(jnp.int32, shape, 0)
-    own = lanes_of(shape) // width == row
-    parts = [
-        jnp.concatenate(
-            [jnp.where(own, part[at : at + 1], 0.0) for at in range(rows.shape[0])], axis=1
-        )
-        for part in (piece.astype(F32) for piece in three_parts(rows))
-    ]
-    coupled = sum(row_groups(couple(jnp.concatenate(parts, axis=0), weights_ref)))
+    coupled = couple_rows(rows, weights_ref)
     far_part = jnp.dot(coupled.astype(BF16), u_ref[...], preferred_element_type=F32)
     step = flat_ref.shape[0] // arrived_ref.shape[0] * VECS
     total = flat_ref[0:step]
     for at in range(step, flat_ref.shape[0], step):
         total = total + flat_ref[at : at + step]
     total = sum(total[at : at + 1] for at in range(1, step, step // VECS))
-    turned = jnp.zeros(shape, F32)
-    for v in range(VECS):
-        moved = pltpu.roll(total, LANES - width * v, 1) if v else total
-        turned = jnp.where(row == v, moved, turned)
-    total = turned
     total = total * (1.0 / rows_all)
     image = near_part_ref[...] + far_part
-    solved, record = orthogonalized(total, 0, lane_tiles(window_ref[...]), lane_tiles(image))
+    solved, record = orthogonalized(total, lane_tiles(window_ref[...]), lane_tiles(image))
     store_rows(block_ref, jnp.concatenate(solved, axis=1))
     used = records_ref.shape[2]
     records_ref[0] = first_ref[:, :used]
@@ -580,6 +615,7 @@
     far_own, top_own, near_own = far_coupling[0, 0], top_coupling[0, 0], near_block[0, 0]
     image_like = ((VECS, size), F32)
     window_like = ((basis, size), F32)
+    per_slot = VECS * size // LANES + 3
     record_like = ((VECS, LANES), F32)
     maps_like = ((4 * LANES, size), BF16)
     choice_like = ((-(-3 * near_own.shape[0] // 8) * 8, LANES), F32)
@@ -610,7 +646,7 @@
     image, slots, window_coupled = call(
         functools.partial(first_kernel, trees),
         "first",
-        [image_like, ((devices, VECS, size + LANES), F32), ((basis, LANES), F32)],
+        [image_like, ((devices * per_slot, LANES), F32), ((basis, LANES), F32)],
         [
             arrived,
             window,
@@ -622,13 +658,14 @@
         ],
         "v" * 7,
     )
-    arrived = exchange(slots)
+    arrived = exchange(slots.reshape(devices, 1, per_slot * LANES))
     slots, window, near_part, record = call(
         functools.partial(middle_kernel, trees, rows_all),
         "middle",
         [((devices, 2, LANES), F32), window_like, image_like, record_like],
         [
             arrived,
+            arrived.reshape(-1, LANES),
             window,
             image,
             window_coupled,
@@ -638,7 +675,7 @@
             u_own,
             maps,
         ],
-        "v" * 9,
+        "v" * 10,
     )
     arrived = exchange(slots)
     block, records = call(

time: 41 us -> 40.4 us (0.985)
  no operation moved by 1% of the time
where the time goes in v7:
time: 40.4 us; the launch traced here: 40 us
  blocking collectives  19.8 us (49%)
  starting transfers between devices  7.33 us (18%)
  waiting for transfers between devices  4.87 us (12%)
  Pallas kernels  4.86 us (12%)
  local copies, waits for them, and re-layouts  1.69 us (4%)
  between operations  1.41 us (3%)
    all_to_all x2, blocking collectives, exchange(): return lax.all_to_all(slots, AXES, 0, 0, tiled=True)  19.8 us
    all_to_all x1, starting transfers between devices, exchange(): return lax.all_to_all(slots, AXES, 0, 0, tiled=True)  7.33 us
    all_to_all x1, waiting for transfers between devices, exchange(): return lax.all_to_all(slots, AXES, 0, 0, tiled=True)  4.87 us
    pallas_call x5, Pallas kernels, call(): pl.pallas_call(kernel, name=name, out_shape=[jax.ShapeDtypeStruct(shape,...  4.86 us
    unnamed x18, local copies, waits for them, and re-layouts  1.69 us
  transfers between devices with their start and end apart: 1, of which 1 were waited for; matrix products, arithmetic and copies ran while one was open for 0% of the time, Pallas kernels for 2%

profile of v7, /device:TPU:0, one launch (start us, length us, event | category | flops | bytes accessed | tf_op | source)
XLA Modules:
  0.0 40.0 jit_solution(4142596511560174401)
XLA Ops:
  0.6 1.8 %begin.1 = (bf16[32,4,512]{2,1,0:T(4,128)(2,1)}, f32[8,256]{1,0:T(8,128)}) custom-call(f32[16,128]{1,0:T(8,128)} %bitcast.25, bf16[32,256]{1,0:T(8,128)(2,1)} %bitcast.21, f32[32,32]{1,0:T(8,128)} %bitcast.23), custom_call_target="tpu_custom_call" | custom-call | bytes 1048576 | tf_op jit(solution)/shard_map/begin/pallas_call | solution.py:579
  2.4 0.0 copy-start.2
  2.4 0.0 copy-start.3
  2.4 0.0 copy-start.4
  2.4 0.0 copy-start.5
  2.5 7.3 %all-to-all-start = ((bf16[32,4,512]{2,1,0:T(4,128)(2,1)}), bf16[32,4,512]{2,1,0:T(4,128)(2,1)S(1)}, u32[]{:S(2)}, u32[]{:S(2)}) async-start(bf16[32,4,512]{2,1,0:T(4,128)(2,1)} %get-tuple-element.17), calls=%async_computation | async-start | bytes 262144 | tf_op jit(solution)/shard_map/all_to_all | solution.py:592
  10.4 0.0 copy-start.7
  10.5 0.0 copy-start.8
  10.5 0.0 copy-done.2
  10.5 0.0 copy-done.3
  10.5 0.0 copy-done.4
  10.5 0.0 copy-done.5
  10.5 0.6 %copy-done.7 = s32[1,1,4]{2,1,0:T(1,128)S(1)} copy-done((s32[1,1,4]{2,1,0:T(1,128)S(1)}, s32[1,1,4]{2,1,0:T(1,128)}, u32[]{:S(2)}) %copy-start.7) | copy-done | bytes 40
  11.1 0.0 copy-done.8
  11.1 0.0 copy-start
  11.1 1.0 %copy-done = bf16[1,1,4,256,256]{4,3,2,1,0:T(8,128)(2,1)S(1)} copy-done((bf16[1,1,4,256,256]{4,3,2,1,0:T(8,128)(2,1)S(1)}, bf16[1,1,4,256,256]{4,3,2,1,0:T(8,128)(2,1)}, u32[]{:S(2)}) %copy-start) | copy-done | bytes 524312
  12.2 0.0 copy-start.1
  12.2 0.9 %prepare.1 = (bf16[3,32,1536]{2,1,0:T(8,128)(2,1)S(1)}, bf16[4,256,256]{2,1,0:T(8,128)(2,1)S(1)}, bf16[512,256]{1,0:T(8,128)(2,1)S(1)}, f32[16,128]{1,0:T(8,128)S(1)}) custom-call(s32[1,1,4]{2,1,0:T(1,128)S(1)} %copy-done.7, s32[1,1]{1,0:T(1,128)S(6)} %copy.13.near_count_ref, s32[1,1,6]{2,1,0:T(1,128)S(1)} %copy-done.8, bf16[4,256,256]{2,1,0:T(8,128)(2,1)S(1)} %bitcast.13, ...), custom_call_target="tpu_custom_call" | custom-call | bytes 1048576 | tf_op jit(solution)/shard_map/prepare/pallas_call | solution.py:579
  13.1 0.0 copy-start.6
  13.1 4.9 %all-to-all-done.arrived_ref = bf16[32,4,512]{2,1,0:T(4,128)(2,1)S(1)} async-done(((bf16[32,4,512]{2,1,0:T(4,128)(2,1)}), bf16[32,4,512]{2,1,0:T(4,128)(2,1)S(1)}, u32[]{:S(2)}, u32[]{:S(2)}) %all-to-all-start) | async-done | bytes 131104 | tf_op jit(solution)/shard_map/all_to_all | solution.py:592
  18.0 0.0 copy-done.1
  18.0 0.0 copy-done.6
  18.0 0.6 %first.1 = (f32[4,256]{1,0:T(4,128)S(1)}, f32[352,128]{1,0:T(8,128)S(1)}, f32[8,128]{1,0:T(8,128)S(1)}) custom-call(bf16[32,4,512]{2,1,0:T(4,128)(2,1)S(1)} %all-to-all-done.arrived_ref, f32[8,256]{1,0:T(8,128)S(1)} %copy-done.6, bf16[3,32,1536]{2,1,0:T(8,128)(2,1)S(1)} %get-tuple-element.19.weights_ref, ...), custom_call_target="tpu_custom_call" | custom-call | bytes 1048576 | tf_op jit(solution)/shard_map/first/pallas_call | solution.py:579
  18.6 10.4 %all_to_all.15.arrived_ref = f32[32,1,1408]{2,1,0:T(1,128)S(1)} all-to-all(f32[32,1,1408]{2,1,0:T(1,128)S(1)} %bitcast.15), channel_id=1, replica_groups=mesh['clus'=8,'lvl'=4] {'lvl','clus'}, dimensions={0} | all-to-all | bytes 360448 | tf_op jit(solution)/shard_map/all_to_all | solution.py:592
  29.0 0.6 %middle.1 = (f32[32,2,128]{2,1,0:T(2,128)S(1)}, f32[8,256]{1,0:T(8,128)S(1)}, f32[4,256]{1,0:T(4,128)S(1)}, f32[4,128]{1,0:T(4,128)S(1)}) custom-call(f32[32,1,1408]{2,1,0:T(1,128)S(1)} %all_to_all.15.arrived_ref, f32[352,128]{1,0:T(8,128)S(1)} %bitcast.12, f32[8,256]{1,0:T(8,128)S(1)} %copy-done.6, f32[4,256]{1,0:T(4,128)S(1)} %get-tuple-element.24.image_ref, ...), custom_call_target="tpu_custom_call" | custom-call | bytes 1048576 | tf_op jit(solution)/shard_map/middle/pallas_call | solution.py:579
  29.6 9.4 %all_to_all.16.arrived_ref = f32[32,2,128]{2,1,0:T(2,128)S(1)} all-to-all(f32[32,2,128]{2,1,0:T(2,128)S(1)} %get-tuple-element.26), channel_id=1, replica_groups=mesh['clus'=8,'lvl'=4] {'lvl','clus'}, dimensions={0} | all-to-all | bytes 65536 | tf_op jit(solution)/shard_map/all_to_all | solution.py:592
  39.0 1.0 %end.1 = (f32[8,128]{1,0:T(8,128)}, f32[2,4,12]{2,1,0:T(4,128)}) custom-call(f32[32,2,128]{2,1,0:T(2,128)S(1)} %all_to_all.16.arrived_ref, f32[64,128]{1,0:T(8,128)S(1)} %bitcast.14, f32[8,256]{1,0:T(8,128)S(1)} %get-tuple-element.27.window_ref, f32[4,256]{1,0:T(4,128)S(1)} %get-tuple-element.28.near_part_ref, ...), custom_call_target="tpu_custom_call" | custom-call | bytes 1048576 | tf_op jit(solution)/shard_map/end/pallas_call | solution.py:579
Async XLA Ops:
  2.4 8.1 %copy-start.2 = (f32[1,1,6,32,32]{4,3,2,1,0:T(8,128)S(1)}, f32[1,1,6,32,32]{4,3,2,1,0:T(8,128)}, u32[]{:S(2)}) copy-start(f32[1,1,6,32,32]{4,3,2,1,0:T(8,128)} %param.17) | copy-start | bytes 73732
  2.4 8.1 %copy-start.3 = (f32[1,1,4,32,32]{4,3,2,1,0:T(8,128)S(1)}, f32[1,1,4,32,32]{4,3,2,1,0:T(8,128)}, u32[]{:S(2)}) copy-start(f32[1,1,4,32,32]{4,3,2,1,0:T(8,128)} %param.19) | copy-start | bytes 49156
  2.4 8.1 %copy-start.4 = (bf16[1,1,32,256]{3,2,1,0:T(8,128)(2,1)S(1)}, bf16[1,1,32,256]{3,2,1,0:T(8,128)(2,1)}, u32[]{:S(2)}) copy-start(bf16[1,1,32,256]{3,2,1,0:T(8,128)(2,1)} %param.15) | copy-start | bytes 49156
  2.4 8.1 %copy-start.5 = (f32[1,1,32,32]{3,2,1,0:T(8,128)S(1)}, f32[1,1,32,32]{3,2,1,0:T(8,128)}, u32[]{:S(2)}) copy-start(f32[1,1,32,32]{3,2,1,0:T(8,128)} %param.18) | copy-start | bytes 12292
  2.5 15.5 %all-to-all-start = ((bf16[32,4,512]{2,1,0:T(4,128)(2,1)}), bf16[32,4,512]{2,1,0:T(4,128)(2,1)S(1)}, u32[]{:S(2)}, u32[]{:S(2)}) async-start(bf16[32,4,512]{2,1,0:T(4,128)(2,1)} %get-tuple-element.17), calls=%async_computation | async-start | bytes 262144 | tf_op jit(solution)/shard_map/all_to_all | solution.py:592
  10.4 0.7 %copy-start.7 = (s32[1,1,4]{2,1,0:T(1,128)S(1)}, s32[1,1,4]{2,1,0:T(1,128)}, u32[]{:S(2)}) copy-start(s32[1,1,4]{2,1,0:T(1,128)} %near_col_ref.1) | copy-start | bytes 52
  10.5 0.7 %copy-start.8 = (s32[1,1,6]{2,1,0:T(1,128)S(1)}, s32[1,1,6]{2,1,0:T(1,128)}, u32[]{:S(2)}) copy-start(s32[1,1,6]{2,1,0:T(1,128)} %far_col_ref.1) | copy-start | bytes 76
  11.1 1.0 %copy-start = (bf16[1,1,4,256,256]{4,3,2,1,0:T(8,128)(2,1)S(1)}, bf16[1,1,4,256,256]{4,3,2,1,0:T(8,128)(2,1)}, u32[]{:S(2)}) copy-start(bf16[1,1,4,256,256]{4,3,2,1,0:T(8,128)(2,1)} %param.11) | copy-start | bytes 1572868
  12.2 5.8 %copy-start.1 = (bf16[1,1,32,256]{3,2,1,0:T(8,128)(2,1)S(1)}, bf16[1,1,32,256]{3,2,1,0:T(8,128)(2,1)}, u32[]{:S(2)}) copy-start(bf16[1,1,32,256]{3,2,1,0:T(8,128)(2,1)} %param.16) | copy-start | bytes 49156
  13.1 4.9 %copy-start.6 = (f32[8,256]{1,0:T(8,128)S(1)}, f32[8,256]{1,0:T(8,128)}, u32[]{:S(2)}) copy-start(f32[8,256]{1,0:T(8,128)} %get-tuple-element.18.window_ref) | copy-start | bytes 24580

commit v8 on v7

--- a/solution.py
+++ b/solution.py
@@ -120,7 +120,10 @@
     rows = row_groups(rows_dot(parts, wide_basis))
     skeletons = jnp.concatenate([rows[0], rows[1] + rows[2] + rows[3], rows[4] + rows[5]], axis=0)
     wide_transfer = jnp.concatenate([transfer_ref[...]] * repeats, axis=1)
-    coarse = precise_dot(skeletons[:, :rank], wide_transfer)
+    wide_transfer = jnp.concatenate(three_parts(wide_transfer), axis=1)
+    wide_transfer = jnp.concatenate([wide_transfer] * repeats, axis=0)
+    split = lane_parts(skeletons, lanes_of(skeletons.shape) // rank).astype(BF16)
+    coarse = sum(lane_tiles(jnp.dot(split, wide_transfer, preferred_element_type=F32)))
     own_tree = lax.axis_index("lvl")
 
     def tails(values):
@@ -186,14 +189,16 @@
     far_slots = far_coupling_ref.shape[0]
     trees, rank = top_ref.shape[0], top_ref.shape[1]
     transfer = transfer_ref[...]
-    for slot in range(leaves + trees):
-        if slot < leaves:
+    own_leaf = lax.axis_index("clus")
+    for slot in range(leaves + trees - 2):
+        if slot < leaves - 1:
+            leaf = lax.rem(own_leaf + 1 + slot, jnp.int32(leaves))
             block = jnp.zeros((rank, rank), F32)
             for at in range(far_slots):
-                block = block + jnp.where(far_col_ref[0, 0, at] == slot, far_coupling_ref[at], 0.0)
+                block = block + jnp.where(far_col_ref[0, 0, at] == leaf, far_coupling_ref[at], 0.0)
         else:
-            tree = slot - leaves
-            block = precise_dot(transfer, jnp.where(tree != own_tree, top_ref[tree], 0.0))
+            tree = lax.rem(own_tree + 2 + slot - leaves, jnp.int32(trees))
+            block = precise_dot(transfer, top_ref[tree])
         wide = jnp.concatenate([block] * (LANES // rank), axis=1)
         for part, piece in enumerate(three_parts(wide)):
             weights_ref[part, :, slot * LANES : (slot + 1) * LANES] = piece
@@ -202,7 +207,6 @@
     for part, piece in enumerate((v_basis, *three_parts(carried))):
         for at in range(part * LANES, (part + 1) * LANES, rank):
             maps_ref[at : at + rank] = piece
-    own_leaf = lax.axis_index("clus")
     count = near_count_ref[0, 0]
     rows = lax.broadcasted_iota(jnp.int32, choice_ref.shape, 0)
     choice = jnp.zeros(choice_ref.shape, F32)
@@ -217,8 +221,10 @@
 def places_of(leaves, trees):
     own_tree = lax.axis_index("lvl")
     own_leaf = lax.axis_index("clus")
-    places = [own_tree * leaves + leaf for leaf in range(leaves)]
-    return places + [tree * leaves + own_leaf for tree in range(trees)]
+    others = [lax.rem(own_leaf + 1 + at, jnp.int32(leaves)) for at in range(leaves - 1)]
+    places = [own_tree * leaves + leaf for leaf in others]
+    others = [lax.rem(own_tree + 1 + at, jnp.int32(trees)) for at in range(trees - 1)]
+    return places + [tree * leaves + own_leaf for tree in others]
 
 
 def near_places(leaves):
@@ -619,7 +625,7 @@
     record_like = ((VECS, LANES), F32)
     maps_like = ((4 * LANES, size), BF16)
     choice_like = ((-(-3 * near_own.shape[0] // 8) * 8, LANES), F32)
-    weights_like = ((3, rank, (leaves + trees) * LANES), BF16)
+    weights_like = ((3, rank, (leaves + trees - 2) * LANES), BF16)
     slots, window = call(
         functools.partial(begin_kernel, leaves),
         "begin",

time: 40.4 us -> 40.4 us (level)
  no operation moved by 1% of the time
where the time goes in v8:
time: 40.4 us; the launch traced here: 40 us
  blocking collectives  19.8 us (49%)
  starting transfers between devices  7.33 us (18%)
  waiting for transfers between devices  4.89 us (12%)
  Pallas kernels  4.83 us (12%)
  local copies, waits for them, and re-layouts  1.69 us (4%)
  between operations  1.41 us (3%)
    all_to_all x2, blocking collectives, exchange(): return lax.all_to_all(slots, AXES, 0, 0, tiled=True)  19.8 us
    all_to_all x1, starting transfers between devices, exchange(): return lax.all_to_all(slots, AXES, 0, 0, tiled=True)  7.33 us
    all_to_all x1, waiting for transfers between devices, exchange(): return lax.all_to_all(slots, AXES, 0, 0, tiled=True)  4.89 us
    pallas_call x5, Pallas kernels, call(): pl.pallas_call(kernel, name=name, out_shape=[jax.ShapeDtypeStruct(shape,...  4.83 us
    unnamed x18, local copies, waits for them, and re-layouts  1.69 us
  transfers between devices with their start and end apart: 1, of which 1 were waited for; matrix products, arithmetic and copies ran while one was open for 0% of the time, Pallas kernels for 2%

profile of v8, /device:TPU:0, one launch (start us, length us, event | category | flops | bytes accessed | tf_op | source)
XLA Modules:
  0.0 40.0 jit_solution(18022677276471390769)
XLA Ops:
  0.6 1.8 %begin.1 = (bf16[32,4,512]{2,1,0:T(4,128)(2,1)}, f32[8,256]{1,0:T(8,128)}) custom-call(f32[16,128]{1,0:T(8,128)} %bitcast.25, bf16[32,256]{1,0:T(8,128)(2,1)} %bitcast.21, f32[32,32]{1,0:T(8,128)} %bitcast.23), custom_call_target="tpu_custom_call" | custom-call | bytes 1048576 | tf_op jit(solution)/shard_map/begin/pallas_call | solution.py:585
  2.4 0.0 copy-start.2
  2.4 0.0 copy-start.3
  2.4 0.0 copy-start.4
  2.4 0.0 copy-start.5
  2.5 7.3 %all-to-all-start = ((bf16[32,4,512]{2,1,0:T(4,128)(2,1)}), bf16[32,4,512]{2,1,0:T(4,128)(2,1)S(1)}, u32[]{:S(2)}, u32[]{:S(2)}) async-start(bf16[32,4,512]{2,1,0:T(4,128)(2,1)} %get-tuple-element.17), calls=%async_computation | async-start | bytes 262144 | tf_op jit(solution)/shard_map/all_to_all | solution.py:598
  10.4 0.0 copy-start.7
  10.5 0.0 copy-start.8
  10.5 0.0 copy-done.2
  10.5 0.0 copy-done.3
  10.5 0.0 copy-done.4
  10.5 0.0 copy-done.5
  10.5 0.6 %copy-done.7 = s32[1,1,4]{2,1,0:T(1,128)S(1)} copy-done((s32[1,1,4]{2,1,0:T(1,128)S(1)}, s32[1,1,4]{2,1,0:T(1,128)}, u32[]{:S(2)}) %copy-start.7) | copy-done | bytes 40
  11.1 0.0 copy-done.8
  11.1 0.0 copy-start
  11.1 1.0 %copy-done = bf16[1,1,4,256,256]{4,3,2,1,0:T(8,128)(2,1)S(1)} copy-done((bf16[1,1,4,256,256]{4,3,2,1,0:T(8,128)(2,1)S(1)}, bf16[1,1,4,256,256]{4,3,2,1,0:T(8,128)(2,1)}, u32[]{:S(2)}) %copy-start) | copy-done | bytes 524312
  12.2 0.0 copy-start.1
  12.2 0.9 %prepare.1 = (bf16[3,32,1280]{2,1,0:T(8,128)(2,1)S(1)}, bf16[4,256,256]{2,1,0:T(8,128)(2,1)S(1)}, bf16[512,256]{1,0:T(8,128)(2,1)S(1)}, f32[16,128]{1,0:T(8,128)S(1)}) custom-call(s32[1,1,4]{2,1,0:T(1,128)S(1)} %copy-done.7, s32[1,1]{1,0:T(1,128)S(6)} %copy.13.near_count_ref, s32[1,1,6]{2,1,0:T(1,128)S(1)} %copy-done.8, bf16[4,256,256]{2,1,0:T(8,128)(2,1)S(1)} %bitcast.13, ...), custom_call_target="tpu_custom_call" | custom-call | bytes 1048576 | tf_op jit(solution)/shard_map/prepare/pallas_call | solution.py:585
  13.1 0.0 copy-start.6
  13.1 4.9 %all-to-all-done.arrived_ref = bf16[32,4,512]{2,1,0:T(4,128)(2,1)S(1)} async-done(((bf16[32,4,512]{2,1,0:T(4,128)(2,1)}), bf16[32,4,512]{2,1,0:T(4,128)(2,1)S(1)}, u32[]{:S(2)}, u32[]{:S(2)}) %all-to-all-start) | async-done | bytes 131104 | tf_op jit(solution)/shard_map/all_to_all | solution.py:598
  18.0 0.0 copy-done.1
  18.0 0.0 copy-done.6
  18.0 0.6 %first.1 = (f32[4,256]{1,0:T(4,128)S(1)}, f32[352,128]{1,0:T(8,128)S(1)}, f32[8,128]{1,0:T(8,128)S(1)}) custom-call(bf16[32,4,512]{2,1,0:T(4,128)(2,1)S(1)} %all-to-all-done.arrived_ref, f32[8,256]{1,0:T(8,128)S(1)} %copy-done.6, bf16[3,32,1280]{2,1,0:T(8,128)(2,1)S(1)} %get-tuple-element.19.weights_ref, ...), custom_call_target="tpu_custom_call" | custom-call | bytes 1048576 | tf_op jit(solution)/shard_map/first/pallas_call | solution.py:585
  18.6 10.4 %all_to_all.15.arrived_ref = f32[32,1,1408]{2,1,0:T(1,128)S(1)} all-to-all(f32[32,1,1408]{2,1,0:T(1,128)S(1)} %bitcast.15), channel_id=1, replica_groups=mesh['clus'=8,'lvl'=4] {'lvl','clus'}, dimensions={0} | all-to-all | bytes 360448 | tf_op jit(solution)/shard_map/all_to_all | solution.py:598
  29.0 0.6 %middle.1 = (f32[32,2,128]{2,1,0:T(2,128)S(1)}, f32[8,256]{1,0:T(8,128)S(1)}, f32[4,256]{1,0:T(4,128)S(1)}, f32[4,128]{1,0:T(4,128)S(1)}) custom-call(f32[32,1,1408]{2,1,0:T(1,128)S(1)} %all_to_all.15.arrived_ref, f32[352,128]{1,0:T(8,128)S(1)} %bitcast.12, f32[8,256]{1,0:T(8,128)S(1)} %copy-done.6, f32[4,256]{1,0:T(4,128)S(1)} %get-tuple-element.24.image_ref, ...), custom_call_target="tpu_custom_call" | custom-call | bytes 1048576 | tf_op jit(solution)/shard_map/middle/pallas_call | solution.py:585
  29.6 9.4 %all_to_all.16.arrived_ref = f32[32,2,128]{2,1,0:T(2,128)S(1)} all-to-all(f32[32,2,128]{2,1,0:T(2,128)S(1)} %get-tuple-element.26), channel_id=1, replica_groups=mesh['clus'=8,'lvl'=4] {'lvl','clus'}, dimensions={0} | all-to-all | bytes 65536 | tf_op jit(solution)/shard_map/all_to_all | solution.py:598
  39.0 1.0 %end.1 = (f32[8,128]{1,0:T(8,128)}, f32[2,4,12]{2,1,0:T(4,128)}) custom-call(f32[32,2,128]{2,1,0:T(2,128)S(1)} %all_to_all.16.arrived_ref, f32[64,128]{1,0:T(8,128)S(1)} %bitcast.14, f32[8,256]{1,0:T(8,128)S(1)} %get-tuple-element.27.window_ref, f32[4,256]{1,0:T(4,128)S(1)} %get-tuple-element.28.near_part_ref, ...), custom_call_target="tpu_custom_call" | custom-call | bytes 1048576 | tf_op jit(solution)/shard_map/end/pallas_call | solution.py:585
Async XLA Ops:
  2.4 8.1 %copy-start.2 = (f32[1,1,6,32,32]{4,3,2,1,0:T(8,128)S(1)}, f32[1,1,6,32,32]{4,3,2,1,0:T(8,128)}, u32[]{:S(2)}) copy-start(f32[1,1,6,32,32]{4,3,2,1,0:T(8,128)} %param.17) | copy-start | bytes 73732
  2.4 8.1 %copy-start.3 = (f32[1,1,4,32,32]{4,3,2,1,0:T(8,128)S(1)}, f32[1,1,4,32,32]{4,3,2,1,0:T(8,128)}, u32[]{:S(2)}) copy-start(f32[1,1,4,32,32]{4,3,2,1,0:T(8,128)} %param.19) | copy-start | bytes 49156
  2.4 8.1 %copy-start.4 = (bf16[1,1,32,256]{3,2,1,0:T(8,128)(2,1)S(1)}, bf16[1,1,32,256]{3,2,1,0:T(8,128)(2,1)}, u32[]{:S(2)}) copy-start(bf16[1,1,32,256]{3,2,1,0:T(8,128)(2,1)} %param.15) | copy-start | bytes 49156
  2.4 8.1 %copy-start.5 = (f32[1,1,32,32]{3,2,1,0:T(8,128)S(1)}, f32[1,1,32,32]{3,2,1,0:T(8,128)}, u32[]{:S(2)}) copy-start(f32[1,1,32,32]{3,2,1,0:T(8,128)} %param.18) | copy-start | bytes 12292
  2.5 15.5 %all-to-all-start = ((bf16[32,4,512]{2,1,0:T(4,128)(2,1)}), bf16[32,4,512]{2,1,0:T(4,128)(2,1)S(1)}, u32[]{:S(2)}, u32[]{:S(2)}) async-start(bf16[32,4,512]{2,1,0:T(4,128)(2,1)} %get-tuple-element.17), calls=%async_computation | async-start | bytes 262144 | tf_op jit(solution)/shard_map/all_to_all | solution.py:598
  10.4 0.7 %copy-start.7 = (s32[1,1,4]{2,1,0:T(1,128)S(1)}, s32[1,1,4]{2,1,0:T(1,128)}, u32[]{:S(2)}) copy-start(s32[1,1,4]{2,1,0:T(1,128)} %near_col_ref.1) | copy-start | bytes 52
  10.5 0.7 %copy-start.8 = (s32[1,1,6]{2,1,0:T(1,128)S(1)}, s32[1,1,6]{2,1,0:T(1,128)}, u32[]{:S(2)}) copy-start(s32[1,1,6]{2,1,0:T(1,128)} %far_col_ref.1) | copy-start | bytes 76
  11.1 1.0 %copy-start = (bf16[1,1,4,256,256]{4,3,2,1,0:T(8,128)(2,1)S(1)}, bf16[1,1,4,256,256]{4,3,2,1,0:T(8,128)(2,1)}, u32[]{:S(2)}) copy-start(bf16[1,1,4,256,256]{4,3,2,1,0:T(8,128)(2,1)} %param.11) | copy-start | bytes 1572868
  12.2 5.8 %copy-start.1 = (bf16[1,1,32,256]{3,2,1,0:T(8,128)(2,1)S(1)}, bf16[1,1,32,256]{3,2,1,0:T(8,128)(2,1)}, u32[]{:S(2)}) copy-start(bf16[1,1,32,256]{3,2,1,0:T(8,128)(2,1)} %param.16) | copy-start | bytes 49156
  13.1 4.9 %copy-start.6 = (f32[8,256]{1,0:T(8,128)S(1)}, f32[8,256]{1,0:T(8,128)}, u32[]{:S(2)}) copy-start(f32[8,256]{1,0:T(8,128)} %get-tuple-element.18.window_ref) | copy-start | bytes 24580

commit v9 on v8

--- a/solution.py
+++ b/solution.py
@@ -94,7 +94,7 @@
     return replicated(jnp.sum(sum(left * right for left, right in pairs), axis=1, keepdims=True))
 
 
-def begin_kernel(leaves, basis_hbm, v_hbm, transfer_hbm, slots_ref, window_ref, *scratch):
+def begin_kernel(leaves, basis_hbm, v_hbm, transfer_hbm, slots_ref, *scratch):
     basis_ref, v_ref, transfer_ref, sems = scratch
     copies = [
         pltpu.make_async_copy(source, target, sems.at[at])
@@ -106,10 +106,9 @@
         copy.start()
     for copy in copies:
         copy.wait()
-    basis, size = window_ref.shape
-    rank = v_ref.shape[0]
+    rank, size = v_ref.shape
+    basis = basis_ref.shape[0] * LANES // size
     window = split_rows(basis_ref, basis)
-    window_ref[...] = window
     current = window[basis - VECS :]
     lowered = current.astype(BF16)
     rest = current - lowered.astype(F32)
@@ -305,7 +304,7 @@
 def first_kernel(
     trees,
     arrived_ref,
-    window_ref,
+    basis_ref,
     weights_ref,
     near_ref,
     choice_ref,
@@ -336,7 +335,7 @@
     image = image + near_field(blocks, choice_ref, near_ref)
     image_ref[...] = image
     width = LANES // VECS
-    packed = one_row(product_lanes(window_ref[...], image, width))
+    packed = one_row(product_lanes(split_rows(basis_ref, window_coupled_ref.shape[0]), image, width))
     parts = [part.astype(F32) for part in three_parts(image)]
     skeleton, coarse = mapped(jnp.concatenate(parts, axis=0).astype(BF16), maps_ref)
     tree_row, level_row = one_row(skeleton), one_row(coarse)
@@ -389,7 +388,7 @@
         lax.fori_loop(0, total // step, body, 0)
 
 
-def orthogonalized(total, windows, images):
+def orthogonalized(total, windows, images, more=()):
     basis = windows[0].shape[0]
     shape = (VECS, LANES)
     row, lane = lax.broadcasted_iota(jnp.int32, shape, 0), lanes_of(shape)
@@ -421,6 +420,7 @@
         for b in range(basis):
             image = image - projection[b] * window[b : b + 1]
         remainders.append(image)
+    remainders = [sum(pair) for pair in zip(remainders, more)] if more else remainders
     record = jnp.zeros(shape, F32)
     for b in range(basis):
         record = jnp.where(lane == b, projection[b], record)
@@ -442,7 +442,7 @@
     rows_all,
     arrived_ref,
     flat_ref,
-    window_ref,
+    basis_ref,
     image_ref,
     window_coupled_ref,
     weights_ref,
@@ -456,8 +456,8 @@
     record_ref,
 ):
     own_tree = lax.axis_index("lvl")
-    window = window_ref[...]
-    basis, size = window.shape
+    basis, size = next_window_ref.shape
+    window = split_rows(basis_ref, basis)
     rank = u_ref.shape[0]
     lane = lanes_of((VECS, LANES))
     slots = arrived_ref.shape[0]
@@ -572,8 +572,12 @@
         total = total + flat_ref[at : at + step]
     total = sum(total[at : at + 1] for at in range(1, step, step // VECS))
     total = total * (1.0 / rows_all)
-    image = near_part_ref[...] + far_part
-    solved, record = orthogonalized(total, lane_tiles(window_ref[...]), lane_tiles(image))
+    solved, record = orthogonalized(
+        total,
+        lane_tiles(window_ref[...]),
+        lane_tiles(near_part_ref[...]),
+        lane_tiles(far_part),
+    )
     store_rows(block_ref, jnp.concatenate(solved, axis=1))
     used = records_ref.shape[2]
     records_ref[0] = first_ref[:, :used]
@@ -626,10 +630,10 @@
     maps_like = ((4 * LANES, size), BF16)
     choice_like = ((-(-3 * near_own.shape[0] // 8) * 8, LANES), F32)
     weights_like = ((3, rank, (leaves + trees - 2) * LANES), BF16)
-    slots, window = call(
+    (slots,) = call(
         functools.partial(begin_kernel, leaves),
         "begin",
-        [((devices, VECS, size + 2 * LANES), BF16), window_like],
+        [((devices, VECS, size + 2 * LANES), BF16)],
         [flat_basis, v_own, transfer_own],
         "hhh",
         [
@@ -655,7 +659,7 @@
         [image_like, ((devices * per_slot, LANES), F32), ((basis, LANES), F32)],
         [
             arrived,
-            window,
+            flat_basis,
             weights,
             near_here,
             choice,
@@ -672,7 +676,7 @@
         [
             arrived,
             arrived.reshape(-1, LANES),
-            window,
+            flat_basis,
             image,
             window_coupled,
             weights,

time: 40.4 us -> 40.4 us (level)
  no operation moved by 1% of the time
where the time goes in v9:
time: 40.4 us; the launch traced here: 39.9 us
  blocking collectives  19.8 us (49%)
  starting transfers between devices  7.33 us (18%)
  waiting for transfers between devices  4.89 us (12%)
  Pallas kernels  4.8 us (12%)
  local copies, waits for them, and re-layouts  1.69 us (4%)
  between operations  1.41 us (3%)
    all_to_all x2, blocking collectives, exchange(): return lax.all_to_all(slots, AXES, 0, 0, tiled=True)  19.8 us
    all_to_all x1, starting transfers between devices, exchange(): return lax.all_to_all(slots, AXES, 0, 0, tiled=True)  7.33 us
    all_to_all x1, waiting for transfers between devices, exchange(): return lax.all_to_all(slots, AXES, 0, 0, tiled=True)  4.89 us
    pallas_call x5, Pallas kernels, call(): pl.pallas_call(kernel, name=name, out_shape=[jax.ShapeDtypeStruct(shape,...  4.8 us
    unnamed x18, local copies, waits for them, and re-layouts  1.69 us
  transfers between devices with their start and end apart: 1, of which 1 were waited for; matrix products, arithmetic and copies ran while one was open for 0% of the time, Pallas kernels for 2%

profile of v9, /device:TPU:0, one launch (start us, length us, event | category | flops | bytes accessed | tf_op | source)
XLA Modules:
  0.0 39.9 jit_solution(15053914314493347408)
XLA Ops:
  0.6 1.8 %begin.1 = bf16[32,4,512]{2,1,0:T(4,128)(2,1)} custom-call(f32[16,128]{1,0:T(8,128)} %bitcast.20, bf16[32,256]{1,0:T(8,128)(2,1)} %bitcast.24, f32[32,32]{1,0:T(8,128)} %bitcast.26), custom_call_target="tpu_custom_call" | custom-call | bytes 1048576 | tf_op jit(solution)/shard_map/begin/pallas_call | solution.py:589
  2.4 0.0 copy-start.2
  2.4 0.0 copy-start.4
  2.4 0.0 copy-start.5
  2.4 0.0 copy-start.6
  2.4 7.3 %all-to-all-start = ((bf16[32,4,512]{2,1,0:T(4,128)(2,1)}), bf16[32,4,512]{2,1,0:T(4,128)(2,1)S(1)}, u32[]{:S(2)}, u32[]{:S(2)}) async-start(bf16[32,4,512]{2,1,0:T(4,128)(2,1)} %begin.1), calls=%async_computation | async-start | bytes 262144 | tf_op jit(solution)/shard_map/all_to_all | solution.py:602
  10.4 0.0 copy-start.7
  10.4 0.0 copy-start.8
  10.5 0.0 copy-done.2
  10.5 0.0 copy-done.4
  10.5 0.0 copy-done.5
  10.5 0.0 copy-done.6
  10.5 0.6 %copy-done.7 = s32[1,1,4]{2,1,0:T(1,128)S(1)} copy-done((s32[1,1,4]{2,1,0:T(1,128)S(1)}, s32[1,1,4]{2,1,0:T(1,128)}, u32[]{:S(2)}) %copy-start.7) | copy-done | bytes 40
  11.1 0.0 copy-done.8
  11.1 0.0 copy-start
  11.1 1.0 %copy-done = bf16[1,1,4,256,256]{4,3,2,1,0:T(8,128)(2,1)S(1)} copy-done((bf16[1,1,4,256,256]{4,3,2,1,0:T(8,128)(2,1)S(1)}, bf16[1,1,4,256,256]{4,3,2,1,0:T(8,128)(2,1)}, u32[]{:S(2)}) %copy-start) | copy-done | bytes 524312
  12.2 0.0 copy-start.1
  12.2 0.9 %prepare.1 = (bf16[3,32,1280]{2,1,0:T(8,128)(2,1)S(1)}, bf16[4,256,256]{2,1,0:T(8,128)(2,1)S(1)}, bf16[512,256]{1,0:T(8,128)(2,1)S(1)}, f32[16,128]{1,0:T(8,128)S(1)}) custom-call(s32[1,1,4]{2,1,0:T(1,128)S(1)} %copy-done.7, s32[1,1]{1,0:T(1,128)S(6)} %copy.13.near_count_ref, s32[1,1,6]{2,1,0:T(1,128)S(1)} %copy-done.8, bf16[4,256,256]{2,1,0:T(8,128)(2,1)S(1)} %bitcast.13, ...), custom_call_target="tpu_custom_call" | custom-call | bytes 1048576 | tf_op jit(solution)/shard_map/prepare/pallas_call | solution.py:589
  13.0 0.0 copy-start.3
  13.1 4.9 %all-to-all-done.arrived_ref = bf16[32,4,512]{2,1,0:T(4,128)(2,1)S(1)} async-done(((bf16[32,4,512]{2,1,0:T(4,128)(2,1)}), bf16[32,4,512]{2,1,0:T(4,128)(2,1)S(1)}, u32[]{:S(2)}, u32[]{:S(2)}) %all-to-all-start) | async-done | bytes 131104 | tf_op jit(solution)/shard_map/all_to_all | solution.py:602
  17.9 0.0 copy-done.1
  17.9 0.0 copy-done.3
  18.0 0.6 %first.1 = (f32[4,256]{1,0:T(4,128)S(1)}, f32[352,128]{1,0:T(8,128)S(1)}, f32[8,128]{1,0:T(8,128)S(1)}) custom-call(bf16[32,4,512]{2,1,0:T(4,128)(2,1)S(1)} %all-to-all-done.arrived_ref, f32[16,128]{1,0:T(8,128)S(1)} %bitcast.21, bf16[3,32,1280]{2,1,0:T(8,128)(2,1)S(1)} %get-tuple-element.15.weights_ref, ...), custom_call_target="tpu_custom_call" | custom-call | bytes 1048576 | tf_op jit(solution)/shard_map/first/pallas_call | solution.py:589
  18.6 10.4 %all_to_all.15.arrived_ref = f32[32,1,1408]{2,1,0:T(1,128)S(1)} all-to-all(f32[32,1,1408]{2,1,0:T(1,128)S(1)} %bitcast.15), channel_id=1, replica_groups=mesh['clus'=8,'lvl'=4] {'lvl','clus'}, dimensions={0} | all-to-all | bytes 360448 | tf_op jit(solution)/shard_map/all_to_all | solution.py:602
  28.9 0.6 %middle.1 = (f32[32,2,128]{2,1,0:T(2,128)S(1)}, f32[8,256]{1,0:T(8,128)S(1)}, f32[4,256]{1,0:T(4,128)S(1)}, f32[4,128]{1,0:T(4,128)S(1)}) custom-call(f32[32,1,1408]{2,1,0:T(1,128)S(1)} %all_to_all.15.arrived_ref, f32[352,128]{1,0:T(8,128)S(1)} %bitcast.12, f32[16,128]{1,0:T(8,128)S(1)} %bitcast.22, f32[4,256]{1,0:T(4,128)S(1)} %get-tuple-element.20.image_ref, ...), custom_call_target="tpu_custom_call" | custom-call | bytes 1048576 | tf_op jit(solution)/shard_map/middle/pallas_call | solution.py:589
  29.5 9.4 %all_to_all.16.arrived_ref = f32[32,2,128]{2,1,0:T(2,128)S(1)} all-to-all(f32[32,2,128]{2,1,0:T(2,128)S(1)} %get-tuple-element.22), channel_id=1, replica_groups=mesh['clus'=8,'lvl'=4] {'lvl','clus'}, dimensions={0} | all-to-all | bytes 65536 | tf_op jit(solution)/shard_map/all_to_all | solution.py:602
  39.0 1.0 %end.1 = (f32[8,128]{1,0:T(8,128)}, f32[2,4,12]{2,1,0:T(4,128)}) custom-call(f32[32,2,128]{2,1,0:T(2,128)S(1)} %all_to_all.16.arrived_ref, f32[64,128]{1,0:T(8,128)S(1)} %bitcast.14, f32[8,256]{1,0:T(8,128)S(1)} %get-tuple-element.23.window_ref, f32[4,256]{1,0:T(4,128)S(1)} %get-tuple-element.24.near_part_ref, ...), custom_call_target="tpu_custom_call" | custom-call | bytes 1048576 | tf_op jit(solution)/shard_map/end/pallas_call | solution.py:589
Async XLA Ops:
  2.4 8.1 %copy-start.2 = (f32[1,1,6,32,32]{4,3,2,1,0:T(8,128)S(1)}, f32[1,1,6,32,32]{4,3,2,1,0:T(8,128)}, u32[]{:S(2)}) copy-start(f32[1,1,6,32,32]{4,3,2,1,0:T(8,128)} %param.17) | copy-start | bytes 73732
  2.4 8.1 %copy-start.4 = (f32[1,1,4,32,32]{4,3,2,1,0:T(8,128)S(1)}, f32[1,1,4,32,32]{4,3,2,1,0:T(8,128)}, u32[]{:S(2)}) copy-start(f32[1,1,4,32,32]{4,3,2,1,0:T(8,128)} %param.19) | copy-start | bytes 49156
  2.4 8.1 %copy-start.5 = (bf16[1,1,32,256]{3,2,1,0:T(8,128)(2,1)S(1)}, bf16[1,1,32,256]{3,2,1,0:T(8,128)(2,1)}, u32[]{:S(2)}) copy-start(bf16[1,1,32,256]{3,2,1,0:T(8,128)(2,1)} %param.15) | copy-start | bytes 49156
  2.4 8.1 %copy-start.6 = (f32[1,1,32,32]{3,2,1,0:T(8,128)S(1)}, f32[1,1,32,32]{3,2,1,0:T(8,128)}, u32[]{:S(2)}) copy-start(f32[1,1,32,32]{3,2,1,0:T(8,128)} %param.18) | copy-start | bytes 12292
  2.4 15.5 %all-to-all-start = ((bf16[32,4,512]{2,1,0:T(4,128)(2,1)}), bf16[32,4,512]{2,1,0:T(4,128)(2,1)S(1)}, u32[]{:S(2)}, u32[]{:S(2)}) async-start(bf16[32,4,512]{2,1,0:T(4,128)(2,1)} %begin.1), calls=%async_computation | async-start | bytes 262144 | tf_op jit(solution)/shard_map/all_to_all | solution.py:602
  10.4 0.7 %copy-start.7 = (s32[1,1,4]{2,1,0:T(1,128)S(1)}, s32[1,1,4]{2,1,0:T(1,128)}, u32[]{:S(2)}) copy-start(s32[1,1,4]{2,1,0:T(1,128)} %near_col_ref.1) | copy-start | bytes 52
  10.4 0.7 %copy-start.8 = (s32[1,1,6]{2,1,0:T(1,128)S(1)}, s32[1,1,6]{2,1,0:T(1,128)}, u32[]{:S(2)}) copy-start(s32[1,1,6]{2,1,0:T(1,128)} %far_col_ref.1) | copy-start | bytes 76
  11.1 1.0 %copy-start = (bf16[1,1,4,256,256]{4,3,2,1,0:T(8,128)(2,1)S(1)}, bf16[1,1,4,256,256]{4,3,2,1,0:T(8,128)(2,1)}, u32[]{:S(2)}) copy-start(bf16[1,1,4,256,256]{4,3,2,1,0:T(8,128)(2,1)} %param.11) | copy-start | bytes 1572868
  12.2 5.8 %copy-start.1 = (bf16[1,1,32,256]{3,2,1,0:T(8,128)(2,1)S(1)}, bf16[1,1,32,256]{3,2,1,0:T(8,128)(2,1)}, u32[]{:S(2)}) copy-start(bf16[1,1,32,256]{3,2,1,0:T(8,128)(2,1)} %param.16) | copy-start | bytes 49156
  13.0 4.9 %copy-start.3 = (f32[8,1,256]{2,1,0:T(1,128)S(1)}, f32[8,1,256]{2,1,0:T(1,128)}, u32[]{:S(2)}) copy-start(f32[8,1,256]{2,1,0:T(1,128)} %param.10) | copy-start | bytes 24580

commit v10 on v9

--- a/solution.py
+++ b/solution.py
@@ -204,8 +204,7 @@
     v_basis = v_ref[...]
     carried = precise_dot(transfer.T, v_basis.astype(F32))
     for part, piece in enumerate((v_basis, *three_parts(carried))):
-        for at in range(part * LANES, (part + 1) * LANES, rank):
-            maps_ref[at : at + rank] = piece
+        maps_ref[part * rank : (part + 1) * rank] = piece
     count = near_count_ref[0, 0]
     rows = lax.broadcasted_iota(jnp.int32, choice_ref.shape, 0)
     choice = jnp.zeros(choice_ref.shape, F32)
@@ -296,9 +295,14 @@
 
 
 def mapped(rows, maps_ref):
-    products = lane_tiles(rows_dot(rows, maps_ref[...]))
-    skeleton, coarse = products[0], products[1] + products[2] + products[3]
-    return sum(row_groups(skeleton)), sum(row_groups(coarse))
+    products = sum(row_groups(rows_dot(rows, maps_ref[...])))
+    rank = maps_ref.shape[0] // 4
+    lane = lanes_of(products.shape) % rank
+    spread = [
+        jnp.take_along_axis(products, lane + part * rank, axis=1, mode="promise_in_bounds")
+        for part in range(4)
+    ]
+    return spread[0], spread[1] + spread[2] + spread[3]
 
 
 def first_kernel(
@@ -627,7 +631,7 @@
     window_like = ((basis, size), F32)
     per_slot = VECS * size // LANES + 3
     record_like = ((VECS, LANES), F32)
-    maps_like = ((4 * LANES, size), BF16)
+    maps_like = ((4 * rank, size), BF16)
     choice_like = ((-(-3 * near_own.shape[0] // 8) * 8, LANES), F32)
     weights_like = ((3, rank, (leaves + trees - 2) * LANES), BF16)
     (slots,) = call(

time: 40.4 us -> 40.3 us (level)
  no operation moved by 1% of the time
where the time goes in v10:
time: 40.3 us; the launch traced here: 39.9 us
  blocking collectives  19.8 us (49%)
  starting transfers between devices  7.33 us (18%)
  waiting for transfers between devices  4.89 us (12%)
  Pallas kernels  4.71 us (12%)
  local copies, waits for them, and re-layouts  1.69 us (4%)
  between operations  1.41 us (3%)
    all_to_all x2, blocking collectives, exchange(): return lax.all_to_all(slots, AXES, 0, 0, tiled=True)  19.8 us
    all_to_all x1, starting transfers between devices, exchange(): return lax.all_to_all(slots, AXES, 0, 0, tiled=True)  7.33 us
    all_to_all x1, waiting for transfers between devices, exchange(): return lax.all_to_all(slots, AXES, 0, 0, tiled=True)  4.89 us
    pallas_call x5, Pallas kernels, call(): pl.pallas_call(kernel, name=name, out_shape=[jax.ShapeDtypeStruct(shape,...  4.71 us
    unnamed x18, local copies, waits for them, and re-layouts  1.69 us
  transfers between devices with their start and end apart: 1, of which 1 were waited for; matrix products, arithmetic and copies ran while one was open for 0% of the time, Pallas kernels for 2%

profile of v10, /device:TPU:0, one launch (start us, length us, event | category | flops | bytes accessed | tf_op | source)
XLA Modules:
  0.0 39.9 jit_solution(1686598168131843235)
XLA Ops:
  0.6 1.8 %begin.1 = bf16[32,4,512]{2,1,0:T(4,128)(2,1)} custom-call(f32[16,128]{1,0:T(8,128)} %bitcast.20, bf16[32,256]{1,0:T(8,128)(2,1)} %bitcast.24, f32[32,32]{1,0:T(8,128)} %bitcast.26), custom_call_target="tpu_custom_call" | custom-call | bytes 1048576 | tf_op jit(solution)/shard_map/begin/pallas_call | solution.py:593
  2.4 0.0 copy-start.2
  2.4 0.0 copy-start.4
  2.4 0.0 copy-start.5
  2.4 0.0 copy-start.6
  2.4 7.3 %all-to-all-start = ((bf16[32,4,512]{2,1,0:T(4,128)(2,1)}), bf16[32,4,512]{2,1,0:T(4,128)(2,1)S(1)}, u32[]{:S(2)}, u32[]{:S(2)}) async-start(bf16[32,4,512]{2,1,0:T(4,128)(2,1)} %begin.1), calls=%async_computation | async-start | bytes 262144 | tf_op jit(solution)/shard_map/all_to_all | solution.py:606
  10.4 0.0 copy-start.7
  10.4 0.0 copy-start.8
  10.5 0.0 copy-done.2
  10.5 0.0 copy-done.4
  10.5 0.0 copy-done.5
  10.5 0.0 copy-done.6
  10.5 0.6 %copy-done.7 = s32[1,1,4]{2,1,0:T(1,128)S(1)} copy-done((s32[1,1,4]{2,1,0:T(1,128)S(1)}, s32[1,1,4]{2,1,0:T(1,128)}, u32[]{:S(2)}) %copy-start.7) | copy-done | bytes 40
  11.1 0.0 copy-done.8
  11.1 0.0 copy-start
  11.1 1.0 %copy-done = bf16[1,1,4,256,256]{4,3,2,1,0:T(8,128)(2,1)S(1)} copy-done((bf16[1,1,4,256,256]{4,3,2,1,0:T(8,128)(2,1)S(1)}, bf16[1,1,4,256,256]{4,3,2,1,0:T(8,128)(2,1)}, u32[]{:S(2)}) %copy-start) | copy-done | bytes 524312
  12.2 0.0 copy-start.1
  12.2 0.9 %prepare.1 = (bf16[3,32,1280]{2,1,0:T(8,128)(2,1)S(1)}, bf16[4,256,256]{2,1,0:T(8,128)(2,1)S(1)}, bf16[128,256]{1,0:T(8,128)(2,1)S(1)}, f32[16,128]{1,0:T(8,128)S(1)}) custom-call(s32[1,1,4]{2,1,0:T(1,128)S(1)} %copy-done.7, s32[1,1]{1,0:T(1,128)S(6)} %copy.13.near_count_ref, s32[1,1,6]{2,1,0:T(1,128)S(1)} %copy-done.8, bf16[4,256,256]{2,1,0:T(8,128)(2,1)S(1)} %bitcast.13, ...), custom_call_target="tpu_custom_call" | custom-call | bytes 1048576 | tf_op jit(solution)/shard_map/prepare/pallas_call | solution.py:593
  13.0 0.0 copy-start.3
  13.1 4.9 %all-to-all-done.arrived_ref = bf16[32,4,512]{2,1,0:T(4,128)(2,1)S(1)} async-done(((bf16[32,4,512]{2,1,0:T(4,128)(2,1)}), bf16[32,4,512]{2,1,0:T(4,128)(2,1)S(1)}, u32[]{:S(2)}, u32[]{:S(2)}) %all-to-all-start) | async-done | bytes 131104 | tf_op jit(solution)/shard_map/all_to_all | solution.py:606
  17.9 0.0 copy-done.1
  17.9 0.0 copy-done.3
  18.0 0.6 %first.1 = (f32[4,256]{1,0:T(4,128)S(1)}, f32[352,128]{1,0:T(8,128)S(1)}, f32[8,128]{1,0:T(8,128)S(1)}) custom-call(bf16[32,4,512]{2,1,0:T(4,128)(2,1)S(1)} %all-to-all-done.arrived_ref, f32[16,128]{1,0:T(8,128)S(1)} %bitcast.21, bf16[3,32,1280]{2,1,0:T(8,128)(2,1)S(1)} %get-tuple-element.15.weights_ref, ...), custom_call_target="tpu_custom_call" | custom-call | bytes 1048576 | tf_op jit(solution)/shard_map/first/pallas_call | solution.py:593
  18.5 10.4 %all_to_all.15.arrived_ref = f32[32,1,1408]{2,1,0:T(1,128)S(1)} all-to-all(f32[32,1,1408]{2,1,0:T(1,128)S(1)} %bitcast.15), channel_id=1, replica_groups=mesh['clus'=8,'lvl'=4] {'lvl','clus'}, dimensions={0} | all-to-all | bytes 360448 | tf_op jit(solution)/shard_map/all_to_all | solution.py:606
  28.9 0.5 %middle.1 = (f32[32,2,128]{2,1,0:T(2,128)S(1)}, f32[8,256]{1,0:T(8,128)S(1)}, f32[4,256]{1,0:T(4,128)S(1)}, f32[4,128]{1,0:T(4,128)S(1)}) custom-call(f32[32,1,1408]{2,1,0:T(1,128)S(1)} %all_to_all.15.arrived_ref, f32[352,128]{1,0:T(8,128)S(1)} %bitcast.12, f32[16,128]{1,0:T(8,128)S(1)} %bitcast.22, f32[4,256]{1,0:T(4,128)S(1)} %get-tuple-element.20.image_ref, ...), custom_call_target="tpu_custom_call" | custom-call | bytes 1048576 | tf_op jit(solution)/shard_map/middle/pallas_call | solution.py:593
  29.5 9.4 %all_to_all.16.arrived_ref = f32[32,2,128]{2,1,0:T(2,128)S(1)} all-to-all(f32[32,2,128]{2,1,0:T(2,128)S(1)} %get-tuple-element.22), channel_id=1, replica_groups=mesh['clus'=8,'lvl'=4] {'lvl','clus'}, dimensions={0} | all-to-all | bytes 65536 | tf_op jit(solution)/shard_map/all_to_all | solution.py:606
  38.9 1.0 %end.1 = (f32[8,128]{1,0:T(8,128)}, f32[2,4,12]{2,1,0:T(4,128)}) custom-call(f32[32,2,128]{2,1,0:T(2,128)S(1)} %all_to_all.16.arrived_ref, f32[64,128]{1,0:T(8,128)S(1)} %bitcast.14, f32[8,256]{1,0:T(8,128)S(1)} %get-tuple-element.23.window_ref, f32[4,256]{1,0:T(4,128)S(1)} %get-tuple-element.24.near_part_ref, ...), custom_call_target="tpu_custom_call" | custom-call | bytes 1048576 | tf_op jit(solution)/shard_map/end/pallas_call | solution.py:593
Async XLA Ops:
  2.4 8.1 %copy-start.2 = (f32[1,1,6,32,32]{4,3,2,1,0:T(8,128)S(1)}, f32[1,1,6,32,32]{4,3,2,1,0:T(8,128)}, u32[]{:S(2)}) copy-start(f32[1,1,6,32,32]{4,3,2,1,0:T(8,128)} %param.17) | copy-start | bytes 73732
  2.4 8.1 %copy-start.4 = (f32[1,1,4,32,32]{4,3,2,1,0:T(8,128)S(1)}, f32[1,1,4,32,32]{4,3,2,1,0:T(8,128)}, u32[]{:S(2)}) copy-start(f32[1,1,4,32,32]{4,3,2,1,0:T(8,128)} %param.19) | copy-start | bytes 49156
  2.4 8.1 %copy-start.5 = (bf16[1,1,32,256]{3,2,1,0:T(8,128)(2,1)S(1)}, bf16[1,1,32,256]{3,2,1,0:T(8,128)(2,1)}, u32[]{:S(2)}) copy-start(bf16[1,1,32,256]{3,2,1,0:T(8,128)(2,1)} %param.15) | copy-start | bytes 49156
  2.4 8.1 %copy-start.6 = (f32[1,1,32,32]{3,2,1,0:T(8,128)S(1)}, f32[1,1,32,32]{3,2,1,0:T(8,128)}, u32[]{:S(2)}) copy-start(f32[1,1,32,32]{3,2,1,0:T(8,128)} %param.18) | copy-start | bytes 12292
  2.4 15.5 %all-to-all-start = ((bf16[32,4,512]{2,1,0:T(4,128)(2,1)}), bf16[32,4,512]{2,1,0:T(4,128)(2,1)S(1)}, u32[]{:S(2)}, u32[]{:S(2)}) async-start(bf16[32,4,512]{2,1,0:T(4,128)(2,1)} %begin.1), calls=%async_computation | async-start | bytes 262144 | tf_op jit(solution)/shard_map/all_to_all | solution.py:606
  10.4 0.7 %copy-start.7 = (s32[1,1,4]{2,1,0:T(1,128)S(1)}, s32[1,1,4]{2,1,0:T(1,128)}, u32[]{:S(2)}) copy-start(s32[1,1,4]{2,1,0:T(1,128)} %near_col_ref.1) | copy-start | bytes 52
  10.4 0.7 %copy-start.8 = (s32[1,1,6]{2,1,0:T(1,128)S(1)}, s32[1,1,6]{2,1,0:T(1,128)}, u32[]{:S(2)}) copy-start(s32[1,1,6]{2,1,0:T(1,128)} %far_col_ref.1) | copy-start | bytes 76
  11.1 1.0 %copy-start = (bf16[1,1,4,256,256]{4,3,2,1,0:T(8,128)(2,1)S(1)}, bf16[1,1,4,256,256]{4,3,2,1,0:T(8,128)(2,1)}, u32[]{:S(2)}) copy-start(bf16[1,1,4,256,256]{4,3,2,1,0:T(8,128)(2,1)} %param.11) | copy-start | bytes 1572868
  12.2 5.8 %copy-start.1 = (bf16[1,1,32,256]{3,2,1,0:T(8,128)(2,1)S(1)}, bf16[1,1,32,256]{3,2,1,0:T(8,128)(2,1)}, u32[]{:S(2)}) copy-start(bf16[1,1,32,256]{3,2,1,0:T(8,128)(2,1)} %param.16) | copy-start | bytes 49156
  13.0 4.9 %copy-start.3 = (f32[8,1,256]{2,1,0:T(1,128)S(1)}, f32[8,1,256]{2,1,0:T(1,128)}, u32[]{:S(2)}) copy-start(f32[8,1,256]{2,1,0:T(1,128)} %param.10) | copy-start | bytes 24580

commit v11 on v10

--- a/solution.py
+++ b/solution.py
@@ -241,11 +241,12 @@
 
 def near_field(blocks, choice_ref, near_ref):
     choice = choice_ref[...]
-    blocks = [[tile.astype(F32) for tile in lane_tiles(block)] for block in blocks]
-    parts = []
-    for slot in range(near_ref.shape[0]):
-        rows = [choice[3 * slot + side : 3 * slot + side + 1] for side in range(3)]
-        tiles = [sum(tile * row for tile, row in zip(sides, rows)) for sides in zip(*blocks)]
+    low, own, high = blocks
+    parts = [rows_dot(own, near_ref[0])]
+    low, high = ([tile.astype(F32) for tile in lane_tiles(block)] for block in (low, high))
+    for slot in range(1, near_ref.shape[0]):
+        rows = [choice[3 * slot + side : 3 * slot + side + 1] for side in (0, 2)]
+        tiles = [before * rows[0] + after * rows[1] for before, after in zip(low, high)]
         parts.append(rows_dot(jnp.concatenate(tiles, axis=1).astype(BF16), near_ref[slot]))
     return tree_sum(parts)
 

time: 40.3 us -> 40.3 us (level)
  no operation moved by 1% of the time
where the time goes in v11:
time: 40.3 us; the launch traced here: 39.8 us
  blocking collectives  19.8 us (49%)
  starting transfers between devices  7.33 us (18%)
  waiting for transfers between devices  4.89 us (12%)
  Pallas kernels  4.71 us (12%)
  local copies, waits for them, and re-layouts  1.69 us (4%)
  between operations  1.41 us (3%)
    all_to_all x2, blocking collectives, exchange(): return lax.all_to_all(slots, AXES, 0, 0, tiled=True)  19.8 us
    all_to_all x1, starting transfers between devices, exchange(): return lax.all_to_all(slots, AXES, 0, 0, tiled=True)  7.33 us
    all_to_all x1, waiting for transfers between devices, exchange(): return lax.all_to_all(slots, AXES, 0, 0, tiled=True)  4.89 us
    pallas_call x5, Pallas kernels, call(): pl.pallas_call(kernel, name=name, out_shape=[jax.ShapeDtypeStruct(shape,...  4.71 us
    unnamed x18, local copies, waits for them, and re-layouts  1.69 us
  transfers between devices with their start and end apart: 1, of which 1 were waited for; matrix products, arithmetic and copies ran while one was open for 0% of the time, Pallas kernels for 2%

profile of v11, /device:TPU:0, one launch (start us, length us, event | category | flops | bytes accessed | tf_op | source)
XLA Modules:
  0.0 39.8 jit_solution(17317352119529457745)
XLA Ops:
  0.6 1.8 %begin.1 = bf16[32,4,512]{2,1,0:T(4,128)(2,1)} custom-call(f32[16,128]{1,0:T(8,128)} %bitcast.20, bf16[32,256]{1,0:T(8,128)(2,1)} %bitcast.24, f32[32,32]{1,0:T(8,128)} %bitcast.26), custom_call_target="tpu_custom_call" | custom-call | bytes 1048576 | tf_op jit(solution)/shard_map/begin/pallas_call | solution.py:594
  2.4 0.0 copy-start.2
  2.4 0.0 copy-start.4
  2.4 0.0 copy-start.5
  2.4 0.0 copy-start.6
  2.4 7.3 %all-to-all-start = ((bf16[32,4,512]{2,1,0:T(4,128)(2,1)}), bf16[32,4,512]{2,1,0:T(4,128)(2,1)S(1)}, u32[]{:S(2)}, u32[]{:S(2)}) async-start(bf16[32,4,512]{2,1,0:T(4,128)(2,1)} %begin.1), calls=%async_computation | async-start | bytes 262144 | tf_op jit(solution)/shard_map/all_to_all | solution.py:607
  10.4 0.0 copy-start.7
  10.4 0.0 copy-start.8
  10.5 0.0 copy-done.2
  10.5 0.0 copy-done.4
  10.5 0.0 copy-done.5
  10.5 0.0 copy-done.6
  10.5 0.6 %copy-done.7 = s32[1,1,4]{2,1,0:T(1,128)S(1)} copy-done((s32[1,1,4]{2,1,0:T(1,128)S(1)}, s32[1,1,4]{2,1,0:T(1,128)}, u32[]{:S(2)}) %copy-start.7) | copy-done | bytes 40
  11.1 0.0 copy-done.8
  11.1 0.0 copy-start
  11.1 1.0 %copy-done = bf16[1,1,4,256,256]{4,3,2,1,0:T(8,128)(2,1)S(1)} copy-done((bf16[1,1,4,256,256]{4,3,2,1,0:T(8,128)(2,1)S(1)}, bf16[1,1,4,256,256]{4,3,2,1,0:T(8,128)(2,1)}, u32[]{:S(2)}) %copy-start) | copy-done | bytes 524312
  12.2 0.0 copy-start.1
  12.2 0.9 %prepare.1 = (bf16[3,32,1280]{2,1,0:T(8,128)(2,1)S(1)}, bf16[4,256,256]{2,1,0:T(8,128)(2,1)S(1)}, bf16[128,256]{1,0:T(8,128)(2,1)S(1)}, f32[16,128]{1,0:T(8,128)S(1)}) custom-call(s32[1,1,4]{2,1,0:T(1,128)S(1)} %copy-done.7, s32[1,1]{1,0:T(1,128)S(6)} %copy.13.near_count_ref, s32[1,1,6]{2,1,0:T(1,128)S(1)} %copy-done.8, bf16[4,256,256]{2,1,0:T(8,128)(2,1)S(1)} %bitcast.13, ...), custom_call_target="tpu_custom_call" | custom-call | bytes 1048576 | tf_op jit(solution)/shard_map/prepare/pallas_call | solution.py:594
  13.0 0.0 copy-start.3
  13.1 4.9 %all-to-all-done.arrived_ref = bf16[32,4,512]{2,1,0:T(4,128)(2,1)S(1)} async-done(((bf16[32,4,512]{2,1,0:T(4,128)(2,1)}), bf16[32,4,512]{2,1,0:T(4,128)(2,1)S(1)}, u32[]{:S(2)}, u32[]{:S(2)}) %all-to-all-start) | async-done | bytes 131104 | tf_op jit(solution)/shard_map/all_to_all | solution.py:607
  17.9 0.0 copy-done.1
  17.9 0.0 copy-done.3
  18.0 0.6 %first.1 = (f32[4,256]{1,0:T(4,128)S(1)}, f32[352,128]{1,0:T(8,128)S(1)}, f32[8,128]{1,0:T(8,128)S(1)}) custom-call(bf16[32,4,512]{2,1,0:T(4,128)(2,1)S(1)} %all-to-all-done.arrived_ref, f32[16,128]{1,0:T(8,128)S(1)} %bitcast.21, bf16[3,32,1280]{2,1,0:T(8,128)(2,1)S(1)} %get-tuple-element.15.weights_ref, ...), custom_call_target="tpu_custom_call" | custom-call | bytes 1048576 | tf_op jit(solution)/shard_map/first/pallas_call | solution.py:594
  18.5 10.4 %all_to_all.15.arrived_ref = f32[32,1,1408]{2,1,0:T(1,128)S(1)} all-to-all(f32[32,1,1408]{2,1,0:T(1,128)S(1)} %bitcast.15), channel_id=1, replica_groups=mesh['clus'=8,'lvl'=4] {'lvl','clus'}, dimensions={0} | all-to-all | bytes 360448 | tf_op jit(solution)/shard_map/all_to_all | solution.py:607
  28.9 0.5 %middle.1 = (f32[32,2,128]{2,1,0:T(2,128)S(1)}, f32[8,256]{1,0:T(8,128)S(1)}, f32[4,256]{1,0:T(4,128)S(1)}, f32[4,128]{1,0:T(4,128)S(1)}) custom-call(f32[32,1,1408]{2,1,0:T(1,128)S(1)} %all_to_all.15.arrived_ref, f32[352,128]{1,0:T(8,128)S(1)} %bitcast.12, f32[16,128]{1,0:T(8,128)S(1)} %bitcast.22, f32[4,256]{1,0:T(4,128)S(1)} %get-tuple-element.20.image_ref, ...), custom_call_target="tpu_custom_call" | custom-call | bytes 1048576 | tf_op jit(solution)/shard_map/middle/pallas_call | solution.py:594
  29.5 9.4 %all_to_all.16.arrived_ref = f32[32,2,128]{2,1,0:T(2,128)S(1)} all-to-all(f32[32,2,128]{2,1,0:T(2,128)S(1)} %get-tuple-element.22), channel_id=1, replica_groups=mesh['clus'=8,'lvl'=4] {'lvl','clus'}, dimensions={0} | all-to-all | bytes 65536 | tf_op jit(solution)/shard_map/all_to_all | solution.py:607
  38.9 1.0 %end.1 = (f32[8,128]{1,0:T(8,128)}, f32[2,4,12]{2,1,0:T(4,128)}) custom-call(f32[32,2,128]{2,1,0:T(2,128)S(1)} %all_to_all.16.arrived_ref, f32[64,128]{1,0:T(8,128)S(1)} %bitcast.14, f32[8,256]{1,0:T(8,128)S(1)} %get-tuple-element.23.window_ref, f32[4,256]{1,0:T(4,128)S(1)} %get-tuple-element.24.near_part_ref, ...), custom_call_target="tpu_custom_call" | custom-call | bytes 1048576 | tf_op jit(solution)/shard_map/end/pallas_call | solution.py:594
Async XLA Ops:
  2.4 8.1 %copy-start.2 = (f32[1,1,6,32,32]{4,3,2,1,0:T(8,128)S(1)}, f32[1,1,6,32,32]{4,3,2,1,0:T(8,128)}, u32[]{:S(2)}) copy-start(f32[1,1,6,32,32]{4,3,2,1,0:T(8,128)} %param.17) | copy-start | bytes 73732
  2.4 8.1 %copy-start.4 = (f32[1,1,4,32,32]{4,3,2,1,0:T(8,128)S(1)}, f32[1,1,4,32,32]{4,3,2,1,0:T(8,128)}, u32[]{:S(2)}) copy-start(f32[1,1,4,32,32]{4,3,2,1,0:T(8,128)} %param.19) | copy-start | bytes 49156
  2.4 8.1 %copy-start.5 = (bf16[1,1,32,256]{3,2,1,0:T(8,128)(2,1)S(1)}, bf16[1,1,32,256]{3,2,1,0:T(8,128)(2,1)}, u32[]{:S(2)}) copy-start(bf16[1,1,32,256]{3,2,1,0:T(8,128)(2,1)} %param.15) | copy-start | bytes 49156
  2.4 8.1 %copy-start.6 = (f32[1,1,32,32]{3,2,1,0:T(8,128)S(1)}, f32[1,1,32,32]{3,2,1,0:T(8,128)}, u32[]{:S(2)}) copy-start(f32[1,1,32,32]{3,2,1,0:T(8,128)} %param.18) | copy-start | bytes 12292
  2.4 15.5 %all-to-all-start = ((bf16[32,4,512]{2,1,0:T(4,128)(2,1)}), bf16[32,4,512]{2,1,0:T(4,128)(2,1)S(1)}, u32[]{:S(2)}, u32[]{:S(2)}) async-start(bf16[32,4,512]{2,1,0:T(4,128)(2,1)} %begin.1), calls=%async_computation | async-start | bytes 262144 | tf_op jit(solution)/shard_map/all_to_all | solution.py:607
  10.4 0.7 %copy-start.7 = (s32[1,1,4]{2,1,0:T(1,128)S(1)}, s32[1,1,4]{2,1,0:T(1,128)}, u32[]{:S(2)}) copy-start(s32[1,1,4]{2,1,0:T(1,128)} %near_col_ref.1) | copy-start | bytes 52
  10.4 0.7 %copy-start.8 = (s32[1,1,6]{2,1,0:T(1,128)S(1)}, s32[1,1,6]{2,1,0:T(1,128)}, u32[]{:S(2)}) copy-start(s32[1,1,6]{2,1,0:T(1,128)} %far_col_ref.1) | copy-start | bytes 76
  11.1 1.0 %copy-start = (bf16[1,1,4,256,256]{4,3,2,1,0:T(8,128)(2,1)S(1)}, bf16[1,1,4,256,256]{4,3,2,1,0:T(8,128)(2,1)}, u32[]{:S(2)}) copy-start(bf16[1,1,4,256,256]{4,3,2,1,0:T(8,128)(2,1)} %param.11) | copy-start | bytes 1572868
  12.2 5.8 %copy-start.1 = (bf16[1,1,32,256]{3,2,1,0:T(8,128)(2,1)S(1)}, bf16[1,1,32,256]{3,2,1,0:T(8,128)(2,1)}, u32[]{:S(2)}) copy-start(bf16[1,1,32,256]{3,2,1,0:T(8,128)(2,1)} %param.16) | copy-start | bytes 49156
  13.0 4.9 %copy-start.3 = (f32[8,1,256]{2,1,0:T(1,128)S(1)}, f32[8,1,256]{2,1,0:T(1,128)}, u32[]{:S(2)}) copy-start(f32[8,1,256]{2,1,0:T(1,128)} %param.10) | copy-start | bytes 24580

commit v12 on v10

--- a/solution.py
+++ b/solution.py
@@ -114,15 +114,22 @@
     rest = current - lowered.astype(F32)
     parts = [lowered, *three_parts(window[: basis - VECS]), *three_parts(rest)[:2]]
     parts = jnp.concatenate([part.astype(F32) for part in parts], axis=0).astype(BF16)
+    def summed(rows):
+        rows = row_groups(rows)
+        return jnp.concatenate(
+            [rows[0], rows[1] + rows[2] + rows[3], rows[4] + rows[5]], axis=0
+        )
+
+    narrow = summed(rows_dot(parts, v_ref[...]))
     repeats = LANES // rank
     wide_basis = jnp.concatenate([v_ref[...]] * repeats, axis=0)
-    rows = row_groups(rows_dot(parts, wide_basis))
-    skeletons = jnp.concatenate([rows[0], rows[1] + rows[2] + rows[3], rows[4] + rows[5]], axis=0)
+    skeletons = summed(rows_dot(parts, wide_basis))
     wide_transfer = jnp.concatenate([transfer_ref[...]] * repeats, axis=1)
     wide_transfer = jnp.concatenate(three_parts(wide_transfer), axis=1)
-    wide_transfer = jnp.concatenate([wide_transfer] * repeats, axis=0)
-    split = lane_parts(skeletons, lanes_of(skeletons.shape) // rank).astype(BF16)
-    coarse = sum(lane_tiles(jnp.dot(split, wide_transfer, preferred_element_type=F32)))
+    narrow = jnp.concatenate([part.astype(F32) for part in three_parts(narrow)], axis=0)
+    coarse = sum(lane_tiles(jnp.dot(narrow.astype(BF16), wide_transfer, preferred_element_type=F32)))
+    count = skeletons.shape[0]
+    coarse = coarse[:count] + coarse[count : 2 * count] + coarse[2 * count :]
     own_tree = lax.axis_index("lvl")
 
     def tails(values):

time: 40.3 us -> 40.3 us (level)
  no operation moved by 1% of the time
where the time goes in v12:
time: 40.3 us; the launch traced here: 39.8 us
  blocking collectives  19.8 us (49%)
  starting transfers between devices  7.33 us (18%)
  waiting for transfers between devices  4.89 us (12%)
  Pallas kernels  4.7 us (12%)
  local copies, waits for them, and re-layouts  1.69 us (4%)
  between operations  1.41 us (3%)
    all_to_all x2, blocking collectives, exchange(): return lax.all_to_all(slots, AXES, 0, 0, tiled=True)  19.8 us
    all_to_all x1, starting transfers between devices, exchange(): return lax.all_to_all(slots, AXES, 0, 0, tiled=True)  7.33 us
    all_to_all x1, waiting for transfers between devices, exchange(): return lax.all_to_all(slots, AXES, 0, 0, tiled=True)  4.89 us
    pallas_call x5, Pallas kernels, call(): pl.pallas_call(kernel, name=name, out_shape=[jax.ShapeDtypeStruct(shape,...  4.7 us
    unnamed x18, local copies, waits for them, and re-layouts  1.69 us
  transfers between devices with their start and end apart: 1, of which 1 were waited for; matrix products, arithmetic and copies ran while one was open for 0% of the time, Pallas kernels for 2%

profile of v12, /device:TPU:0, one launch (start us, length us, event | category | flops | bytes accessed | tf_op | source)
XLA Modules:
  0.0 39.8 jit_solution(2495944265343136282)
XLA Ops:
  0.6 1.7 %begin.1 = bf16[32,4,512]{2,1,0:T(4,128)(2,1)} custom-call(f32[16,128]{1,0:T(8,128)} %bitcast.20, bf16[32,256]{1,0:T(8,128)(2,1)} %bitcast.24, f32[32,32]{1,0:T(8,128)} %bitcast.26), custom_call_target="tpu_custom_call" | custom-call | bytes 1048576 | tf_op jit(solution)/shard_map/begin/pallas_call | solution.py:600
  2.4 0.0 copy-start.2
  2.4 0.0 copy-start.4
  2.4 0.0 copy-start.5
  2.4 0.0 copy-start.6
  2.4 7.3 %all-to-all-start = ((bf16[32,4,512]{2,1,0:T(4,128)(2,1)}), bf16[32,4,512]{2,1,0:T(4,128)(2,1)S(1)}, u32[]{:S(2)}, u32[]{:S(2)}) async-start(bf16[32,4,512]{2,1,0:T(4,128)(2,1)} %begin.1), calls=%async_computation | async-start | bytes 262144 | tf_op jit(solution)/shard_map/all_to_all | solution.py:613
  10.4 0.0 copy-start.7
  10.4 0.0 copy-start.8
  10.4 0.0 copy-done.2
  10.5 0.0 copy-done.4
  10.5 0.0 copy-done.5
  10.5 0.0 copy-done.6
  10.5 0.6 %copy-done.7 = s32[1,1,4]{2,1,0:T(1,128)S(1)} copy-done((s32[1,1,4]{2,1,0:T(1,128)S(1)}, s32[1,1,4]{2,1,0:T(1,128)}, u32[]{:S(2)}) %copy-start.7) | copy-done | bytes 40
  11.1 0.0 copy-done.8
  11.1 0.0 copy-start
  11.1 1.0 %copy-done = bf16[1,1,4,256,256]{4,3,2,1,0:T(8,128)(2,1)S(1)} copy-done((bf16[1,1,4,256,256]{4,3,2,1,0:T(8,128)(2,1)S(1)}, bf16[1,1,4,256,256]{4,3,2,1,0:T(8,128)(2,1)}, u32[]{:S(2)}) %copy-start) | copy-done | bytes 524312
  12.1 0.0 copy-start.1
  12.1 0.9 %prepare.1 = (bf16[3,32,1280]{2,1,0:T(8,128)(2,1)S(1)}, bf16[4,256,256]{2,1,0:T(8,128)(2,1)S(1)}, bf16[128,256]{1,0:T(8,128)(2,1)S(1)}, f32[16,128]{1,0:T(8,128)S(1)}) custom-call(s32[1,1,4]{2,1,0:T(1,128)S(1)} %copy-done.7, s32[1,1]{1,0:T(1,128)S(6)} %copy.13.near_count_ref, s32[1,1,6]{2,1,0:T(1,128)S(1)} %copy-done.8, bf16[4,256,256]{2,1,0:T(8,128)(2,1)S(1)} %bitcast.13, ...), custom_call_target="tpu_custom_call" | custom-call | bytes 1048576 | tf_op jit(solution)/shard_map/prepare/pallas_call | solution.py:600
  13.0 0.0 copy-start.3
  13.0 4.9 %all-to-all-done.arrived_ref = bf16[32,4,512]{2,1,0:T(4,128)(2,1)S(1)} async-done(((bf16[32,4,512]{2,1,0:T(4,128)(2,1)}), bf16[32,4,512]{2,1,0:T(4,128)(2,1)S(1)}, u32[]{:S(2)}, u32[]{:S(2)}) %all-to-all-start) | async-done | bytes 131104 | tf_op jit(solution)/shard_map/all_to_all | solution.py:613
  17.9 0.0 copy-done.1
  17.9 0.0 copy-done.3
  17.9 0.6 %first.1 = (f32[4,256]{1,0:T(4,128)S(1)}, f32[352,128]{1,0:T(8,128)S(1)}, f32[8,128]{1,0:T(8,128)S(1)}) custom-call(bf16[32,4,512]{2,1,0:T(4,128)(2,1)S(1)} %all-to-all-done.arrived_ref, f32[16,128]{1,0:T(8,128)S(1)} %bitcast.21, bf16[3,32,1280]{2,1,0:T(8,128)(2,1)S(1)} %get-tuple-element.15.weights_ref, ...), custom_call_target="tpu_custom_call" | custom-call | bytes 1048576 | tf_op jit(solution)/shard_map/first/pallas_call | solution.py:600
  18.5 10.4 %all_to_all.15.arrived_ref = f32[32,1,1408]{2,1,0:T(1,128)S(1)} all-to-all(f32[32,1,1408]{2,1,0:T(1,128)S(1)} %bitcast.15), channel_id=1, replica_groups=mesh['clus'=8,'lvl'=4] {'lvl','clus'}, dimensions={0} | all-to-all | bytes 360448 | tf_op jit(solution)/shard_map/all_to_all | solution.py:613
  28.9 0.5 %middle.1 = (f32[32,2,128]{2,1,0:T(2,128)S(1)}, f32[8,256]{1,0:T(8,128)S(1)}, f32[4,256]{1,0:T(4,128)S(1)}, f32[4,128]{1,0:T(4,128)S(1)}) custom-call(f32[32,1,1408]{2,1,0:T(1,128)S(1)} %all_to_all.15.arrived_ref, f32[352,128]{1,0:T(8,128)S(1)} %bitcast.12, f32[16,128]{1,0:T(8,128)S(1)} %bitcast.22, f32[4,256]{1,0:T(4,128)S(1)} %get-tuple-element.20.image_ref, ...), custom_call_target="tpu_custom_call" | custom-call | bytes 1048576 | tf_op jit(solution)/shard_map/middle/pallas_call | solution.py:600
  29.4 9.4 %all_to_all.16.arrived_ref = f32[32,2,128]{2,1,0:T(2,128)S(1)} all-to-all(f32[32,2,128]{2,1,0:T(2,128)S(1)} %get-tuple-element.22), channel_id=1, replica_groups=mesh['clus'=8,'lvl'=4] {'lvl','clus'}, dimensions={0} | all-to-all | bytes 65536 | tf_op jit(solution)/shard_map/all_to_all | solution.py:613
  38.9 1.0 %end.1 = (f32[8,128]{1,0:T(8,128)}, f32[2,4,12]{2,1,0:T(4,128)}) custom-call(f32[32,2,128]{2,1,0:T(2,128)S(1)} %all_to_all.16.arrived_ref, f32[64,128]{1,0:T(8,128)S(1)} %bitcast.14, f32[8,256]{1,0:T(8,128)S(1)} %get-tuple-element.23.window_ref, f32[4,256]{1,0:T(4,128)S(1)} %get-tuple-element.24.near_part_ref, ...), custom_call_target="tpu_custom_call" | custom-call | bytes 1048576 | tf_op jit(solution)/shard_map/end/pallas_call | solution.py:600
Async XLA Ops:
  2.4 8.1 %copy-start.2 = (f32[1,1,6,32,32]{4,3,2,1,0:T(8,128)S(1)}, f32[1,1,6,32,32]{4,3,2,1,0:T(8,128)}, u32[]{:S(2)}) copy-start(f32[1,1,6,32,32]{4,3,2,1,0:T(8,128)} %param.17) | copy-start | bytes 73732
  2.4 8.1 %copy-start.4 = (f32[1,1,4,32,32]{4,3,2,1,0:T(8,128)S(1)}, f32[1,1,4,32,32]{4,3,2,1,0:T(8,128)}, u32[]{:S(2)}) copy-start(f32[1,1,4,32,32]{4,3,2,1,0:T(8,128)} %param.19) | copy-start | bytes 49156
  2.4 8.1 %copy-start.5 = (bf16[1,1,32,256]{3,2,1,0:T(8,128)(2,1)S(1)}, bf16[1,1,32,256]{3,2,1,0:T(8,128)(2,1)}, u32[]{:S(2)}) copy-start(bf16[1,1,32,256]{3,2,1,0:T(8,128)(2,1)} %param.15) | copy-start | bytes 49156
  2.4 8.1 %copy-start.6 = (f32[1,1,32,32]{3,2,1,0:T(8,128)S(1)}, f32[1,1,32,32]{3,2,1,0:T(8,128)}, u32[]{:S(2)}) copy-start(f32[1,1,32,32]{3,2,1,0:T(8,128)} %param.18) | copy-start | bytes 12292
  2.4 15.5 %all-to-all-start = ((bf16[32,4,512]{2,1,0:T(4,128)(2,1)}), bf16[32,4,512]{2,1,0:T(4,128)(2,1)S(1)}, u32[]{:S(2)}, u32[]{:S(2)}) async-start(bf16[32,4,512]{2,1,0:T(4,128)(2,1)} %begin.1), calls=%async_computation | async-start | bytes 262144 | tf_op jit(solution)/shard_map/all_to_all | solution.py:613
  10.4 0.7 %copy-start.7 = (s32[1,1,4]{2,1,0:T(1,128)S(1)}, s32[1,1,4]{2,1,0:T(1,128)}, u32[]{:S(2)}) copy-start(s32[1,1,4]{2,1,0:T(1,128)} %near_col_ref.1) | copy-start | bytes 52
  10.4 0.7 %copy-start.8 = (s32[1,1,6]{2,1,0:T(1,128)S(1)}, s32[1,1,6]{2,1,0:T(1,128)}, u32[]{:S(2)}) copy-start(s32[1,1,6]{2,1,0:T(1,128)} %far_col_ref.1) | copy-start | bytes 76
  11.1 1.0 %copy-start = (bf16[1,1,4,256,256]{4,3,2,1,0:T(8,128)(2,1)S(1)}, bf16[1,1,4,256,256]{4,3,2,1,0:T(8,128)(2,1)}, u32[]{:S(2)}) copy-start(bf16[1,1,4,256,256]{4,3,2,1,0:T(8,128)(2,1)} %param.11) | copy-start | bytes 1572868
  12.1 5.8 %copy-start.1 = (bf16[1,1,32,256]{3,2,1,0:T(8,128)(2,1)S(1)}, bf16[1,1,32,256]{3,2,1,0:T(8,128)(2,1)}, u32[]{:S(2)}) copy-start(bf16[1,1,32,256]{3,2,1,0:T(8,128)(2,1)} %param.16) | copy-start | bytes 49156
  13.0 4.9 %copy-start.3 = (f32[8,1,256]{2,1,0:T(1,128)S(1)}, f32[8,1,256]{2,1,0:T(1,128)}, u32[]{:S(2)}) copy-start(f32[8,1,256]{2,1,0:T(1,128)} %param.10) | copy-start | bytes 24580

commit v13 on v12

--- a/solution.py
+++ b/solution.py
@@ -248,11 +248,12 @@
 
 def near_field(blocks, choice_ref, near_ref):
     choice = choice_ref[...]
-    blocks = [[tile.astype(F32) for tile in lane_tiles(block)] for block in blocks]
-    parts = []
-    for slot in range(near_ref.shape[0]):
-        rows = [choice[3 * slot + side : 3 * slot + side + 1] for side in range(3)]
-        tiles = [sum(tile * row for tile, row in zip(sides, rows)) for sides in zip(*blocks)]
+    low, own, high = blocks
+    parts = [rows_dot(own, near_ref[0])]
+    low, high = ([tile.astype(F32) for tile in lane_tiles(block)] for block in (low, high))
+    for slot in range(1, near_ref.shape[0]):
+        rows = [choice[3 * slot + side : 3 * slot + side + 1] for side in (0, 2)]
+        tiles = [before * rows[0] + after * rows[1] for before, after in zip(low, high)]
         parts.append(rows_dot(jnp.concatenate(tiles, axis=1).astype(BF16), near_ref[slot]))
     return tree_sum(parts)
 

time: 40.3 us -> 40.3 us (level)
  no operation moved by 1% of the time
where the time goes in v13:
time: 40.3 us; the launch traced here: 39.8 us
  blocking collectives  19.8 us (49%)
  starting transfers between devices  7.33 us (18%)
  waiting for transfers between devices  4.89 us (12%)
  Pallas kernels  4.69 us (12%)
  local copies, waits for them, and re-layouts  1.69 us (4%)
  between operations  1.41 us (3%)
    all_to_all x2, blocking collectives, exchange(): return lax.all_to_all(slots, AXES, 0, 0, tiled=True)  19.8 us
    all_to_all x1, starting transfers between devices, exchange(): return lax.all_to_all(slots, AXES, 0, 0, tiled=True)  7.33 us
    all_to_all x1, waiting for transfers between devices, exchange(): return lax.all_to_all(slots, AXES, 0, 0, tiled=True)  4.89 us
    pallas_call x5, Pallas kernels, call(): pl.pallas_call(kernel, name=name, out_shape=[jax.ShapeDtypeStruct(shape,...  4.69 us
    unnamed x18, local copies, waits for them, and re-layouts  1.69 us
  transfers between devices with their start and end apart: 1, of which 1 were waited for; matrix products, arithmetic and copies ran while one was open for 0% of the time, Pallas kernels for 2%

profile of v13, /device:TPU:0, one launch (start us, length us, event | category | flops | bytes accessed | tf_op | source)
XLA Modules:
  0.0 39.8 jit_solution(16065794861698072112)
XLA Ops:
  0.6 1.7 %begin.1 = bf16[32,4,512]{2,1,0:T(4,128)(2,1)} custom-call(f32[16,128]{1,0:T(8,128)} %bitcast.20, bf16[32,256]{1,0:T(8,128)(2,1)} %bitcast.24, f32[32,32]{1,0:T(8,128)} %bitcast.26), custom_call_target="tpu_custom_call" | custom-call | bytes 1048576 | tf_op jit(solution)/shard_map/begin/pallas_call | solution.py:601
  2.4 0.0 copy-start.2
  2.4 0.0 copy-start.4
  2.4 0.0 copy-start.5
  2.4 0.0 copy-start.6
  2.4 7.3 %all-to-all-start = ((bf16[32,4,512]{2,1,0:T(4,128)(2,1)}), bf16[32,4,512]{2,1,0:T(4,128)(2,1)S(1)}, u32[]{:S(2)}, u32[]{:S(2)}) async-start(bf16[32,4,512]{2,1,0:T(4,128)(2,1)} %begin.1), calls=%async_computation | async-start | bytes 262144 | tf_op jit(solution)/shard_map/all_to_all | solution.py:614
  10.4 0.0 copy-start.7
  10.4 0.0 copy-start.8
  10.4 0.0 copy-done.2
  10.5 0.0 copy-done.4
  10.5 0.0 copy-done.5
  10.5 0.0 copy-done.6
  10.5 0.6 %copy-done.7 = s32[1,1,4]{2,1,0:T(1,128)S(1)} copy-done((s32[1,1,4]{2,1,0:T(1,128)S(1)}, s32[1,1,4]{2,1,0:T(1,128)}, u32[]{:S(2)}) %copy-start.7) | copy-done | bytes 40
  11.1 0.0 copy-done.8
  11.1 0.0 copy-start
  11.1 1.0 %copy-done = bf16[1,1,4,256,256]{4,3,2,1,0:T(8,128)(2,1)S(1)} copy-done((bf16[1,1,4,256,256]{4,3,2,1,0:T(8,128)(2,1)S(1)}, bf16[1,1,4,256,256]{4,3,2,1,0:T(8,128)(2,1)}, u32[]{:S(2)}) %copy-start) | copy-done | bytes 524312
  12.1 0.0 copy-start.1
  12.1 0.9 %prepare.1 = (bf16[3,32,1280]{2,1,0:T(8,128)(2,1)S(1)}, bf16[4,256,256]{2,1,0:T(8,128)(2,1)S(1)}, bf16[128,256]{1,0:T(8,128)(2,1)S(1)}, f32[16,128]{1,0:T(8,128)S(1)}) custom-call(s32[1,1,4]{2,1,0:T(1,128)S(1)} %copy-done.7, s32[1,1]{1,0:T(1,128)S(6)} %copy.13.near_count_ref, s32[1,1,6]{2,1,0:T(1,128)S(1)} %copy-done.8, bf16[4,256,256]{2,1,0:T(8,128)(2,1)S(1)} %bitcast.13, ...), custom_call_target="tpu_custom_call" | custom-call | bytes 1048576 | tf_op jit(solution)/shard_map/prepare/pallas_call | solution.py:601
  13.0 0.0 copy-start.3
  13.0 4.9 %all-to-all-done.arrived_ref = bf16[32,4,512]{2,1,0:T(4,128)(2,1)S(1)} async-done(((bf16[32,4,512]{2,1,0:T(4,128)(2,1)}), bf16[32,4,512]{2,1,0:T(4,128)(2,1)S(1)}, u32[]{:S(2)}, u32[]{:S(2)}) %all-to-all-start) | async-done | bytes 131104 | tf_op jit(solution)/shard_map/all_to_all | solution.py:614
  17.9 0.0 copy-done.1
  17.9 0.0 copy-done.3
  17.9 0.6 %first.1 = (f32[4,256]{1,0:T(4,128)S(1)}, f32[352,128]{1,0:T(8,128)S(1)}, f32[8,128]{1,0:T(8,128)S(1)}) custom-call(bf16[32,4,512]{2,1,0:T(4,128)(2,1)S(1)} %all-to-all-done.arrived_ref, f32[16,128]{1,0:T(8,128)S(1)} %bitcast.21, bf16[3,32,1280]{2,1,0:T(8,128)(2,1)S(1)} %get-tuple-element.15.weights_ref, ...), custom_call_target="tpu_custom_call" | custom-call | bytes 1048576 | tf_op jit(solution)/shard_map/first/pallas_call | solution.py:601
  18.5 10.4 %all_to_all.15.arrived_ref = f32[32,1,1408]{2,1,0:T(1,128)S(1)} all-to-all(f32[32,1,1408]{2,1,0:T(1,128)S(1)} %bitcast.15), channel_id=1, replica_groups=mesh['clus'=8,'lvl'=4] {'lvl','clus'}, dimensions={0} | all-to-all | bytes 360448 | tf_op jit(solution)/shard_map/all_to_all | solution.py:614
  28.9 0.5 %middle.1 = (f32[32,2,128]{2,1,0:T(2,128)S(1)}, f32[8,256]{1,0:T(8,128)S(1)}, f32[4,256]{1,0:T(4,128)S(1)}, f32[4,128]{1,0:T(4,128)S(1)}) custom-call(f32[32,1,1408]{2,1,0:T(1,128)S(1)} %all_to_all.15.arrived_ref, f32[352,128]{1,0:T(8,128)S(1)} %bitcast.12, f32[16,128]{1,0:T(8,128)S(1)} %bitcast.22, f32[4,256]{1,0:T(4,128)S(1)} %get-tuple-element.20.image_ref, ...), custom_call_target="tpu_custom_call" | custom-call | bytes 1048576 | tf_op jit(solution)/shard_map/middle/pallas_call | solution.py:601
  29.4 9.4 %all_to_all.16.arrived_ref = f32[32,2,128]{2,1,0:T(2,128)S(1)} all-to-all(f32[32,2,128]{2,1,0:T(2,128)S(1)} %get-tuple-element.22), channel_id=1, replica_groups=mesh['clus'=8,'lvl'=4] {'lvl','clus'}, dimensions={0} | all-to-all | bytes 65536 | tf_op jit(solution)/shard_map/all_to_all | solution.py:614
  38.9 1.0 %end.1 = (f32[8,128]{1,0:T(8,128)}, f32[2,4,12]{2,1,0:T(4,128)}) custom-call(f32[32,2,128]{2,1,0:T(2,128)S(1)} %all_to_all.16.arrived_ref, f32[64,128]{1,0:T(8,128)S(1)} %bitcast.14, f32[8,256]{1,0:T(8,128)S(1)} %get-tuple-element.23.window_ref, f32[4,256]{1,0:T(4,128)S(1)} %get-tuple-element.24.near_part_ref, ...), custom_call_target="tpu_custom_call" | custom-call | bytes 1048576 | tf_op jit(solution)/shard_map/end/pallas_call | solution.py:601
Async XLA Ops:
  2.4 8.1 %copy-start.2 = (f32[1,1,6,32,32]{4,3,2,1,0:T(8,128)S(1)}, f32[1,1,6,32,32]{4,3,2,1,0:T(8,128)}, u32[]{:S(2)}) copy-start(f32[1,1,6,32,32]{4,3,2,1,0:T(8,128)} %param.17) | copy-start | bytes 73732
  2.4 8.1 %copy-start.4 = (f32[1,1,4,32,32]{4,3,2,1,0:T(8,128)S(1)}, f32[1,1,4,32,32]{4,3,2,1,0:T(8,128)}, u32[]{:S(2)}) copy-start(f32[1,1,4,32,32]{4,3,2,1,0:T(8,128)} %param.19) | copy-start | bytes 49156
  2.4 8.1 %copy-start.5 = (bf16[1,1,32,256]{3,2,1,0:T(8,128)(2,1)S(1)}, bf16[1,1,32,256]{3,2,1,0:T(8,128)(2,1)}, u32[]{:S(2)}) copy-start(bf16[1,1,32,256]{3,2,1,0:T(8,128)(2,1)} %param.15) | copy-start | bytes 49156
  2.4 8.1 %copy-start.6 = (f32[1,1,32,32]{3,2,1,0:T(8,128)S(1)}, f32[1,1,32,32]{3,2,1,0:T(8,128)}, u32[]{:S(2)}) copy-start(f32[1,1,32,32]{3,2,1,0:T(8,128)} %param.18) | copy-start | bytes 12292
  2.4 15.5 %all-to-all-start = ((bf16[32,4,512]{2,1,0:T(4,128)(2,1)}), bf16[32,4,512]{2,1,0:T(4,128)(2,1)S(1)}, u32[]{:S(2)}, u32[]{:S(2)}) async-start(bf16[32,4,512]{2,1,0:T(4,128)(2,1)} %begin.1), calls=%async_computation | async-start | bytes 262144 | tf_op jit(solution)/shard_map/all_to_all | solution.py:614
  10.4 0.7 %copy-start.7 = (s32[1,1,4]{2,1,0:T(1,128)S(1)}, s32[1,1,4]{2,1,0:T(1,128)}, u32[]{:S(2)}) copy-start(s32[1,1,4]{2,1,0:T(1,128)} %near_col_ref.1) | copy-start | bytes 52
  10.4 0.7 %copy-start.8 = (s32[1,1,6]{2,1,0:T(1,128)S(1)}, s32[1,1,6]{2,1,0:T(1,128)}, u32[]{:S(2)}) copy-start(s32[1,1,6]{2,1,0:T(1,128)} %far_col_ref.1) | copy-start | bytes 76
  11.1 1.0 %copy-start = (bf16[1,1,4,256,256]{4,3,2,1,0:T(8,128)(2,1)S(1)}, bf16[1,1,4,256,256]{4,3,2,1,0:T(8,128)(2,1)}, u32[]{:S(2)}) copy-start(bf16[1,1,4,256,256]{4,3,2,1,0:T(8,128)(2,1)} %param.11) | copy-start | bytes 1572868
  12.1 5.8 %copy-start.1 = (bf16[1,1,32,256]{3,2,1,0:T(8,128)(2,1)S(1)}, bf16[1,1,32,256]{3,2,1,0:T(8,128)(2,1)}, u32[]{:S(2)}) copy-start(bf16[1,1,32,256]{3,2,1,0:T(8,128)(2,1)} %param.16) | copy-start | bytes 49156
  13.0 4.9 %copy-start.3 = (f32[8,1,256]{2,1,0:T(1,128)S(1)}, f32[8,1,256]{2,1,0:T(1,128)}, u32[]{:S(2)}) copy-start(f32[8,1,256]{2,1,0:T(1,128)} %param.10) | copy-start | bytes 24580
